TPU v7x, 256 devices: a whole 4x4x8 slice. The times are simulated.
256 devices in a mesh: dp: 32 (over z, x), mp: 8 (over y, core).
Axes of the slice: x: 4, y: 4, z: 8, core: 2. Of those that a mesh axis runs over, the one named last changes fastest.
Arguments:
- query: bfloat16 [8192, 4096], P('dp', 'mp'), may hold values from -400 to 400
- keys_values: bfloat16 [2, 8192, 512], P(None, 'dp'), may hold values from -6 to 6
- ancestors: int32 [64, 12], P('dp'), may hold values from -1 to 63, as said below
- tile_of_slot: int32 [64], replicated, may hold values from 0 to 63, as said below
- residual: bfloat16 [8192, 8192], P('dp', 'mp'), may hold values from -6 to 6
- norm_gain: float32 [8192], P('mp'), may hold values from 0.25 to 1.75
- out_weight: bfloat16 [4096, 8192], P('mp'), may hold values from -0.09375 to 0.09375
Outputs:
- hidden_out: bfloat16 [8192, 8192], P('dp', 'mp')
- normed: bfloat16 [8192, 8192], P('dp', 'mp')
Inputs may be any that keep to these rules, and one draw needn't show every extreme that they name: Ids of tiles, or -1. Over all query tiles of one device's 2 positions, the ancestors that lie at the positions of any one device number at most 1 distinct tiles; some device reaches 1 in every draw. `tile_of_slot`: a permutation of the tile ids.
All inputs are finite; a program needn't handle non-finite values.
Results may differ from a plain program's by a relative error of at most 0.008.
Values may be sent and summed in bfloat16 or wider, within the bound.
No kernel may reach another device: no remote copies, remote signals or barrier semaphores. Data moves between devices by JAX's collectives and lax.ppermute only.
A program may use at most 64 MiB of HBM per device.

v0:
```python
import jax
import jax.numpy as jnp
from jax import lax
from jax.experimental import pallas as pl
from jax.experimental.pallas import tpu as pltpu
from jax.sharding import Mesh, PartitionSpec as P


D = 8192
HEAD = 128
TILE = 128
ANC = 12
NZ, NX, NY, NC = 8, 4, 4, 2
TILES = 64
BLOCK = 512
GROUP = 4
LOG2E = 1.4426950408889634
AXES = ("z", "x", "y", "c")


def permutation(target):
    pairs = []
    for z in range(NZ):
        for x in range(NX):
            for y in range(NY):
                for c in range(NC):
                    tz, tx, ty, tc = target(z, x, y, c)
                    source = ((z * NX + x) * NY + y) * NC + c
                    pairs.append(
                        (source, (((tz % NZ) * NX + tx % NX) * NY + ty % NY) * NC + tc % NC)
                    )
    return pairs


def along_z(array, hops):
    return lax.ppermute(
        array, AXES, permutation(lambda z, x, y, c: (z + hops * (1 - 2 * c), x, y, c))
    )


def along_x(array, hops):
    return lax.ppermute(
        array, AXES, permutation(lambda z, x, y, c: (z, x + hops * (1 - 2 * c), y, c))
    )


def along_y(array, hops):
    return lax.ppermute(
        array, AXES, permutation(lambda z, x, y, c: (z, x, y + hops * (1 - 2 * c), c))
    )


def other_core(array):
    return lax.ppermute(array, AXES, permutation(lambda z, x, y, c: (z, x, y, c + 1)))


def gather_pairs(own, c):
    def half(block):
        return lax.dynamic_slice_in_dim(block, c * 256, 256, 0)

    near1 = along_z(own, 1)
    near2 = along_z(own, 2)
    near3 = along_z(own, 3)
    half4 = along_z(half(own), 4)
    group1 = jnp.concatenate([half(own), near1, near2], axis=0)
    ahead1 = along_x(group1, 1)
    back1 = along_x(group1, -1)
    group2 = jnp.concatenate([near3, half4], axis=0)
    ahead2 = along_x(group2, 1)
    back2 = along_x(group2, -1)
    far1, far1_low = along_x(ahead1[:640], 1), along_x(back1[640:], -1)
    far2, far2_low = along_x(ahead2[:384], 1), along_x(back2[384:], -1)
    arrays = [near1, near2, group2, ahead1, back1, ahead2, back2, far1, far1_low, far2, far2_low]
    return arrays, [other_core(array) for array in arrays]


def spot(refs, steps, hops, row):
    near1, near2, group2, ahead1, back1, ahead2, back2, far1, far1_low, far2, far2_low = refs
    if hops == 0 and steps < 3:
        return (near1, near2)[steps - 1], row
    row += {0: 0, 1: 256, 2: 768, 3: 0, 4: 512}[steps]
    if steps < 3:
        held, far, cut = (None, ahead1, None, back1)[hops], (far1, far1_low), 640
    else:
        held, far, cut = (group2, ahead2, None, back2)[hops], (far2, far2_low), 384
    if hops == 2:
        return (far[0], row) if row < cut else (far[1], row - cut)
    return held, row


def attend(query, own, mine, theirs, ancestors, tile_of_slot):
    scale = HEAD**-0.5 * LOG2E
    keys_total = (ANC + 1) * TILE
    count = len(mine)

    def kernel(ancestors_hbm, tile_of_slot_hbm, query_hbm, own_ref, *rest):
        mine_refs, theirs_refs = rest[:count], rest[count : 2 * count]
        out_ref, keys, values, scores, weights, bias, query_ref = rest[2 * count : 2 * count + 7]
        ancestors_ref, tile_of_slot_ref, slot_of, wanted, sems = rest[2 * count + 7 :]
        z, x, c = (lax.axis_index(name) for name in ("z", "x", "c"))
        sign = 1 - 2 * c
        copies = [
            pltpu.make_async_copy(ancestors_hbm, ancestors_ref, sems.at[0]),
            pltpu.make_async_copy(tile_of_slot_hbm, tile_of_slot_ref, sems.at[1]),
            pltpu.make_async_copy(query_hbm, query_ref, sems.at[2]),
        ]
        for copy in copies:
            copy.start()
        for copy in copies[:2]:
            copy.wait()
        for s in range(TILES):
            slot_of[tile_of_slot_ref[s]] = s
        for t in range(2):
            start = t * keys_total
            keys[start : start + TILE] = own_ref[t * TILE : (t + 1) * TILE]
            values[start : start + TILE] = own_ref[256 + t * TILE : 256 + (t + 1) * TILE]
            own_slot = (z * NX + x) * 2 + t
            located = []
            for j in range(ANC):
                tile = ancestors_ref[t, j]
                slot = jnp.where(tile >= 0, slot_of[jnp.maximum(tile, 0)], -1)
                keep = jnp.logical_and(slot >= 0, slot != own_slot)
                for earlier in located:
                    keep = jnp.logical_and(keep, slot != earlier)
                located.append(slot)
                wanted[t * ANC + j] = jnp.where(keep, slot, own_slot)
                bias[t, :, (j + 1) * TILE : (j + 2) * TILE] = jnp.full(
                    (8, TILE), jnp.where(keep, 0.0, -jnp.inf), jnp.float32
                )

        def take(i, carry):
            slot = wanted[i]
            second = slot % 2
            chip = slot // 2
            steps = lax.rem((z - chip // NX) * sign + NZ, NZ)
            hops = lax.rem((x - chip % NX) * sign + NX, NX)
            to = pl.multiple_of((i + 1 + jnp.where(i >= ANC, 1, 0)) * TILE, TILE)

            def put(target, source, row):
                start = pl.multiple_of(row + second * TILE, TILE)
                target[pl.ds(to, TILE)] = source[pl.ds(start, TILE)]

            def put_from(target, refs, n, h, row):
                (ref0, row0), (ref1, row1) = (spot(refs, n, h, row + r) for r in (0, TILE))
                if ref0 is ref1:
                    put(target, ref0, row0)
                else:

                    @pl.when(second == 0)
                    def _():
                        target[pl.ds(to, TILE)] = ref0[row0 : row0 + TILE]

                    @pl.when(second == 1)
                    def _():
                        target[pl.ds(to, TILE)] = ref1[row1 : row1 + TILE]

            def from_chip(n, h):
                h_other = (NX - h) % NX
                if n == 0 and h == 0:
                    put(keys, own_ref, 0)
                    put(values, own_ref, 256)
                elif n in (0, 4):

                    @pl.when(c == 0)
                    def _():
                        put_from(keys, mine_refs, n, h, 0)
                        put_from(values, theirs_refs, n, h_other, 0)

                    @pl.when(c == 1)
                    def _():
                        put_from(keys, theirs_refs, n, h_other, 0)
                        put_from(values, mine_refs, n, h, 0)

                elif n < 4:
                    put_from(keys, mine_refs, n, h, 0)
                    put_from(values, mine_refs, n, h, 256)
                else:
                    put_from(keys, theirs_refs, NZ - n, h_other, 0)
                    put_from(values, theirs_refs, NZ - n, h_other, 256)

            for h in range(NX):

                @pl.when(hops == h)
                def _(h=h):
                    for n in range(NZ):

                        @pl.when(steps == n)
                        def _(n=n):
                            from_chip(n, h)

            return carry

        lax.fori_loop(0, 2 * ANC, take, 0)
        copies[2].wait()
        rows_id = lax.broadcasted_iota(jnp.int32, (TILE, TILE), 0)
        cols_id = lax.broadcasted_iota(jnp.int32, (TILE, TILE), 1)
        causal = jnp.where(rows_id >= cols_id, 0.0, -jnp.inf)
        for t in range(2):
            q = jnp.concatenate(
                [
                    query_ref[t * TILE : (t + 1) * TILE, h * HEAD : (h + 1) * HEAD]
                    for h in range(GROUP)
                ],
                axis=0,
            )
            scores[t] = lax.dot_general(
                q,
                keys[t * keys_total : (t + 1) * keys_total],
                (((1,), (1,)), ((), ())),
                preferred_element_type=jnp.float32,
            )
        for t in range(2):
            totals = []
            for h in range(GROUP):
                rows = slice(h * TILE, (h + 1) * TILE)
                near = scores[t, rows, :TILE] + causal
                far = scores[t, rows, TILE:] + bias[t, 0:1, TILE:]
                peak = jnp.maximum(
                    jnp.max(near, axis=1, keepdims=True), jnp.max(far, axis=1, keepdims=True)
                )
                near = jnp.exp2((near - peak) * scale)
                far = jnp.exp2((far - peak) * scale)
                totals.append(
                    jnp.sum(near, axis=1, keepdims=True) + jnp.sum(far, axis=1, keepdims=True)
                )
                weights[t, rows, :TILE] = near.astype(jnp.bfloat16)
                weights[t, rows, TILE:] = far.astype(jnp.bfloat16)
            mixed = jnp.dot(
                weights[t],
                values[t * keys_total : (t + 1) * keys_total],
                preferred_element_type=jnp.float32,
            )
            for h in range(GROUP):
                out_ref[t * TILE : (t + 1) * TILE, h * HEAD : (h + 1) * HEAD] = (
                    mixed[h * TILE : (h + 1) * TILE] / totals[h]
                ).astype(jnp.bfloat16)

    return pl.pallas_call(
        kernel,
        out_shape=jax.ShapeDtypeStruct((2 * TILE, GROUP * HEAD), jnp.bfloat16),
        in_specs=[pl.BlockSpec(memory_space=pltpu.HBM)] * 3
        + [pl.BlockSpec(memory_space=pltpu.VMEM)] * (1 + 2 * count),
        out_specs=pl.BlockSpec(memory_space=pltpu.VMEM),
        scratch_shapes=[
            pltpu.VMEM((2 * keys_total, HEAD), jnp.bfloat16),
            pltpu.VMEM((2 * keys_total, HEAD), jnp.bfloat16),
            pltpu.VMEM((2, GROUP * TILE, keys_total), jnp.float32),
            pltpu.VMEM((2, GROUP * TILE, keys_total), jnp.bfloat16),
            pltpu.VMEM((2, 8, keys_total), jnp.float32),
            pltpu.VMEM((2 * TILE, GROUP * HEAD), jnp.bfloat16),
            pltpu.SMEM((2, ANC), jnp.int32),
            pltpu.SMEM((TILES,), jnp.int32),
            pltpu.SMEM((TILES,), jnp.int32),
            pltpu.SMEM((2 * ANC,), jnp.int32),
            pltpu.SemaphoreType.DMA((3,)),
        ],
        compiler_params=pltpu.CompilerParams(vmem_limit_bytes=28 << 20),
        name="attend",
    )(
        *(pltpu.with_memory_space_constraint(a, pltpu.HBM) for a in (ancestors, tile_of_slot, query)),
        own,
        *mine,
        *theirs,
    )


def fetch(weight, weight_other):
    def kernel(weight_ref, other_ref, out_ref, sem):
        y, c = lax.axis_index("y"), lax.axis_index("c")
        sign = 1 - 2 * c
        copies = []
        for hops in range(NY):
            column = pl.multiple_of((lax.rem(y + hops * sign + NY, NY) * 2 + c) * 1024, 1024)
            for ref, row in ((weight_ref, 0), (other_ref, 512)):
                copies.append(
                    pltpu.make_async_copy(
                        ref.at[:, pl.ds(column, 1024)], out_ref.at[hops, pl.ds(row, 512)], sem
                    )
                )
        for copy in copies:
            copy.start()
        for copy in copies:
            copy.wait()

    return pl.pallas_call(
        kernel,
        out_shape=pltpu.VMEM((NY, 1024, 1024), jnp.bfloat16),
        in_specs=[pl.BlockSpec(memory_space=pltpu.HBM)] * 2,
        out_specs=pl.BlockSpec(memory_space=pltpu.VMEM),
        scratch_shapes=[pltpu.SemaphoreType.DMA],
        compiler_params=pltpu.CompilerParams(vmem_limit_bytes=12 << 20),
        name="fetch",
    )(
        pltpu.with_memory_space_constraint(weight, pltpu.HBM),
        pltpu.with_memory_space_constraint(weight_other, pltpu.HBM),
    )


def project(attended, attended_other, weights, parts, added=(), dtype=jnp.bfloat16):
    count = len(parts)
    sizes = [2 * TILE if tile is None else TILE for _, tile in parts]

    def kernel(a_ref, b_ref, w_ref, *rest):
        added_refs, out_refs = rest[: len(added)], rest[len(added) :]
        c = lax.axis_index("c")
        for k, ((hops, tile), rows) in enumerate(zip(parts, sizes)):
            row = 0 if tile is None else pl.multiple_of((c if tile == 0 else 1 - c) * TILE, TILE)
            for n in range(0, 1024, 256):
                term = jnp.dot(
                    a_ref[pl.ds(row, rows)],
                    w_ref[hops, 0:512, n : n + 256],
                    preferred_element_type=jnp.float32,
                )
                term += jnp.dot(
                    b_ref[pl.ds(row, rows)],
                    w_ref[hops, 512:1024, n : n + 256],
                    preferred_element_type=jnp.float32,
                )
                if added:
                    term += added_refs[k][:, n : n + 256].astype(jnp.float32)
                out_refs[k][:, n : n + 256] = term.astype(dtype)

    return pl.pallas_call(
        kernel,
        out_shape=[jax.ShapeDtypeStruct((rows, 1024), dtype) for rows in sizes],
        in_specs=[pl.BlockSpec(memory_space=pltpu.VMEM)] * (3 + len(added)),
        out_specs=[pl.BlockSpec(memory_space=pltpu.VMEM)] * count,
        compiler_params=pltpu.CompilerParams(vmem_limit_bytes=16 << 20),
        name="project",
    )(attended, attended_other, weights, *added)


def layer(query, keys_values, ancestors, tile_of_slot, residual, norm_gain, out_weight):
    y, c = lax.axis_index("y"), lax.axis_index("c")
    own = lax.dynamic_slice_in_dim(keys_values, y * HEAD, HEAD, 2).reshape(BLOCK, HEAD)
    weight_other = other_core(out_weight)
    weights = fetch(out_weight, weight_other)
    mine, theirs = gather_pairs(own, c)
    attended = attend(query, own, mine, theirs, ancestors, tile_of_slot)
    args = (attended, other_core(attended), weights)
    across0, across1 = project(*args, [(2, 0), (2, 1)])
    relay_ahead = along_y(across0, 1)
    relay_back = along_y(across1, -1)
    direct1, direct0 = project(*args, [(1, 1), (3, 0)])
    from_back1 = along_y(direct1, 1)
    from_ahead0 = along_y(direct0, -1)
    joined0, joined1 = project(*args, [(1, 0), (3, 1)], (relay_ahead, relay_back))
    from_back0 = along_y(joined0, 1)
    from_ahead1 = along_y(joined1, -1)
    (here,) = project(*args, [(0, None)], (), jnp.float32)
    share0 = from_back0.astype(jnp.float32) + from_ahead0.astype(jnp.float32)
    share1 = from_ahead1.astype(jnp.float32) + from_back1.astype(jnp.float32)
    total = here + jnp.where(
        c == 0,
        jnp.concatenate([share0, share1], axis=0),
        jnp.concatenate([share1, share0], axis=0),
    )
    hidden_out = (residual.astype(jnp.float32) + total).astype(jnp.bfloat16)
    hidden_f32 = hidden_out.astype(jnp.float32)
    squares = jnp.sum(hidden_f32 * hidden_f32, axis=1)
    copies = jnp.broadcast_to(squares[None, None], (NY * NC, 1, squares.shape[0]))
    mean_sq = jnp.sum(lax.all_to_all(copies, ("y", "c"), 0, 0, tiled=True), axis=(0, 1)) / D
    normed = hidden_f32 * lax.rsqrt(mean_sq + 1e-05)[:, None] * norm_gain[None, :]
    return (hidden_out, normed.astype(jnp.bfloat16))


def solution(mesh):
    fine = Mesh(mesh.devices.reshape(NZ, NX, NY, NC), AXES)
    rows, columns = ("z", "x"), ("y", "c")
    return jax.shard_map(
        layer,
        mesh=fine,
        in_specs=(
            P(rows, columns),
            P(None, rows, None),
            P(rows, None),
            P(),
            P(rows, columns),
            P(columns),
            P(columns, None),
        ),
        out_specs=(P(rows, columns), P(rows, columns)),
        check_vma=False,
    )
```

profile of v0, /device:TPU:1, one launch (start us, length us, event | category | flops | bytes accessed | tf_op | source)
XLA Modules:
  0.0 98.0 jit_solution(17639996841917964562)
XLA Ops:
  0.6 3.3 %collective-permute-start.24 = (bf16[512,8192]{1,0:T(8,128)(2,1)}, bf16[512,8192]{1,0:T(8,128)(2,1)}, u32[]{:S(2)}, u32[]{:S(2)}) collective-permute-start(bf16[512,8192]{1,0:T(8,128)(2,1)} %weight_ref.1), channel_id=1, source_target_pairs={{0,1},{1,0},{2,3},{3,2},{4,5},{5,4},{6,7},{7,6},{8,9},{9,8},{10,11... | collective-permute-start | bytes 25165832 | tf_op jit(solution)/shard_map/ppermute | solution.py:54
  4.0 4.7 %collective-permute-start.1 = (bf16[512,128]{1,0:T(8,128)(2,1)S(1)}, bf16[512,128]{1,0:T(8,128)(2,1)S(1)}, u32[]{:S(2)}, u32[]{:S(2)}) collective-permute-start(bf16[512,128]{1,0:T(8,128)(2,1)S(1)} %bitcast.1), channel_id=1, source_target_pairs={{0,64},{1,193},{2,66},{3,195},{4,68},{5,197},{6,70},{7,199},{8,72}... | collective-permute-start | bytes 393224 | tf_op jit(solution)/shard_map/ppermute | solution.py:36
  9.9 4.4 %collective-permute-start.3 = (bf16[256,128]{1,0:T(8,128)(2,1)S(1)}, bf16[256,128]{1,0:T(8,128)(2,1)S(1)}, u32[]{:S(2)}, u32[]{:S(2)}) collective-permute-start(bf16[256,128]{1,0:T(8,128)(2,1)S(1)} %constant_dynamic-slice_fusion), channel_id=1, source_target_pairs={{0,128},{1,129},{2,130},{3,131},{4,132},{5,133},{6,134},{7,135},{8... | collective-permute-start | bytes 196616 | tf_op jit(solution)/shard_map/ppermute | solution.py:36
  14.7 3.1 %collective-permute-done.2 = bf16[512,128]{1,0:T(8,128)(2,1)S(1)} collective-permute-done((bf16[512,128]{1,0:T(8,128)(2,1)S(1)}, bf16[512,128]{1,0:T(8,128)(2,1)S(1)}, u32[]{:S(2)}, u32[]{:S(2)}) %collective-permute-start.2) | collective-permute-done | bytes 131104 | tf_op jit(solution)/shard_map/ppermute | solution.py:36
  18.3 5.9 %collective-permute-start.14 = (bf16[768,128]{1,0:T(8,128)(2,1)S(1)}, bf16[768,128]{1,0:T(8,128)(2,1)S(1)}, u32[]{:S(2)}, u32[]{:S(2)}) collective-permute-start(bf16[768,128]{1,0:T(8,128)(2,1)S(1)} %constant_dynamic-update-slice_fusion.rest_2_), channel_id=1, source_target_pairs={{0,1},{1,0},{2,3},{3,2},{4,5},{5,4},{6,7},{7,6},{8,9},{9,8},{10,11... | collective-permute-start | bytes 589832 | tf_op jit(solution)/shard_map/ppermute | solution.py:54
  24.1 1.2 %collective-permute-start.7 = (bf16[768,128]{1,0:T(8,128)(2,1)S(1)}, bf16[768,128]{1,0:T(8,128)(2,1)S(1)}, u32[]{:S(2)}, u32[]{:S(2)}) collective-permute-start(bf16[768,128]{1,0:T(8,128)(2,1)S(1)} %constant_dynamic-update-slice_fusion.rest_2_), channel_id=1, source_target_pairs={{0,24},{1,9},{2,26},{3,11},{4,28},{5,13},{6,30},{7,15},{8,0},{9,17... | collective-permute-start | bytes 589832 | tf_op jit(solution)/shard_map/ppermute | solution.py:42
  25.4 1.5 %collective-permute-start.6 = (bf16[768,128]{1,0:T(8,128)(2,1)S(1)}, bf16[768,128]{1,0:T(8,128)(2,1)S(1)}, u32[]{:S(2)}, u32[]{:S(2)}) collective-permute-start(bf16[768,128]{1,0:T(8,128)(2,1)S(1)} %constant_dynamic-update-slice_fusion.rest_2_), channel_id=1, source_target_pairs={{0,8},{1,25},{2,10},{3,27},{4,12},{5,29},{6,14},{7,31},{8,16},{9,1... | collective-permute-start | bytes 589832 | tf_op jit(solution)/shard_map/ppermute | solution.py:42
  27.1 1.1 %collective-permute-done.12.rest_11_ = bf16[512,128]{1,0:T(8,128)(2,1)S(1)} collective-permute-done((bf16[512,128]{1,0:T(8,128)(2,1)S(1)}, bf16[512,128]{1,0:T(8,128)(2,1)S(1)}, u32[]{:S(2)}, u32[]{:S(2)}) %collective-permute-start.12) | collective-permute-done | bytes 131104 | tf_op jit(solution)/shard_map/ppermute | solution.py:54
  28.5 1.4 %collective-permute-done.7.rest_6_ = bf16[768,128]{1,0:T(8,128)(2,1)S(1)} collective-permute-done((bf16[768,128]{1,0:T(8,128)(2,1)S(1)}, bf16[768,128]{1,0:T(8,128)(2,1)S(1)}, u32[]{:S(2)}, u32[]{:S(2)}) %collective-permute-start.7) | collective-permute-done | bytes 196640 | tf_op jit(solution)/shard_map/ppermute | solution.py:42
  29.9 2.3 %collective-permute-start.4 = (bf16[1280,128]{1,0:T(8,128)(2,1)S(1)}, bf16[1280,128]{1,0:T(8,128)(2,1)S(1)}, u32[]{:S(2)}, u32[]{:S(2)}) collective-permute-start(bf16[1280,128]{1,0:T(8,128)(2,1)S(1)} %pad_maximum_fusion), channel_id=1, source_target_pairs={{0,8},{1,25},{2,10},{3,27},{4,12},{5,29},{6,14},{7,31},{8,16},{9,1... | collective-permute-start | bytes 983048 | tf_op jit(solution)/shard_map/ppermute | solution.py:42
  32.2 1.3 %collective-permute-start.11 = (bf16[384,128]{1,0:T(8,128)(2,1)S(1)}, bf16[384,128]{1,0:T(8,128)(2,1)S(1)}, u32[]{:S(2)}, u32[]{:S(2)}) collective-permute-start(bf16[384,128]{1,0:T(8,128)(2,1)S(1)} %slice.19), channel_id=1, source_target_pairs={{0,24},{1,9},{2,26},{3,11},{4,28},{5,13},{6,30},{7,15},{8,0},{9,17... | collective-permute-start | bytes 294920 | tf_op jit(solution)/shard_map/ppermute | solution.py:42
  33.5 1.5 %collective-permute-start.10 = (bf16[384,128]{1,0:T(8,128)(2,1)S(1)}, bf16[384,128]{1,0:T(8,128)(2,1)S(1)}, u32[]{:S(2)}, u32[]{:S(2)}) collective-permute-start(bf16[384,128]{1,0:T(8,128)(2,1)S(1)} %slice.18), channel_id=1, source_target_pairs={{0,8},{1,25},{2,10},{3,27},{4,12},{5,29},{6,14},{7,31},{8,16},{9,1... | collective-permute-start | bytes 294920 | tf_op jit(solution)/shard_map/ppermute | solution.py:42
  35.0 4.3 %collective-permute-done.11.rest_10_ = bf16[384,128]{1,0:T(8,128)(2,1)S(1)} collective-permute-done((bf16[384,128]{1,0:T(8,128)(2,1)S(1)}, bf16[384,128]{1,0:T(8,128)(2,1)S(1)}, u32[]{:S(2)}, u32[]{:S(2)}) %collective-permute-start.11) | collective-permute-done | bytes 98336 | tf_op jit(solution)/shard_map/ppermute | solution.py:42
  39.3 2.1 %collective-permute-start.18 = (bf16[768,128]{1,0:T(8,128)(2,1)S(1)}, bf16[768,128]{1,0:T(8,128)(2,1)S(1)}, u32[]{:S(2)}, u32[]{:S(2)}) collective-permute-start(bf16[768,128]{1,0:T(8,128)(2,1)S(1)} %collective-permute-done.7.rest_6_), channel_id=1, source_target_pairs={{0,1},{1,0},{2,3},{3,2},{4,5},{5,4},{6,7},{7,6},{8,9},{9,8},{10,11... | collective-permute-start | bytes 589832 | tf_op jit(solution)/shard_map/ppermute | solution.py:54
  41.4 1.6 %collective-permute-start.17 = (bf16[768,128]{1,0:T(8,128)(2,1)S(1)}, bf16[768,128]{1,0:T(8,128)(2,1)S(1)}, u32[]{:S(2)}, u32[]{:S(2)}) collective-permute-start(bf16[768,128]{1,0:T(8,128)(2,1)S(1)} %collective-permute-done.6.rest_5_), channel_id=1, source_target_pairs={{0,1},{1,0},{2,3},{3,2},{4,5},{5,4},{6,7},{7,6},{8,9},{9,8},{10,11... | collective-permute-start | bytes 589832 | tf_op jit(solution)/shard_map/ppermute | solution.py:54
  44.3 2.7 %collective-permute-start.8 = (bf16[640,128]{1,0:T(8,128)(2,1)S(1)}, bf16[640,128]{1,0:T(8,128)(2,1)S(1)}, u32[]{:S(2)}, u32[]{:S(2)}) collective-permute-start(bf16[640,128]{1,0:T(8,128)(2,1)S(1)} %slice.16), channel_id=1, source_target_pairs={{0,8},{1,25},{2,10},{3,27},{4,12},{5,29},{6,14},{7,31},{8,16},{9,1... | collective-permute-start | bytes 491528 | tf_op jit(solution)/shard_map/ppermute | solution.py:42
  47.5 2.2 %collective-permute-done.9.rest_8_ = bf16[640,128]{1,0:T(8,128)(2,1)S(1)} collective-permute-done((bf16[640,128]{1,0:T(8,128)(2,1)S(1)}, bf16[640,128]{1,0:T(8,128)(2,1)S(1)}, u32[]{:S(2)}, u32[]{:S(2)}) %collective-permute-start.9) | collective-permute-done | bytes 163872 | tf_op jit(solution)/shard_map/ppermute | solution.py:42
  49.7 1.7 %collective-permute-start.20 = (bf16[640,128]{1,0:T(8,128)(2,1)S(1)}, bf16[640,128]{1,0:T(8,128)(2,1)S(1)}, u32[]{:S(2)}, u32[]{:S(2)}) collective-permute-start(bf16[640,128]{1,0:T(8,128)(2,1)S(1)} %collective-permute-done.9.rest_8_), channel_id=1, source_target_pairs={{0,1},{1,0},{2,3},{3,2},{4,5},{5,4},{6,7},{7,6},{8,9},{9,8},{10,11... | collective-permute-start | bytes 491528 | tf_op jit(solution)/shard_map/ppermute | solution.py:54
  51.4 2.1 %collective-permute-start.19 = (bf16[640,128]{1,0:T(8,128)(2,1)S(1)}, bf16[640,128]{1,0:T(8,128)(2,1)S(1)}, u32[]{:S(2)}, u32[]{:S(2)}) collective-permute-start(bf16[640,128]{1,0:T(8,128)(2,1)S(1)} %collective-permute-done.8.rest_7_), channel_id=1, source_target_pairs={{0,1},{1,0},{2,3},{3,2},{4,5},{5,4},{6,7},{7,6},{8,9},{9,8},{10,11... | collective-permute-start | bytes 491528 | tf_op jit(solution)/shard_map/ppermute | solution.py:54
  53.5 1.0 %collective-permute-done.19.rest_18_ = bf16[640,128]{1,0:T(8,128)(2,1)S(1)} collective-permute-done((bf16[640,128]{1,0:T(8,128)(2,1)S(1)}, bf16[640,128]{1,0:T(8,128)(2,1)S(1)}, u32[]{:S(2)}, u32[]{:S(2)}) %collective-permute-start.19) | collective-permute-done | bytes 163872 | tf_op jit(solution)/shard_map/ppermute | solution.py:54
  54.5 6.0 %attend.1.a_ref = bf16[256,512]{1,0:T(8,128)(2,1)S(1)} custom-call(s32[2,12]{1,0:T(2,128)} %ancestors_hbm.1, s32[64]{0:T(128)} %tile_of_slot_hbm.1, bf16[256,512]{1,0:T(8,128)(2,1)} %query_hbm.1, bf16[512,128]{1,0:T(8,128)(2,1)S(1)} %bitcast.5, bf16[512,128]{1,0:T(8,128)(2,1)S(1)} %collective-permute-done.rest_0_, ...), custom_call_target="tpu_custom_call" | custom-call | tf_op jit(solution)/shard_map/attend/pallas_call | solution.py:238
  61.0 3.4 %fetch.1.w_ref = bf16[4,1024,1024]{2,1,0:T(8,128)(2,1)S(1)} custom-call(bf16[512,8192]{1,0:T(8,128)(2,1)} %weight_ref.1, bf16[512,8192]{1,0:T(8,128)(2,1)} %collective-permute-done.24.other_ref), custom_call_target="tpu_custom_call" | custom-call | tf_op jit(solution)/shard_map/fetch/pallas_call | solution.py:285
  65.2 2.8 %collective-permute-start.25 = (bf16[128,1024]{1,0:T(8,128)(2,1)S(1)}, bf16[128,1024]{1,0:T(8,128)(2,1)S(1)}, u32[]{:S(2)}, u32[]{:S(2)}) collective-permute-start(bf16[128,1024]{1,0:T(8,128)(2,1)S(1)} %get-tuple-element.8), channel_id=1, source_target_pairs={{0,2},{1,7},{2,4},{3,1},{4,6},{5,3},{6,0},{7,5},{8,10},{9,15},{10,... | collective-permute-start | bytes 786440 | tf_op jit(solution)/shard_map/ppermute | solution.py:48
  68.9 4.4 %collective-permute-done.25.rest_0_ = bf16[128,1024]{1,0:T(8,128)(2,1)S(1)} collective-permute-done((bf16[128,1024]{1,0:T(8,128)(2,1)S(1)}, bf16[128,1024]{1,0:T(8,128)(2,1)S(1)}, u32[]{:S(2)}, u32[]{:S(2)}) %collective-permute-start.25) | collective-permute-done | bytes 262176 | tf_op jit(solution)/shard_map/ppermute | solution.py:48
  73.4 1.8 %collective-permute-done.26.rest_1_ = bf16[128,1024]{1,0:T(8,128)(2,1)S(1)} collective-permute-done((bf16[128,1024]{1,0:T(8,128)(2,1)S(1)}, bf16[128,1024]{1,0:T(8,128)(2,1)S(1)}, u32[]{:S(2)}, u32[]{:S(2)}) %collective-permute-start.26) | collective-permute-done | bytes 262176 | tf_op jit(solution)/shard_map/ppermute | solution.py:48
  75.9 1.9 %collective-permute-start.27 = (bf16[128,1024]{1,0:T(8,128)(2,1)S(1)}, bf16[128,1024]{1,0:T(8,128)(2,1)}, u32[]{:S(2)}, u32[]{:S(2)}) collective-permute-start(bf16[128,1024]{1,0:T(8,128)(2,1)S(1)} %get-tuple-element.10), channel_id=1, source_target_pairs={{0,2},{1,7},{2,4},{3,1},{4,6},{5,3},{6,0},{7,5},{8,10},{9,15},{10,... | collective-permute-start | bytes 786440 | tf_op jit(solution)/shard_map/ppermute | solution.py:48
  77.9 1.4 %collective-permute-start.29 = (bf16[128,1024]{1,0:T(8,128)(2,1)S(1)}, bf16[128,1024]{1,0:T(8,128)(2,1)S(1)}, u32[]{:S(2)}, u32[]{:S(2)}) collective-permute-start(bf16[128,1024]{1,0:T(8,128)(2,1)S(1)} %get-tuple-element.12), channel_id=1, source_target_pairs={{0,6},{1,3},{2,0},{3,5},{4,2},{5,7},{6,4},{7,1},{8,14},{9,11},{10,... | collective-permute-start | bytes 786440 | tf_op jit(solution)/shard_map/ppermute | solution.py:48
  79.3 3.4 %copy-done.2 = bf16[4,1024,1024]{2,1,0:T(8,128)(2,1)S(1)} copy-done((bf16[4,1024,1024]{2,1,0:T(8,128)(2,1)S(1)}, bf16[4,1024,1024]{2,1,0:T(8,128)(2,1)}, u32[]{:S(2)}) %copy-start.2) | copy-done | bytes 8388632
  83.4 1.0 %convert_add_fusion.1 = f32[128,1024]{1,0:T(8,128)S(1)} fusion(bf16[128,1024]{1,0:T(8,128)(2,1)S(1)} %collective-permute-done.28, bf16[128,1024]{1,0:T(8,128)(2,1)} %collective-permute-done.27), kind=kLoop, calls=%fused_computation.10 | loop fusion | flops 393216 | bytes 1048576 | tf_op jit(solution)/shard_map/add | solution.py:351
  84.4 2.6 %collective-permute-done.30 = bf16[128,1024]{1,0:T(8,128)(2,1)S(1)} collective-permute-done((bf16[128,1024]{1,0:T(8,128)(2,1)S(1)}, bf16[128,1024]{1,0:T(8,128)(2,1)S(1)}, u32[]{:S(2)}, u32[]{:S(2)}) %collective-permute-start.30) | collective-permute-done | bytes 262176 | tf_op jit(solution)/shard_map/ppermute | solution.py:48
  87.9 9.1 %all_to_all.5 = f32[8,1,256]{2,1,0:T(1,128)S(1)} all-to-all(f32[8,1,256]{2,1,0:T(1,128)S(1)} %broadcast_in_dim.2), channel_id=1, replica_groups=mesh['z'=8,'x'=4,'y'=4,'c'=2] {'y','c'}, dimensions={0} | all-to-all | bytes 16384 | tf_op jit(solution)/shard_map/all_to_all | solution.py:362
  97.0 1.0 %fusion.2 = bf16[256,1024]{1,0:T(8,128)(2,1)} fusion(bf16[256,1024]{1,0:T(8,128)(2,1)S(1)} %get-tuple-element.15, f32[1024]{0:T(1024)S(1)} %copy-done.5, f32[256]{0:T(256)S(1)} %add_rsqrt_fusion), kind=kLoop, calls=%fused_computation.4 | loop fusion | flops 1048576 | bytes 1053696 | tf_op jit(solution)/shard_map/convert_element_type | solution.py:364
  (65 shorter events, 9.0 us)
Async XLA Ops:
  0.6 60.4 %collective-permute-start.24 = (bf16[512,8192]{1,0:T(8,128)(2,1)}, bf16[512,8192]{1,0:T(8,128)(2,1)}, u32[]{:S(2)}, u32[]{:S(2)}) collective-permute-start(bf16[512,8192]{1,0:T(8,128)(2,1)} %weight_ref.1), channel_id=1, source_target_pairs={{0,1},{1,0},{2,3},{3,2},{4,5},{5,4},{6,7},{7,6},{8,9},{9,8},{10,11... | collective-permute-start | bytes 25165832 | tf_op jit(solution)/shard_map/ppermute | solution.py:54
  4.0 10.8 %collective-permute-start.1 = (bf16[512,128]{1,0:T(8,128)(2,1)S(1)}, bf16[512,128]{1,0:T(8,128)(2,1)S(1)}, u32[]{:S(2)}, u32[]{:S(2)}) collective-permute-start(bf16[512,128]{1,0:T(8,128)(2,1)S(1)} %bitcast.1), channel_id=1, source_target_pairs={{0,64},{1,193},{2,66},{3,195},{4,68},{5,197},{6,70},{7,199},{8,72}... | collective-permute-start | bytes 393224 | tf_op jit(solution)/shard_map/ppermute | solution.py:36
  8.6 9.2 %collective-permute-start.2 = (bf16[512,128]{1,0:T(8,128)(2,1)S(1)}, bf16[512,128]{1,0:T(8,128)(2,1)S(1)}, u32[]{:S(2)}, u32[]{:S(2)}) collective-permute-start(bf16[512,128]{1,0:T(8,128)(2,1)S(1)} %bitcast.2), channel_id=1, source_target_pairs={{0,96},{1,161},{2,98},{3,163},{4,100},{5,165},{6,102},{7,167},{8,1... | collective-permute-start | bytes 393224 | tf_op jit(solution)/shard_map/ppermute | solution.py:36
  9.3 16.0 %collective-permute-start = (bf16[512,128]{1,0:T(8,128)(2,1)S(1)}, bf16[512,128]{1,0:T(8,128)(2,1)S(1)}, u32[]{:S(2)}, u32[]{:S(2)}) collective-permute-start(bf16[512,128]{1,0:T(8,128)(2,1)S(1)} %bitcast.3), channel_id=1, source_target_pairs={{0,32},{1,225},{2,34},{3,227},{4,36},{5,229},{6,38},{7,231},{8,40}... | collective-permute-start | bytes 393224 | tf_op jit(solution)/shard_map/ppermute | solution.py:36
  9.9 8.4 %collective-permute-start.3 = (bf16[256,128]{1,0:T(8,128)(2,1)S(1)}, bf16[256,128]{1,0:T(8,128)(2,1)S(1)}, u32[]{:S(2)}, u32[]{:S(2)}) collective-permute-start(bf16[256,128]{1,0:T(8,128)(2,1)S(1)} %constant_dynamic-slice_fusion), channel_id=1, source_target_pairs={{0,128},{1,129},{2,130},{3,131},{4,132},{5,133},{6,134},{7,135},{8... | collective-permute-start | bytes 196616 | tf_op jit(solution)/shard_map/ppermute | solution.py:36
  14.7 12.1 %collective-permute-start.13 = (bf16[512,128]{1,0:T(8,128)(2,1)S(1)}, bf16[512,128]{1,0:T(8,128)(2,1)S(1)}, u32[]{:S(2)}, u32[]{:S(2)}) collective-permute-start(bf16[512,128]{1,0:T(8,128)(2,1)S(1)} %collective-permute-done.1.rest_1_), channel_id=1, source_target_pairs={{0,1},{1,0},{2,3},{3,2},{4,5},{5,4},{6,7},{7,6},{8,9},{9,8},{10,11... | collective-permute-start | bytes 393224 | tf_op jit(solution)/shard_map/ppermute | solution.py:54
  18.3 15.2 %collective-permute-start.14 = (bf16[768,128]{1,0:T(8,128)(2,1)S(1)}, bf16[768,128]{1,0:T(8,128)(2,1)S(1)}, u32[]{:S(2)}, u32[]{:S(2)}) collective-permute-start(bf16[768,128]{1,0:T(8,128)(2,1)S(1)} %constant_dynamic-update-slice_fusion.rest_2_), channel_id=1, source_target_pairs={{0,1},{1,0},{2,3},{3,2},{4,5},{5,4},{6,7},{7,6},{8,9},{9,8},{10,11... | collective-permute-start | bytes 589832 | tf_op jit(solution)/shard_map/ppermute | solution.py:54
  24.1 5.7 %collective-permute-start.7 = (bf16[768,128]{1,0:T(8,128)(2,1)S(1)}, bf16[768,128]{1,0:T(8,128)(2,1)S(1)}, u32[]{:S(2)}, u32[]{:S(2)}) collective-permute-start(bf16[768,128]{1,0:T(8,128)(2,1)S(1)} %constant_dynamic-update-slice_fusion.rest_2_), channel_id=1, source_target_pairs={{0,24},{1,9},{2,26},{3,11},{4,28},{5,13},{6,30},{7,15},{8,0},{9,17... | collective-permute-start | bytes 589832 | tf_op jit(solution)/shard_map/ppermute | solution.py:42
  25.4 6.8 %collective-permute-start.6 = (bf16[768,128]{1,0:T(8,128)(2,1)S(1)}, bf16[768,128]{1,0:T(8,128)(2,1)S(1)}, u32[]{:S(2)}, u32[]{:S(2)}) collective-permute-start(bf16[768,128]{1,0:T(8,128)(2,1)S(1)} %constant_dynamic-update-slice_fusion.rest_2_), channel_id=1, source_target_pairs={{0,8},{1,25},{2,10},{3,27},{4,12},{5,29},{6,14},{7,31},{8,16},{9,1... | collective-permute-start | bytes 589832 | tf_op jit(solution)/shard_map/ppermute | solution.py:42
  26.8 1.3 %collective-permute-start.12 = (bf16[512,128]{1,0:T(8,128)(2,1)S(1)}, bf16[512,128]{1,0:T(8,128)(2,1)S(1)}, u32[]{:S(2)}, u32[]{:S(2)}) collective-permute-start(bf16[512,128]{1,0:T(8,128)(2,1)S(1)} %collective-permute-done.rest_0_), channel_id=1, source_target_pairs={{0,1},{1,0},{2,3},{3,2},{4,5},{5,4},{6,7},{7,6},{8,9},{9,8},{10,11... | collective-permute-start | bytes 393224 | tf_op jit(solution)/shard_map/ppermute | solution.py:54
  28.2 14.8 %collective-permute-start.5 = (bf16[1280,128]{1,0:T(8,128)(2,1)S(1)}, bf16[1280,128]{1,0:T(8,128)(2,1)S(1)}, u32[]{:S(2)}, u32[]{:S(2)}) collective-permute-start(bf16[1280,128]{1,0:T(8,128)(2,1)S(1)} %pad_maximum_fusion), channel_id=1, source_target_pairs={{0,24},{1,9},{2,26},{3,11},{4,28},{5,13},{6,30},{7,15},{8,0},{9,17... | collective-permute-start | bytes 983048 | tf_op jit(solution)/shard_map/ppermute | solution.py:42
  29.9 13.1 %collective-permute-start.4 = (bf16[1280,128]{1,0:T(8,128)(2,1)S(1)}, bf16[1280,128]{1,0:T(8,128)(2,1)S(1)}, u32[]{:S(2)}, u32[]{:S(2)}) collective-permute-start(bf16[1280,128]{1,0:T(8,128)(2,1)S(1)} %pad_maximum_fusion), channel_id=1, source_target_pairs={{0,8},{1,25},{2,10},{3,27},{4,12},{5,29},{6,14},{7,31},{8,16},{9,1... | collective-permute-start | bytes 983048 | tf_op jit(solution)/shard_map/ppermute | solution.py:42
  32.2 7.1 %collective-permute-start.11 = (bf16[384,128]{1,0:T(8,128)(2,1)S(1)}, bf16[384,128]{1,0:T(8,128)(2,1)S(1)}, u32[]{:S(2)}, u32[]{:S(2)}) collective-permute-start(bf16[384,128]{1,0:T(8,128)(2,1)S(1)} %slice.19), channel_id=1, source_target_pairs={{0,24},{1,9},{2,26},{3,11},{4,28},{5,13},{6,30},{7,15},{8,0},{9,17... | collective-permute-start | bytes 294920 | tf_op jit(solution)/shard_map/ppermute | solution.py:42
  33.5 7.9 %collective-permute-start.10 = (bf16[384,128]{1,0:T(8,128)(2,1)S(1)}, bf16[384,128]{1,0:T(8,128)(2,1)S(1)}, u32[]{:S(2)}, u32[]{:S(2)}) collective-permute-start(bf16[384,128]{1,0:T(8,128)(2,1)S(1)} %slice.18), channel_id=1, source_target_pairs={{0,8},{1,25},{2,10},{3,27},{4,12},{5,29},{6,14},{7,31},{8,16},{9,1... | collective-permute-start | bytes 294920 | tf_op jit(solution)/shard_map/ppermute | solution.py:42
  39.3 5.0 %collective-permute-start.18 = (bf16[768,128]{1,0:T(8,128)(2,1)S(1)}, bf16[768,128]{1,0:T(8,128)(2,1)S(1)}, u32[]{:S(2)}, u32[]{:S(2)}) collective-permute-start(bf16[768,128]{1,0:T(8,128)(2,1)S(1)} %collective-permute-done.7.rest_6_), channel_id=1, source_target_pairs={{0,1},{1,0},{2,3},{3,2},{4,5},{5,4},{6,7},{7,6},{8,9},{9,8},{10,11... | collective-permute-start | bytes 589832 | tf_op jit(solution)/shard_map/ppermute | solution.py:54
  41.4 5.7 %collective-permute-start.17 = (bf16[768,128]{1,0:T(8,128)(2,1)S(1)}, bf16[768,128]{1,0:T(8,128)(2,1)S(1)}, u32[]{:S(2)}, u32[]{:S(2)}) collective-permute-start(bf16[768,128]{1,0:T(8,128)(2,1)S(1)} %collective-permute-done.6.rest_5_), channel_id=1, source_target_pairs={{0,1},{1,0},{2,3},{3,2},{4,5},{5,4},{6,7},{7,6},{8,9},{9,8},{10,11... | collective-permute-start | bytes 589832 | tf_op jit(solution)/shard_map/ppermute | solution.py:54
  43.0 1.3 %collective-permute-start.22 = (bf16[384,128]{1,0:T(8,128)(2,1)S(1)}, bf16[384,128]{1,0:T(8,128)(2,1)S(1)}, u32[]{:S(2)}, u32[]{:S(2)}) collective-permute-start(bf16[384,128]{1,0:T(8,128)(2,1)S(1)} %collective-permute-done.11.rest_10_), channel_id=1, source_target_pairs={{0,1},{1,0},{2,3},{3,2},{4,5},{5,4},{6,7},{7,6},{8,9},{9,8},{10,11... | collective-permute-start | bytes 294920 | tf_op jit(solution)/shard_map/ppermute | solution.py:54
  43.0 4.0 %collective-permute-start.21 = (bf16[384,128]{1,0:T(8,128)(2,1)S(1)}, bf16[384,128]{1,0:T(8,128)(2,1)S(1)}, u32[]{:S(2)}, u32[]{:S(2)}) collective-permute-start(bf16[384,128]{1,0:T(8,128)(2,1)S(1)} %collective-permute-done.10.rest_9_), channel_id=1, source_target_pairs={{0,1},{1,0},{2,3},{3,2},{4,5},{5,4},{6,7},{7,6},{8,9},{9,8},{10,11... | collective-permute-start | bytes 294920 | tf_op jit(solution)/shard_map/ppermute | solution.py:54
  44.3 5.4 %collective-permute-start.9 = (bf16[640,128]{1,0:T(8,128)(2,1)S(1)}, bf16[640,128]{1,0:T(8,128)(2,1)S(1)}, u32[]{:S(2)}, u32[]{:S(2)}) collective-permute-start(bf16[640,128]{1,0:T(8,128)(2,1)S(1)} %slice.17), channel_id=1, source_target_pairs={{0,24},{1,9},{2,26},{3,11},{4,28},{5,13},{6,30},{7,15},{8,0},{9,17... | collective-permute-start | bytes 491528 | tf_op jit(solution)/shard_map/ppermute | solution.py:42
  44.3 7.1 %collective-permute-start.8 = (bf16[640,128]{1,0:T(8,128)(2,1)S(1)}, bf16[640,128]{1,0:T(8,128)(2,1)S(1)}, u32[]{:S(2)}, u32[]{:S(2)}) collective-permute-start(bf16[640,128]{1,0:T(8,128)(2,1)S(1)} %slice.16), channel_id=1, source_target_pairs={{0,8},{1,25},{2,10},{3,27},{4,12},{5,29},{6,14},{7,31},{8,16},{9,1... | collective-permute-start | bytes 491528 | tf_op jit(solution)/shard_map/ppermute | solution.py:42
  47.0 7.5 %collective-permute-start.16 = (bf16[1280,128]{1,0:T(8,128)(2,1)S(1)}, bf16[1280,128]{1,0:T(8,128)(2,1)S(1)}, u32[]{:S(2)}, u32[]{:S(2)}) collective-permute-start(bf16[1280,128]{1,0:T(8,128)(2,1)S(1)} %collective-permute-done.5.rest_4_), channel_id=1, source_target_pairs={{0,1},{1,0},{2,3},{3,2},{4,5},{5,4},{6,7},{7,6},{8,9},{9,8},{10,11... | collective-permute-start | bytes 983048 | tf_op jit(solution)/shard_map/ppermute | solution.py:54
  47.1 7.5 %collective-permute-start.15 = (bf16[1280,128]{1,0:T(8,128)(2,1)S(1)}, bf16[1280,128]{1,0:T(8,128)(2,1)S(1)}, u32[]{:S(2)}, u32[]{:S(2)}) collective-permute-start(bf16[1280,128]{1,0:T(8,128)(2,1)S(1)} %collective-permute-done.4.rest_3_), channel_id=1, source_target_pairs={{0,1},{1,0},{2,3},{3,2},{4,5},{5,4},{6,7},{7,6},{8,9},{9,8},{10,11... | collective-permute-start | bytes 983048 | tf_op jit(solution)/shard_map/ppermute | solution.py:54
  49.7 3.8 %collective-permute-start.20 = (bf16[640,128]{1,0:T(8,128)(2,1)S(1)}, bf16[640,128]{1,0:T(8,128)(2,1)S(1)}, u32[]{:S(2)}, u32[]{:S(2)}) collective-permute-start(bf16[640,128]{1,0:T(8,128)(2,1)S(1)} %collective-permute-done.9.rest_8_), channel_id=1, source_target_pairs={{0,1},{1,0},{2,3},{3,2},{4,5},{5,4},{6,7},{7,6},{8,9},{9,8},{10,11... | collective-permute-start | bytes 491528 | tf_op jit(solution)/shard_map/ppermute | solution.py:54
  51.4 3.1 %collective-permute-start.19 = (bf16[640,128]{1,0:T(8,128)(2,1)S(1)}, bf16[640,128]{1,0:T(8,128)(2,1)S(1)}, u32[]{:S(2)}, u32[]{:S(2)}) collective-permute-start(bf16[640,128]{1,0:T(8,128)(2,1)S(1)} %collective-permute-done.8.rest_7_), channel_id=1, source_target_pairs={{0,1},{1,0},{2,3},{3,2},{4,5},{5,4},{6,7},{7,6},{8,9},{9,8},{10,11... | collective-permute-start | bytes 491528 | tf_op jit(solution)/shard_map/ppermute | solution.py:54
  60.6 3.9 %collective-permute-start.23 = (bf16[256,512]{1,0:T(8,128)(2,1)S(1)}, bf16[256,512]{1,0:T(8,128)(2,1)S(1)}, u32[]{:S(2)}, u32[]{:S(2)}) collective-permute-start(bf16[256,512]{1,0:T(8,128)(2,1)S(1)} %attend.1.a_ref), channel_id=1, source_target_pairs={{0,1},{1,0},{2,3},{3,2},{4,5},{5,4},{6,7},{7,6},{8,9},{9,8},{10,11... | collective-permute-start | bytes 786440 | tf_op jit(solution)/shard_map/ppermute | solution.py:54
  65.2 8.1 %collective-permute-start.25 = (bf16[128,1024]{1,0:T(8,128)(2,1)S(1)}, bf16[128,1024]{1,0:T(8,128)(2,1)S(1)}, u32[]{:S(2)}, u32[]{:S(2)}) collective-permute-start(bf16[128,1024]{1,0:T(8,128)(2,1)S(1)} %get-tuple-element.8), channel_id=1, source_target_pairs={{0,2},{1,7},{2,4},{3,1},{4,6},{5,3},{6,0},{7,5},{8,10},{9,15},{10,... | collective-permute-start | bytes 786440 | tf_op jit(solution)/shard_map/ppermute | solution.py:48
  68.1 7.1 %collective-permute-start.26 = (bf16[128,1024]{1,0:T(8,128)(2,1)S(1)}, bf16[128,1024]{1,0:T(8,128)(2,1)S(1)}, u32[]{:S(2)}, u32[]{:S(2)}) collective-permute-start(bf16[128,1024]{1,0:T(8,128)(2,1)S(1)} %get-tuple-element.9), channel_id=1, source_target_pairs={{0,6},{1,3},{2,0},{3,5},{4,2},{5,7},{6,4},{7,1},{8,14},{9,11},{10,... | collective-permute-start | bytes 786440 | tf_op jit(solution)/shard_map/ppermute | solution.py:48
  68.8 14.6 %collective-permute-start.28 = (bf16[128,1024]{1,0:T(8,128)(2,1)S(1)}, bf16[128,1024]{1,0:T(8,128)(2,1)S(1)}, u32[]{:S(2)}, u32[]{:S(2)}) collective-permute-start(bf16[128,1024]{1,0:T(8,128)(2,1)S(1)} %get-tuple-element.11), channel_id=1, source_target_pairs={{0,6},{1,3},{2,0},{3,5},{4,2},{5,7},{6,4},{7,1},{8,14},{9,11},{10,... | collective-permute-start | bytes 786440 | tf_op jit(solution)/shard_map/ppermute | solution.py:48
  75.9 21.2 %copy-start.5 = (f32[1024]{0:T(1024)S(1)}, f32[1024]{0:T(1024)}, u32[]{:S(2)}) copy-start(f32[1024]{0:T(1024)} %param.12) | copy-start | bytes 12292
  75.9 7.5 %collective-permute-start.27 = (bf16[128,1024]{1,0:T(8,128)(2,1)S(1)}, bf16[128,1024]{1,0:T(8,128)(2,1)}, u32[]{:S(2)}, u32[]{:S(2)}) collective-permute-start(bf16[128,1024]{1,0:T(8,128)(2,1)S(1)} %get-tuple-element.10), channel_id=1, source_target_pairs={{0,2},{1,7},{2,4},{3,1},{4,6},{5,3},{6,0},{7,5},{8,10},{9,15},{10,... | collective-permute-start | bytes 786440 | tf_op jit(solution)/shard_map/ppermute | solution.py:48
  77.8 9.2 %collective-permute-start.30 = (bf16[128,1024]{1,0:T(8,128)(2,1)S(1)}, bf16[128,1024]{1,0:T(8,128)(2,1)S(1)}, u32[]{:S(2)}, u32[]{:S(2)}) collective-permute-start(bf16[128,1024]{1,0:T(8,128)(2,1)S(1)} %get-tuple-element.13), channel_id=1, source_target_pairs={{0,2},{1,7},{2,4},{3,1},{4,6},{5,3},{6,0},{7,5},{8,10},{9,15},{10,... | collective-permute-start | bytes 786440 | tf_op jit(solution)/shard_map/ppermute | solution.py:48
  77.9 9.5 %collective-permute-start.29 = (bf16[128,1024]{1,0:T(8,128)(2,1)S(1)}, bf16[128,1024]{1,0:T(8,128)(2,1)S(1)}, u32[]{:S(2)}, u32[]{:S(2)}) collective-permute-start(bf16[128,1024]{1,0:T(8,128)(2,1)S(1)} %get-tuple-element.12), channel_id=1, source_target_pairs={{0,6},{1,3},{2,0},{3,5},{4,2},{5,7},{6,4},{7,1},{8,14},{9,11},{10,... | collective-permute-start | bytes 786440 | tf_op jit(solution)/shard_map/ppermute | solution.py:48
  (5 other events, 39.9 us)
where the time goes:
time: 98.3 us; the launch traced here: 98 us
  starting transfers between devices  45.8 us (47%)
  waiting for transfers between devices  24 us (24%)
  Pallas kernels  12.3 us (13%)
  blocking collectives  9.13 us (9%)
  local copies, waits for them, and re-layouts  3.5 us (4%)
  other arithmetic  2.45 us (2%)
    ppermute x13, starting transfers between devices, other_core(): lax.ppermute(array, AXES, permutation(lambda z, x, y, c: (z, x, y, c + 1)))  18.4 us
    ppermute x8, starting transfers between devices, along_x(): lax.ppermute(array, AXES, permutation(lambda z, x, y, c: (z, x + hops * (...  10.8 us
    ppermute x4, starting transfers between devices, along_z(): lax.ppermute(array, AXES, permutation(lambda z, x, y, c: (z + hops * (1 -...  10.3 us
    ppermute x6, waiting for transfers between devices, along_y(): lax.ppermute(array, AXES, permutation(lambda z, x, y, c: (z, x, y + hops...  9.29 us
    all_to_all x1, blocking collectives, layer(): lax.all_to_all(copies, ('y', 'c'), 0, 0, tiled=True)  9.13 us
    ppermute x8, waiting for transfers between devices, along_x(): lax.ppermute(array, AXES, permutation(lambda z, x, y, c: (z, x + hops * (...  7.9 us
    ppermute x6, starting transfers between devices, along_y(): lax.ppermute(array, AXES, permutation(lambda z, x, y, c: (z, x, y + hops...  6.31 us
    pallas_call x1, Pallas kernels, attend(): pl.pallas_call(kernel, out_shape=jax.ShapeDtypeStruct((2 * TILE, GROUP *...  6.04 us
  transfers between devices with their start and end apart: 31, of which 13 were waited for; matrix products, arithmetic and copies ran while one was open for 1% of the time, Pallas kernels for 12%

commit v1 on v0

--- a/solution.py
+++ b/solution.py
@@ -54,24 +54,52 @@
     return lax.ppermute(array, AXES, permutation(lambda z, x, y, c: (z, x, y, c + 1)))
 
 
-def gather_pairs(own, c):
-    def half(block):
-        return lax.dynamic_slice_in_dim(block, c * 256, 256, 0)
-
+def gather_pairs(own, own_half):
     near1 = along_z(own, 1)
     near2 = along_z(own, 2)
-    near3 = along_z(own, 3)
-    half4 = along_z(half(own), 4)
-    group1 = jnp.concatenate([half(own), near1, near2], axis=0)
+    near3 = along_z(near1, 2)
+    half4 = along_z(lax.dynamic_slice_in_dim(near2, lax.axis_index("c") * 256, 256, 0), 2)
+    group1 = jnp.concatenate([own_half, near1, near2], axis=0)
     ahead1 = along_x(group1, 1)
     back1 = along_x(group1, -1)
     group2 = jnp.concatenate([near3, half4], axis=0)
     ahead2 = along_x(group2, 1)
     back2 = along_x(group2, -1)
-    far1, far1_low = along_x(ahead1[:640], 1), along_x(back1[640:], -1)
-    far2, far2_low = along_x(ahead2[:384], 1), along_x(back2[384:], -1)
+    far1 = along_x(ahead1[:640], 1)
+    far1_low = along_x(back1[640:], -1)
+    far2 = along_x(ahead2[:384], 1)
+    far2_low = along_x(back2[384:], -1)
     arrays = [near1, near2, group2, ahead1, back1, ahead2, back2, far1, far1_low, far2, far2_low]
-    return arrays, [other_core(array) for array in arrays]
+    theirs = []
+    for array in arrays:
+        theirs.append(other_core(array))
+    return arrays, theirs
+
+
+def pick(keys_values):
+    def kernel(all_ref, block_ref, half_ref, sems):
+        y, c = lax.axis_index("y"), lax.axis_index("c")
+        head = all_ref.at[:, :, pl.ds(pl.multiple_of(y * HEAD, HEAD), HEAD)]
+        copies = [
+            pltpu.make_async_copy(head, block_ref, sems.at[0]),
+            pltpu.make_async_copy(head.at[c], half_ref, sems.at[1]),
+        ]
+        for copy in copies:
+            copy.start()
+        for copy in copies:
+            copy.wait()
+
+    return pl.pallas_call(
+        kernel,
+        out_shape=[
+            pltpu.VMEM((2, 256, HEAD), jnp.bfloat16),
+            pltpu.VMEM((256, HEAD), jnp.bfloat16),
+        ],
+        in_specs=[pl.BlockSpec(memory_space=pltpu.HBM)],
+        out_specs=[pl.BlockSpec(memory_space=pltpu.VMEM)] * 2,
+        scratch_shapes=[pltpu.SemaphoreType.DMA((2,))],
+        name="pick",
+    )(pltpu.with_memory_space_constraint(keys_values, pltpu.HBM))
 
 
 def spot(refs, steps, hops, row):
@@ -88,16 +116,18 @@
     return held, row
 
 
-def attend(query, own, mine, theirs, ancestors, tile_of_slot):
+def attend(query, own, mine, theirs, ancestors, tile_of_slot, weight, weight_other):
     scale = HEAD**-0.5 * LOG2E
     keys_total = (ANC + 1) * TILE
     count = len(mine)
 
-    def kernel(ancestors_hbm, tile_of_slot_hbm, query_hbm, own_ref, *rest):
+    def kernel(ancestors_hbm, tile_of_slot_hbm, query_hbm, *rest):
+        weight_refs, own_ref, rest = rest[:2], rest[2], rest[3:]
         mine_refs, theirs_refs = rest[:count], rest[count : 2 * count]
-        out_ref, keys, values, scores, weights, bias, query_ref = rest[2 * count : 2 * count + 7]
-        ancestors_ref, tile_of_slot_ref, slot_of, wanted, sems = rest[2 * count + 7 :]
-        z, x, c = (lax.axis_index(name) for name in ("z", "x", "c"))
+        out_ref, *loaded_refs = rest[2 * count : 2 * count + 3]
+        keys, values, scores, weights, bias, query_ref = rest[2 * count + 3 : 2 * count + 9]
+        ancestors_ref, tile_of_slot_ref, slot_of, wanted, sems = rest[2 * count + 9 :]
+        z, x, y, c = (lax.axis_index(name) for name in AXES)
         sign = 1 - 2 * c
         copies = [
             pltpu.make_async_copy(ancestors_hbm, ancestors_ref, sems.at[0]),
@@ -105,6 +135,17 @@
             pltpu.make_async_copy(query_hbm, query_ref, sems.at[2]),
         ]
         for copy in copies:
+            copy.start()
+        loads = []
+        for hops in (2, 1, 3, 0):
+            column = pl.multiple_of((lax.rem(y + hops * sign + NY, NY) * 2 + c) * 1024, 1024)
+            for source, target in zip(weight_refs, loaded_refs):
+                loads.append(
+                    pltpu.make_async_copy(
+                        source.at[:, pl.ds(column, 1024)], target.at[hops], sems.at[3]
+                    )
+                )
+        for copy in loads:
             copy.start()
         for copy in copies[:2]:
             copy.wait()
@@ -178,16 +219,18 @@
                     put_from(keys, theirs_refs, NZ - n, h_other, 0)
                     put_from(values, theirs_refs, NZ - n, h_other, 256)
 
-            for h in range(NX):
-
-                @pl.when(hops == h)
-                def _(h=h):
-                    for n in range(NZ):
-
-                        @pl.when(steps == n)
-                        def _(n=n):
-                            from_chip(n, h)
-
+            def branch(case, low, high):
+                if high - low == 1:
+                    from_chip(low % NZ, low // NZ)
+                    return
+                middle = (low + high) // 2
+                lax.cond(
+                    case < middle,
+                    lambda: branch(case, low, middle),
+                    lambda: branch(case, middle, high),
+                )
+
+            branch(hops * NZ + steps, 0, NX * NZ)
             return carry
 
         lax.fori_loop(0, 2 * ANC, take, 0)
@@ -234,13 +277,19 @@
                 out_ref[t * TILE : (t + 1) * TILE, h * HEAD : (h + 1) * HEAD] = (
                     mixed[h * TILE : (h + 1) * TILE] / totals[h]
                 ).astype(jnp.bfloat16)
+        for copy in loads:
+            copy.wait()
 
     return pl.pallas_call(
         kernel,
-        out_shape=jax.ShapeDtypeStruct((2 * TILE, GROUP * HEAD), jnp.bfloat16),
-        in_specs=[pl.BlockSpec(memory_space=pltpu.HBM)] * 3
+        out_shape=[
+            pltpu.VMEM((2 * TILE, GROUP * HEAD), jnp.bfloat16),
+            pltpu.VMEM((NY, 512, 1024), jnp.bfloat16),
+            pltpu.VMEM((NY, 512, 1024), jnp.bfloat16),
+        ],
+        in_specs=[pl.BlockSpec(memory_space=pltpu.HBM)] * 5
         + [pl.BlockSpec(memory_space=pltpu.VMEM)] * (1 + 2 * count),
-        out_specs=pl.BlockSpec(memory_space=pltpu.VMEM),
+        out_specs=[pl.BlockSpec(memory_space=pltpu.VMEM)] * 3,
         scratch_shapes=[
             pltpu.VMEM((2 * keys_total, HEAD), jnp.bfloat16),
             pltpu.VMEM((2 * keys_total, HEAD), jnp.bfloat16),
@@ -252,55 +301,26 @@
             pltpu.SMEM((TILES,), jnp.int32),
             pltpu.SMEM((TILES,), jnp.int32),
             pltpu.SMEM((2 * ANC,), jnp.int32),
-            pltpu.SemaphoreType.DMA((3,)),
+            pltpu.SemaphoreType.DMA((4,)),
         ],
         compiler_params=pltpu.CompilerParams(vmem_limit_bytes=28 << 20),
         name="attend",
     )(
-        *(pltpu.with_memory_space_constraint(a, pltpu.HBM) for a in (ancestors, tile_of_slot, query)),
+        *(
+            pltpu.with_memory_space_constraint(array, pltpu.HBM)
+            for array in (ancestors, tile_of_slot, query, weight, weight_other)
+        ),
         own,
         *mine,
         *theirs,
     )
 
 
-def fetch(weight, weight_other):
-    def kernel(weight_ref, other_ref, out_ref, sem):
-        y, c = lax.axis_index("y"), lax.axis_index("c")
-        sign = 1 - 2 * c
-        copies = []
-        for hops in range(NY):
-            column = pl.multiple_of((lax.rem(y + hops * sign + NY, NY) * 2 + c) * 1024, 1024)
-            for ref, row in ((weight_ref, 0), (other_ref, 512)):
-                copies.append(
-                    pltpu.make_async_copy(
-                        ref.at[:, pl.ds(column, 1024)], out_ref.at[hops, pl.ds(row, 512)], sem
-                    )
-                )
-        for copy in copies:
-            copy.start()
-        for copy in copies:
-            copy.wait()
-
-    return pl.pallas_call(
-        kernel,
-        out_shape=pltpu.VMEM((NY, 1024, 1024), jnp.bfloat16),
-        in_specs=[pl.BlockSpec(memory_space=pltpu.HBM)] * 2,
-        out_specs=pl.BlockSpec(memory_space=pltpu.VMEM),
-        scratch_shapes=[pltpu.SemaphoreType.DMA],
-        compiler_params=pltpu.CompilerParams(vmem_limit_bytes=12 << 20),
-        name="fetch",
-    )(
-        pltpu.with_memory_space_constraint(weight, pltpu.HBM),
-        pltpu.with_memory_space_constraint(weight_other, pltpu.HBM),
-    )
-
-
-def project(attended, attended_other, weights, parts, added=(), dtype=jnp.bfloat16):
+def project(attended, attended_other, weights, weights_other, parts, added=(), dtype=jnp.bfloat16):
     count = len(parts)
     sizes = [2 * TILE if tile is None else TILE for _, tile in parts]
 
-    def kernel(a_ref, b_ref, w_ref, *rest):
+    def kernel(a_ref, b_ref, w_ref, v_ref, *rest):
         added_refs, out_refs = rest[: len(added)], rest[len(added) :]
         c = lax.axis_index("c")
         for k, ((hops, tile), rows) in enumerate(zip(parts, sizes)):
@@ -308,12 +328,12 @@
             for n in range(0, 1024, 256):
                 term = jnp.dot(
                     a_ref[pl.ds(row, rows)],
-                    w_ref[hops, 0:512, n : n + 256],
+                    w_ref[hops, :, n : n + 256],
                     preferred_element_type=jnp.float32,
                 )
                 term += jnp.dot(
                     b_ref[pl.ds(row, rows)],
-                    w_ref[hops, 512:1024, n : n + 256],
+                    v_ref[hops, :, n : n + 256],
                     preferred_element_type=jnp.float32,
                 )
                 if added:
@@ -323,21 +343,102 @@
     return pl.pallas_call(
         kernel,
         out_shape=[jax.ShapeDtypeStruct((rows, 1024), dtype) for rows in sizes],
-        in_specs=[pl.BlockSpec(memory_space=pltpu.VMEM)] * (3 + len(added)),
+        in_specs=[pl.BlockSpec(memory_space=pltpu.VMEM)] * (4 + len(added)),
         out_specs=[pl.BlockSpec(memory_space=pltpu.VMEM)] * count,
         compiler_params=pltpu.CompilerParams(vmem_limit_bytes=16 << 20),
         name="project",
-    )(attended, attended_other, weights, *added)
+    )(attended, attended_other, weights, weights_other, *added)
+
+
+def finish(here, from_back0, from_ahead0, from_ahead1, from_back1, residual):
+    def kernel(here_ref, b0_ref, a0_ref, a1_ref, b1_ref, residual_ref, hidden_ref, sums_ref):
+        c = lax.axis_index("c")
+        ones = jnp.ones((8, 128), jnp.float32)
+        for tile, first_ref, second_ref in ((c, b0_ref, a0_ref), (1 - c, a1_ref, b1_ref)):
+            row = pl.multiple_of(tile * TILE, TILE)
+            squares = jnp.zeros((TILE, 128), jnp.float32)
+            for n in range(0, 1024, 128):
+                columns = slice(n, n + 128)
+                share = first_ref[:, columns].astype(jnp.float32)
+                share += second_ref[:, columns].astype(jnp.float32)
+                share += here_ref[pl.ds(row, TILE), columns]
+                share += residual_ref[pl.ds(row, TILE), columns].astype(jnp.float32)
+                hidden = share.astype(jnp.bfloat16)
+                hidden_ref[pl.ds(row, TILE), columns] = hidden
+                hidden = hidden.astype(jnp.float32)
+                squares += hidden * hidden
+            sums = lax.dot_general(
+                ones,
+                squares,
+                (((1,), (1,)), ((), ())),
+                precision=lax.Precision.HIGHEST,
+                preferred_element_type=jnp.float32,
+            )
+            for k in range(NY * NC):
+                sums_ref[k, :, pl.ds(row, TILE)] = sums[0:1]
+
+    return pl.pallas_call(
+        kernel,
+        out_shape=[
+            pltpu.VMEM((2 * TILE, 1024), jnp.bfloat16),
+            pltpu.VMEM((NY * NC, 1, 2 * TILE), jnp.float32),
+        ],
+        in_specs=[pl.BlockSpec(memory_space=pltpu.VMEM)] * 6,
+        out_specs=[pl.BlockSpec(memory_space=pltpu.VMEM)] * 2,
+        compiler_params=pltpu.CompilerParams(vmem_limit_bytes=8 << 20),
+        name="finish",
+    )(here, from_back0, from_ahead0, from_ahead1, from_back1, residual)
+
+
+def normalize(hidden, sums, gain):
+    def kernel(hidden_ref, sums_ref, gain_ref, hidden_hbm, normed_hbm, normed_ref, sems):
+        out = pltpu.make_async_copy(hidden_ref, hidden_hbm, sems.at[0])
+        out.start()
+        copies = []
+        for tile in range(2):
+            rows = slice(tile * TILE, (tile + 1) * TILE)
+            total = sums_ref[0, :, rows]
+            for k in range(1, NY * NC):
+                total += sums_ref[k, :, rows]
+            scale = lax.rsqrt(jnp.broadcast_to(total, (TILE, TILE)) / D + 1e-05)
+            scale = jnp.transpose(scale)
+            for n in range(0, 1024, 128):
+                columns = slice(n, n + 128)
+                normed_ref[rows, columns] = (
+                    hidden_ref[rows, columns].astype(jnp.float32) * scale * gain_ref[:, columns]
+                ).astype(jnp.bfloat16)
+            copies.append(
+                pltpu.make_async_copy(normed_ref.at[rows], normed_hbm.at[rows], sems.at[1 + tile])
+            )
+            copies[-1].start()
+        out.wait()
+        for copy in copies:
+            copy.wait()
+
+    shape = jax.ShapeDtypeStruct((2 * TILE, 1024), jnp.bfloat16)
+    return pl.pallas_call(
+        kernel,
+        out_shape=[shape, shape],
+        in_specs=[pl.BlockSpec(memory_space=pltpu.VMEM)] * 3,
+        out_specs=[pl.BlockSpec(memory_space=pltpu.HBM)] * 2,
+        scratch_shapes=[
+            pltpu.VMEM((2 * TILE, 1024), jnp.bfloat16),
+            pltpu.SemaphoreType.DMA((3,)),
+        ],
+        compiler_params=pltpu.CompilerParams(vmem_limit_bytes=8 << 20),
+        name="normalize",
+    )(hidden, sums, gain.reshape(1, 1024))
 
 
 def layer(query, keys_values, ancestors, tile_of_slot, residual, norm_gain, out_weight):
-    y, c = lax.axis_index("y"), lax.axis_index("c")
-    own = lax.dynamic_slice_in_dim(keys_values, y * HEAD, HEAD, 2).reshape(BLOCK, HEAD)
+    own, own_half = pick(keys_values)
+    own = own.reshape(BLOCK, HEAD)
     weight_other = other_core(out_weight)
-    weights = fetch(out_weight, weight_other)
-    mine, theirs = gather_pairs(own, c)
-    attended = attend(query, own, mine, theirs, ancestors, tile_of_slot)
-    args = (attended, other_core(attended), weights)
+    mine, theirs = gather_pairs(own, own_half)
+    attended, *weights = attend(
+        query, own, mine, theirs, ancestors, tile_of_slot, out_weight, weight_other
+    )
+    args = (attended, other_core(attended), *weights)
     across0, across1 = project(*args, [(2, 0), (2, 1)])
     relay_ahead = along_y(across0, 1)
     relay_back = along_y(across1, -1)
@@ -348,20 +449,9 @@
     from_back0 = along_y(joined0, 1)
     from_ahead1 = along_y(joined1, -1)
     (here,) = project(*args, [(0, None)], (), jnp.float32)
-    share0 = from_back0.astype(jnp.float32) + from_ahead0.astype(jnp.float32)
-    share1 = from_ahead1.astype(jnp.float32) + from_back1.astype(jnp.float32)
-    total = here + jnp.where(
-        c == 0,
-        jnp.concatenate([share0, share1], axis=0),
-        jnp.concatenate([share1, share0], axis=0),
-    )
-    hidden_out = (residual.astype(jnp.float32) + total).astype(jnp.bfloat16)
-    hidden_f32 = hidden_out.astype(jnp.float32)
-    squares = jnp.sum(hidden_f32 * hidden_f32, axis=1)
-    copies = jnp.broadcast_to(squares[None, None], (NY * NC, 1, squares.shape[0]))
-    mean_sq = jnp.sum(lax.all_to_all(copies, ("y", "c"), 0, 0, tiled=True), axis=(0, 1)) / D
-    normed = hidden_f32 * lax.rsqrt(mean_sq + 1e-05)[:, None] * norm_gain[None, :]
-    return (hidden_out, normed.astype(jnp.bfloat16))
+    hidden, sums = finish(here, from_back0, from_ahead0, from_ahead1, from_back1, residual)
+    sums = lax.all_to_all(sums, ("y", "c"), 0, 0, tiled=True)
+    return tuple(normalize(hidden, sums, norm_gain))
 
 
 def solution(mesh):

time: 98.3 us -> 87.8 us (0.89)
  local copies, waits for them, and re-layouts: 3.5 us -> 0.12 us
  starting transfers between devices: 45.8 us -> 43.2 us
  other arithmetic: 2.45 us -> 0 us
  Pallas kernels: 12.3 us -> 11 us
    ppermute x8, waiting for transfers between devices: 7.9 us -> 3.78 us  [along_x(): lax.ppermute(array, AXES, permutation(lambda z, x, y, c: (z, x + hops * (...]
    unnamed x13 -> x7, local copies, waits for them, and re-layouts: 3.42 us -> 0.05 us
    ppermute x6, waiting for transfers between devices: 9.29 us -> 11.4 us  [along_y(): lax.ppermute(array, AXES, permutation(lambda z, x, y, c: (z, x, y + hops...]
    ppermute x13, waiting for transfers between devices: 2.86 us -> 4.78 us  [other_core(): lax.ppermute(array, AXES, permutation(lambda z, x, y, c: (z, x, y, c + 1)))]
    ppermute x8, starting transfers between devices: 10.8 us -> 8.85 us  [along_x(): lax.ppermute(array, AXES, permutation(lambda z, x, y, c: (z, x + hops * (...]
    ppermute x6, starting transfers between devices: 6.31 us -> 7.61 us  [along_y(): lax.ppermute(array, AXES, permutation(lambda z, x, y, c: (z, x, y + hops...]
    pallas_call x2 -> x4, Pallas kernels: 9.48 us -> 8.18 us  [the longest x1 5.63 us: attend(): pl.pallas_call(kernel, out_shape=[pltpu.VMEM((2 * TILE, GROUP * HEAD), jn...]
    add x2 -> x0, other arithmetic: 1.07 us -> none  [the longest x1 1.01 us: layer(): share0 = from_back0.astype(jnp.float32) + from_ahead0.astype(jnp.float32)]
  transfers between devices with their start and end apart: 31 -> 31, of which waited for: 13 -> 15; matrix products, arithmetic and copies ran while one was open for 1% -> 0% of each run, Pallas kernels for 12% -> 4%
where the time goes in v1:
time: 87.8 us; the launch traced here: 87.6 us
  starting transfers between devices  43.2 us (49%)
  waiting for transfers between devices  23.4 us (27%)
  Pallas kernels  11 us (13%)
  blocking collectives  8.8 us (10%)
  between operations  0.98 us (1%)
    ppermute x13, starting transfers between devices, other_core(): lax.ppermute(array, AXES, permutation(lambda z, x, y, c: (z, x, y, c + 1)))  17.4 us
    ppermute x6, waiting for transfers between devices, along_y(): lax.ppermute(array, AXES, permutation(lambda z, x, y, c: (z, x, y + hops...  11.4 us
    ppermute x4, starting transfers between devices, along_z(): lax.ppermute(array, AXES, permutation(lambda z, x, y, c: (z + hops * (1 -...  9.39 us
    ppermute x8, starting transfers between devices, along_x(): lax.ppermute(array, AXES, permutation(lambda z, x, y, c: (z, x + hops * (...  8.85 us
    all_to_all x1, blocking collectives, layer(): sums = lax.all_to_all(sums, ('y', 'c'), 0, 0, tiled=True)  8.8 us
    ppermute x6, starting transfers between devices, along_y(): lax.ppermute(array, AXES, permutation(lambda z, x, y, c: (z, x, y + hops...  7.61 us
    pallas_call x1, Pallas kernels, attend(): pl.pallas_call(kernel, out_shape=[pltpu.VMEM((2 * TILE, GROUP * HEAD), jn...  5.63 us
    ppermute x13, waiting for transfers between devices, other_core(): lax.ppermute(array, AXES, permutation(lambda z, x, y, c: (z, x, y, c + 1)))  4.78 us
  transfers between devices with their start and end apart: 31, of which 15 were waited for; matrix products, arithmetic and copies ran while one was open for 0% of the time, Pallas kernels for 4%

profile of v1, /device:TPU:1, one launch (start us, length us, event | category | flops | bytes accessed | tf_op | source)
XLA Modules:
  0.0 87.6 jit_solution(18186106441772422787)
XLA Ops:
  0.6 3.3 %collective-permute-start = (bf16[512,8192]{1,0:T(8,128)(2,1)}, bf16[512,8192]{1,0:T(8,128)(2,1)}, u32[]{:S(2)}, u32[]{:S(2)}) collective-permute-start(bf16[512,8192]{1,0:T(8,128)(2,1)} %rest_0_.1), channel_id=1, source_target_pairs={{0,1},{1,0},{2,3},{3,2},{4,5},{5,4},{6,7},{7,6},{8,9},{9,8},{10,11... | collective-permute-start | bytes 25165832 | tf_op jit(solution)/shard_map/ppermute | solution.py:54
  3.9 0.9 %pick.1 = (bf16[2,256,128]{2,1,0:T(8,128)(2,1)S(1)}, bf16[256,128]{1,0:T(8,128)(2,1)S(1)}) custom-call(bf16[2,256,512]{2,1,0:T(8,128)(2,1)} %all_ref.1), custom_call_target="tpu_custom_call" | custom-call | tf_op jit(solution)/shard_map/pick/pallas_call | solution.py:92
  4.9 4.4 %collective-permute-start.2 = (bf16[512,128]{1,0:T(8,128)(2,1)S(1)}, bf16[512,128]{1,0:T(8,128)(2,1)S(1)}, u32[]{:S(2)}, u32[]{:S(2)}) collective-permute-start(bf16[512,128]{1,0:T(8,128)(2,1)S(1)} %bitcast.2), channel_id=1, source_target_pairs={{0,64},{1,193},{2,66},{3,195},{4,68},{5,197},{6,70},{7,199},{8,72}... | collective-permute-start | bytes 393224 | tf_op jit(solution)/shard_map/ppermute | solution.py:36
  10.0 2.6 %collective-permute-done.2.rest_4_ = bf16[512,128]{1,0:T(8,128)(2,1)S(1)} collective-permute-done((bf16[512,128]{1,0:T(8,128)(2,1)S(1)}, bf16[512,128]{1,0:T(8,128)(2,1)S(1)}, u32[]{:S(2)}, u32[]{:S(2)}) %collective-permute-start.2) | collective-permute-done | bytes 131104 | tf_op jit(solution)/shard_map/ppermute | solution.py:36
  12.6 4.0 %collective-permute-start.4 = (bf16[256,128]{1,0:T(8,128)(2,1)S(1)}, bf16[256,128]{1,0:T(8,128)(2,1)S(1)}, u32[]{:S(2)}, u32[]{:S(2)}) collective-permute-start(bf16[256,128]{1,0:T(8,128)(2,1)S(1)} %constant_dynamic-slice_fusion), channel_id=1, source_target_pairs={{0,64},{1,193},{2,66},{3,195},{4,68},{5,197},{6,70},{7,199},{8,72}... | collective-permute-start | bytes 196616 | tf_op jit(solution)/shard_map/ppermute | solution.py:36
  16.9 1.3 %collective-permute-start.6 = (bf16[1280,128]{1,0:T(8,128)(2,1)S(1)}, bf16[1280,128]{1,0:T(8,128)(2,1)S(1)}, u32[]{:S(2)}, u32[]{:S(2)}) collective-permute-start(bf16[1280,128]{1,0:T(8,128)(2,1)S(1)} %constant_dynamic-update-slice_fusion.2), channel_id=1, source_target_pairs={{0,24},{1,9},{2,26},{3,11},{4,28},{5,13},{6,30},{7,15},{8,0},{9,17... | collective-permute-start | bytes 983048 | tf_op jit(solution)/shard_map/ppermute | solution.py:42
  18.2 3.6 %collective-permute-start.14 = (bf16[512,128]{1,0:T(8,128)(2,1)S(1)}, bf16[512,128]{1,0:T(8,128)(2,1)S(1)}, u32[]{:S(2)}, u32[]{:S(2)}) collective-permute-start(bf16[512,128]{1,0:T(8,128)(2,1)S(1)} %collective-permute-done.2.rest_4_), channel_id=1, source_target_pairs={{0,1},{1,0},{2,3},{3,2},{4,5},{5,4},{6,7},{7,6},{8,9},{9,8},{10,11... | collective-permute-start | bytes 393224 | tf_op jit(solution)/shard_map/ppermute | solution.py:54
  21.8 0.9 collective-permute-done.3
  22.7 1.3 %collective-permute-start.8 = (bf16[768,128]{1,0:T(8,128)(2,1)S(1)}, bf16[768,128]{1,0:T(8,128)(2,1)S(1)}, u32[]{:S(2)}, u32[]{:S(2)}) collective-permute-start(bf16[768,128]{1,0:T(8,128)(2,1)S(1)} %constant_dynamic-update-slice_fusion.rest_5_), channel_id=1, source_target_pairs={{0,24},{1,9},{2,26},{3,11},{4,28},{5,13},{6,30},{7,15},{8,0},{9,17... | collective-permute-start | bytes 589832 | tf_op jit(solution)/shard_map/ppermute | solution.py:42
  24.0 1.5 %collective-permute-start.7 = (bf16[768,128]{1,0:T(8,128)(2,1)S(1)}, bf16[768,128]{1,0:T(8,128)(2,1)S(1)}, u32[]{:S(2)}, u32[]{:S(2)}) collective-permute-start(bf16[768,128]{1,0:T(8,128)(2,1)S(1)} %constant_dynamic-update-slice_fusion.rest_5_), channel_id=1, source_target_pairs={{0,8},{1,25},{2,10},{3,27},{4,12},{5,29},{6,14},{7,31},{8,16},{9,1... | collective-permute-start | bytes 589832 | tf_op jit(solution)/shard_map/ppermute | solution.py:42
  25.4 1.3 %collective-permute-start.5 = (bf16[1280,128]{1,0:T(8,128)(2,1)S(1)}, bf16[1280,128]{1,0:T(8,128)(2,1)S(1)}, u32[]{:S(2)}, u32[]{:S(2)}) collective-permute-start(bf16[1280,128]{1,0:T(8,128)(2,1)S(1)} %constant_dynamic-update-slice_fusion.2), channel_id=1, source_target_pairs={{0,8},{1,25},{2,10},{3,27},{4,12},{5,29},{6,14},{7,31},{8,16},{9,1... | collective-permute-start | bytes 983048 | tf_op jit(solution)/shard_map/ppermute | solution.py:42
  26.7 1.8 %collective-permute-done.8.rest_9_ = bf16[768,128]{1,0:T(8,128)(2,1)S(1)} collective-permute-done((bf16[768,128]{1,0:T(8,128)(2,1)S(1)}, bf16[768,128]{1,0:T(8,128)(2,1)S(1)}, u32[]{:S(2)}, u32[]{:S(2)}) %collective-permute-start.8) | collective-permute-done | bytes 196640 | tf_op jit(solution)/shard_map/ppermute | solution.py:42
  28.5 2.6 %collective-permute-start.15 = (bf16[768,128]{1,0:T(8,128)(2,1)S(1)}, bf16[768,128]{1,0:T(8,128)(2,1)S(1)}, u32[]{:S(2)}, u32[]{:S(2)}) collective-permute-start(bf16[768,128]{1,0:T(8,128)(2,1)S(1)} %constant_dynamic-update-slice_fusion.rest_5_), channel_id=1, source_target_pairs={{0,1},{1,0},{2,3},{3,2},{4,5},{5,4},{6,7},{7,6},{8,9},{9,8},{10,11... | collective-permute-start | bytes 589832 | tf_op jit(solution)/shard_map/ppermute | solution.py:54
  31.1 1.6 %collective-permute-start.13 = (bf16[512,128]{1,0:T(8,128)(2,1)S(1)}, bf16[512,128]{1,0:T(8,128)(2,1)S(1)}, u32[]{:S(2)}, u32[]{:S(2)}) collective-permute-start(bf16[512,128]{1,0:T(8,128)(2,1)S(1)} %collective-permute-done.1.rest_3_), channel_id=1, source_target_pairs={{0,1},{1,0},{2,3},{3,2},{4,5},{5,4},{6,7},{7,6},{8,9},{9,8},{10,11... | collective-permute-start | bytes 393224 | tf_op jit(solution)/shard_map/ppermute | solution.py:54
  33.9 2.9 %collective-permute-start.11 = (bf16[384,128]{1,0:T(8,128)(2,1)S(1)}, bf16[384,128]{1,0:T(8,128)(2,1)S(1)}, u32[]{:S(2)}, u32[]{:S(2)}) collective-permute-start(bf16[384,128]{1,0:T(8,128)(2,1)S(1)} %slice.18), channel_id=1, source_target_pairs={{0,8},{1,25},{2,10},{3,27},{4,12},{5,29},{6,14},{7,31},{8,16},{9,1... | collective-permute-start | bytes 294920 | tf_op jit(solution)/shard_map/ppermute | solution.py:42
  37.7 1.7 %collective-permute-done.11.rest_12_ = bf16[384,128]{1,0:T(8,128)(2,1)S(1)} collective-permute-done((bf16[384,128]{1,0:T(8,128)(2,1)S(1)}, bf16[384,128]{1,0:T(8,128)(2,1)S(1)}, u32[]{:S(2)}, u32[]{:S(2)}) %collective-permute-start.11) | collective-permute-done | bytes 98336 | tf_op jit(solution)/shard_map/ppermute | solution.py:42
  39.4 2.8 %collective-permute-start.23 = (bf16[384,128]{1,0:T(8,128)(2,1)S(1)}, bf16[384,128]{1,0:T(8,128)(2,1)S(1)}, u32[]{:S(2)}, u32[]{:S(2)}) collective-permute-start(bf16[384,128]{1,0:T(8,128)(2,1)S(1)} %collective-permute-done.12.rest_13_), channel_id=1, source_target_pairs={{0,1},{1,0},{2,3},{3,2},{4,5},{5,4},{6,7},{7,6},{8,9},{9,8},{10,11... | collective-permute-start | bytes 294920 | tf_op jit(solution)/shard_map/ppermute | solution.py:54
  42.2 1.9 %collective-permute-start.17 = (bf16[1280,128]{1,0:T(8,128)(2,1)S(1)}, bf16[1280,128]{1,0:T(8,128)(2,1)S(1)}, u32[]{:S(2)}, u32[]{:S(2)}) collective-permute-start(bf16[1280,128]{1,0:T(8,128)(2,1)S(1)} %collective-permute-done.6.rest_7_), channel_id=1, source_target_pairs={{0,1},{1,0},{2,3},{3,2},{4,5},{5,4},{6,7},{7,6},{8,9},{9,8},{10,11... | collective-permute-start | bytes 983048 | tf_op jit(solution)/shard_map/ppermute | solution.py:54
  44.7 1.3 %collective-permute-done.22.rest_23_ = bf16[384,128]{1,0:T(8,128)(2,1)S(1)} collective-permute-done((bf16[384,128]{1,0:T(8,128)(2,1)S(1)}, bf16[384,128]{1,0:T(8,128)(2,1)S(1)}, u32[]{:S(2)}, u32[]{:S(2)}) %collective-permute-start.22) | collective-permute-done | bytes 98336 | tf_op jit(solution)/shard_map/ppermute | solution.py:54
  46.5 0.9 %collective-permute-done.21.rest_22_ = bf16[640,128]{1,0:T(8,128)(2,1)S(1)} collective-permute-done((bf16[640,128]{1,0:T(8,128)(2,1)S(1)}, bf16[640,128]{1,0:T(8,128)(2,1)S(1)}, u32[]{:S(2)}, u32[]{:S(2)}) %collective-permute-start.21) | collective-permute-done | bytes 163872 | tf_op jit(solution)/shard_map/ppermute | solution.py:54
  47.8 5.6 %attend.1 = (bf16[256,512]{1,0:T(8,128)(2,1)S(1)}, bf16[4,512,1024]{2,1,0:T(8,128)(2,1)S(1)}, bf16[4,512,1024]{2,1,0:T(8,128)(2,1)S(1)}) custom-call(s32[2,12]{1,0:T(2,128)} %ancestors_hbm.1, s32[64]{0:T(128)} %tile_of_slot_hbm.1, bf16[256,512]{1,0:T(8,128)(2,1)} %query_hbm.1, bf16[512,8192]{1,0:T(8,128)(2,1)} %rest_0_.1, ...), custom_call_target="tpu_custom_call" | custom-call | tf_op jit(solution)/shard_map/attend/pallas_call | solution.py:283
  53.8 1.3 %collective-permute-done.24.b_ref = bf16[256,512]{1,0:T(8,128)(2,1)S(1)} collective-permute-done((bf16[256,512]{1,0:T(8,128)(2,1)S(1)}, bf16[256,512]{1,0:T(8,128)(2,1)S(1)}, u32[]{:S(2)}, u32[]{:S(2)}) %collective-permute-start.24) | collective-permute-done | bytes 262176 | tf_op jit(solution)/shard_map/ppermute | solution.py:54
  55.8 2.9 %collective-permute-start.25 = (bf16[128,1024]{1,0:T(8,128)(2,1)S(1)}, bf16[128,1024]{1,0:T(8,128)(2,1)S(1)}, u32[]{:S(2)}, u32[]{:S(2)}) collective-permute-start(bf16[128,1024]{1,0:T(8,128)(2,1)S(1)} %get-tuple-element.20), channel_id=1, source_target_pairs={{0,2},{1,7},{2,4},{3,1},{4,6},{5,3},{6,0},{7,5},{8,10},{9,15},{10,... | collective-permute-start | bytes 786440 | tf_op jit(solution)/shard_map/ppermute | solution.py:48
  59.5 3.0 %collective-permute-start.30 = (bf16[128,1024]{1,0:T(8,128)(2,1)S(1)}, bf16[128,1024]{1,0:T(8,128)(2,1)S(1)}, u32[]{:S(2)}, u32[]{:S(2)}) collective-permute-start(bf16[128,1024]{1,0:T(8,128)(2,1)S(1)} %get-tuple-element.25), channel_id=1, source_target_pairs={{0,2},{1,7},{2,4},{3,1},{4,6},{5,3},{6,0},{7,5},{8,10},{9,15},{10,... | collective-permute-start | bytes 786440 | tf_op jit(solution)/shard_map/ppermute | solution.py:48
  62.5 1.5 %collective-permute-done.25.rest_0_ = bf16[128,1024]{1,0:T(8,128)(2,1)S(1)} collective-permute-done((bf16[128,1024]{1,0:T(8,128)(2,1)S(1)}, bf16[128,1024]{1,0:T(8,128)(2,1)S(1)}, u32[]{:S(2)}, u32[]{:S(2)}) %collective-permute-start.25) | collective-permute-done | bytes 262176 | tf_op jit(solution)/shard_map/ppermute | solution.py:48
  64.0 1.8 %collective-permute-done.26.rest_1_ = bf16[128,1024]{1,0:T(8,128)(2,1)S(1)} collective-permute-done((bf16[128,1024]{1,0:T(8,128)(2,1)S(1)}, bf16[128,1024]{1,0:T(8,128)(2,1)S(1)}, u32[]{:S(2)}, u32[]{:S(2)}) %collective-permute-start.26) | collective-permute-done | bytes 262176 | tf_op jit(solution)/shard_map/ppermute | solution.py:48
  66.5 1.7 %collective-permute-start.27 = (bf16[128,1024]{1,0:T(8,128)(2,1)S(1)}, bf16[128,1024]{1,0:T(8,128)(2,1)S(1)}, u32[]{:S(2)}, u32[]{:S(2)}) collective-permute-start(bf16[128,1024]{1,0:T(8,128)(2,1)S(1)} %get-tuple-element.22), channel_id=1, source_target_pairs={{0,2},{1,7},{2,4},{3,1},{4,6},{5,3},{6,0},{7,5},{8,10},{9,15},{10,... | collective-permute-start | bytes 786440 | tf_op jit(solution)/shard_map/ppermute | solution.py:48
  68.9 2.5 %collective-permute-done.28.a0_ref = bf16[128,1024]{1,0:T(8,128)(2,1)S(1)} collective-permute-done((bf16[128,1024]{1,0:T(8,128)(2,1)S(1)}, bf16[128,1024]{1,0:T(8,128)(2,1)S(1)}, u32[]{:S(2)}, u32[]{:S(2)}) %collective-permute-start.28) | collective-permute-done | bytes 262176 | tf_op jit(solution)/shard_map/ppermute | solution.py:48
  71.4 3.8 %collective-permute-done.27.b0_ref = bf16[128,1024]{1,0:T(8,128)(2,1)S(1)} collective-permute-done((bf16[128,1024]{1,0:T(8,128)(2,1)S(1)}, bf16[128,1024]{1,0:T(8,128)(2,1)S(1)}, u32[]{:S(2)}, u32[]{:S(2)}) %collective-permute-start.27) | collective-permute-done | bytes 262176 | tf_op jit(solution)/shard_map/ppermute | solution.py:48
  75.1 1.9 %collective-permute-done.29.a1_ref = bf16[128,1024]{1,0:T(8,128)(2,1)S(1)} collective-permute-done((bf16[128,1024]{1,0:T(8,128)(2,1)S(1)}, bf16[128,1024]{1,0:T(8,128)(2,1)S(1)}, u32[]{:S(2)}, u32[]{:S(2)}) %collective-permute-start.29) | collective-permute-done | bytes 262176 | tf_op jit(solution)/shard_map/ppermute | solution.py:48
  77.6 8.8 %all_to_all.5.sums_ref = f32[8,1,256]{2,1,0:T(1,128)S(1)} all-to-all(f32[8,1,256]{2,1,0:T(1,128)S(1)} %get-tuple-element.27), channel_id=1, replica_groups=mesh['z'=8,'x'=4,'y'=4,'c'=2] {'y','c'}, dimensions={0} | all-to-all | bytes 16384 | tf_op jit(solution)/shard_map/all_to_all | solution.py:453
  86.4 1.0 %normalize.1 = (bf16[256,1024]{1,0:T(8,128)(2,1)}, bf16[256,1024]{1,0:T(8,128)(2,1)}) custom-call(bf16[256,1024]{1,0:T(8,128)(2,1)S(1)} %get-tuple-element.26.hidden_ref, f32[8,1,256]{2,1,0:T(1,128)S(1)} %all_to_all.5.sums_ref, f32[1,1024]{1,0:T(1,128)S(1)} %bitcast.5), custom_call_target="tpu_custom_call" | custom-call | tf_op jit(solution)/shard_map/normalize/pallas_call | solution.py:419
  (53 shorter events, 8.5 us)
Async XLA Ops:
  0.6 47.2 %collective-permute-start = (bf16[512,8192]{1,0:T(8,128)(2,1)}, bf16[512,8192]{1,0:T(8,128)(2,1)}, u32[]{:S(2)}, u32[]{:S(2)}) collective-permute-start(bf16[512,8192]{1,0:T(8,128)(2,1)} %rest_0_.1), channel_id=1, source_target_pairs={{0,1},{1,0},{2,3},{3,2},{4,5},{5,4},{6,7},{7,6},{8,9},{9,8},{10,11... | collective-permute-start | bytes 25165832 | tf_op jit(solution)/shard_map/ppermute | solution.py:54
  4.9 7.7 %collective-permute-start.2 = (bf16[512,128]{1,0:T(8,128)(2,1)S(1)}, bf16[512,128]{1,0:T(8,128)(2,1)S(1)}, u32[]{:S(2)}, u32[]{:S(2)}) collective-permute-start(bf16[512,128]{1,0:T(8,128)(2,1)S(1)} %bitcast.2), channel_id=1, source_target_pairs={{0,64},{1,193},{2,66},{3,195},{4,68},{5,197},{6,70},{7,199},{8,72}... | collective-permute-start | bytes 393224 | tf_op jit(solution)/shard_map/ppermute | solution.py:36
  9.2 7.3 %collective-permute-start.1 = (bf16[512,128]{1,0:T(8,128)(2,1)S(1)}, bf16[512,128]{1,0:T(8,128)(2,1)S(1)}, u32[]{:S(2)}, u32[]{:S(2)}) collective-permute-start(bf16[512,128]{1,0:T(8,128)(2,1)S(1)} %bitcast.3), channel_id=1, source_target_pairs={{0,32},{1,225},{2,34},{3,227},{4,36},{5,229},{6,38},{7,231},{8,40}... | collective-permute-start | bytes 393224 | tf_op jit(solution)/shard_map/ppermute | solution.py:36
  12.6 10.1 %collective-permute-start.4 = (bf16[256,128]{1,0:T(8,128)(2,1)S(1)}, bf16[256,128]{1,0:T(8,128)(2,1)S(1)}, u32[]{:S(2)}, u32[]{:S(2)}) collective-permute-start(bf16[256,128]{1,0:T(8,128)(2,1)S(1)} %constant_dynamic-slice_fusion), channel_id=1, source_target_pairs={{0,64},{1,193},{2,66},{3,195},{4,68},{5,197},{6,70},{7,199},{8,72}... | collective-permute-start | bytes 196616 | tf_op jit(solution)/shard_map/ppermute | solution.py:36
  16.6 6.1 %collective-permute-start.3 = (bf16[512,128]{1,0:T(8,128)(2,1)S(1)}, bf16[512,128]{1,0:T(8,128)(2,1)S(1)}, u32[]{:S(2)}, u32[]{:S(2)}) collective-permute-start(bf16[512,128]{1,0:T(8,128)(2,1)S(1)} %collective-permute-done.1.rest_3_), channel_id=1, source_target_pairs={{0,64},{1,193},{2,66},{3,195},{4,68},{5,197},{6,70},{7,199},{8,72}... | collective-permute-start | bytes 393224 | tf_op jit(solution)/shard_map/ppermute | solution.py:36
  16.9 15.8 %collective-permute-start.6 = (bf16[1280,128]{1,0:T(8,128)(2,1)S(1)}, bf16[1280,128]{1,0:T(8,128)(2,1)S(1)}, u32[]{:S(2)}, u32[]{:S(2)}) collective-permute-start(bf16[1280,128]{1,0:T(8,128)(2,1)S(1)} %constant_dynamic-update-slice_fusion.2), channel_id=1, source_target_pairs={{0,24},{1,9},{2,26},{3,11},{4,28},{5,13},{6,30},{7,15},{8,0},{9,17... | collective-permute-start | bytes 983048 | tf_op jit(solution)/shard_map/ppermute | solution.py:42
  18.2 7.3 %collective-permute-start.14 = (bf16[512,128]{1,0:T(8,128)(2,1)S(1)}, bf16[512,128]{1,0:T(8,128)(2,1)S(1)}, u32[]{:S(2)}, u32[]{:S(2)}) collective-permute-start(bf16[512,128]{1,0:T(8,128)(2,1)S(1)} %collective-permute-done.2.rest_4_), channel_id=1, source_target_pairs={{0,1},{1,0},{2,3},{3,2},{4,5},{5,4},{6,7},{7,6},{8,9},{9,8},{10,11... | collective-permute-start | bytes 393224 | tf_op jit(solution)/shard_map/ppermute | solution.py:54
  22.7 5.8 %collective-permute-start.8 = (bf16[768,128]{1,0:T(8,128)(2,1)S(1)}, bf16[768,128]{1,0:T(8,128)(2,1)S(1)}, u32[]{:S(2)}, u32[]{:S(2)}) collective-permute-start(bf16[768,128]{1,0:T(8,128)(2,1)S(1)} %constant_dynamic-update-slice_fusion.rest_5_), channel_id=1, source_target_pairs={{0,24},{1,9},{2,26},{3,11},{4,28},{5,13},{6,30},{7,15},{8,0},{9,17... | collective-permute-start | bytes 589832 | tf_op jit(solution)/shard_map/ppermute | solution.py:42
  24.0 7.1 %collective-permute-start.7 = (bf16[768,128]{1,0:T(8,128)(2,1)S(1)}, bf16[768,128]{1,0:T(8,128)(2,1)S(1)}, u32[]{:S(2)}, u32[]{:S(2)}) collective-permute-start(bf16[768,128]{1,0:T(8,128)(2,1)S(1)} %constant_dynamic-update-slice_fusion.rest_5_), channel_id=1, source_target_pairs={{0,8},{1,25},{2,10},{3,27},{4,12},{5,29},{6,14},{7,31},{8,16},{9,1... | collective-permute-start | bytes 589832 | tf_op jit(solution)/shard_map/ppermute | solution.py:42
  25.4 8.5 %collective-permute-start.5 = (bf16[1280,128]{1,0:T(8,128)(2,1)S(1)}, bf16[1280,128]{1,0:T(8,128)(2,1)S(1)}, u32[]{:S(2)}, u32[]{:S(2)}) collective-permute-start(bf16[1280,128]{1,0:T(8,128)(2,1)S(1)} %constant_dynamic-update-slice_fusion.2), channel_id=1, source_target_pairs={{0,8},{1,25},{2,10},{3,27},{4,12},{5,29},{6,14},{7,31},{8,16},{9,1... | collective-permute-start | bytes 983048 | tf_op jit(solution)/shard_map/ppermute | solution.py:42
  28.5 8.3 %collective-permute-start.15 = (bf16[768,128]{1,0:T(8,128)(2,1)S(1)}, bf16[768,128]{1,0:T(8,128)(2,1)S(1)}, u32[]{:S(2)}, u32[]{:S(2)}) collective-permute-start(bf16[768,128]{1,0:T(8,128)(2,1)S(1)} %constant_dynamic-update-slice_fusion.rest_5_), channel_id=1, source_target_pairs={{0,1},{1,0},{2,3},{3,2},{4,5},{5,4},{6,7},{7,6},{8,9},{9,8},{10,11... | collective-permute-start | bytes 589832 | tf_op jit(solution)/shard_map/ppermute | solution.py:54
  31.1 2.6 %collective-permute-start.13 = (bf16[512,128]{1,0:T(8,128)(2,1)S(1)}, bf16[512,128]{1,0:T(8,128)(2,1)S(1)}, u32[]{:S(2)}, u32[]{:S(2)}) collective-permute-start(bf16[512,128]{1,0:T(8,128)(2,1)S(1)} %collective-permute-done.1.rest_3_), channel_id=1, source_target_pairs={{0,1},{1,0},{2,3},{3,2},{4,5},{5,4},{6,7},{7,6},{8,9},{9,8},{10,11... | collective-permute-start | bytes 393224 | tf_op jit(solution)/shard_map/ppermute | solution.py:54
  32.7 4.8 %collective-permute-start.12 = (bf16[384,128]{1,0:T(8,128)(2,1)S(1)}, bf16[384,128]{1,0:T(8,128)(2,1)S(1)}, u32[]{:S(2)}, u32[]{:S(2)}) collective-permute-start(bf16[384,128]{1,0:T(8,128)(2,1)S(1)} %slice.19), channel_id=1, source_target_pairs={{0,24},{1,9},{2,26},{3,11},{4,28},{5,13},{6,30},{7,15},{8,0},{9,17... | collective-permute-start | bytes 294920 | tf_op jit(solution)/shard_map/ppermute | solution.py:42
  33.7 8.6 %collective-permute-start.10 = (bf16[640,128]{1,0:T(8,128)(2,1)S(1)}, bf16[640,128]{1,0:T(8,128)(2,1)S(1)}, u32[]{:S(2)}, u32[]{:S(2)}) collective-permute-start(bf16[640,128]{1,0:T(8,128)(2,1)S(1)} %slice.17), channel_id=1, source_target_pairs={{0,24},{1,9},{2,26},{3,11},{4,28},{5,13},{6,30},{7,15},{8,0},{9,17... | collective-permute-start | bytes 491528 | tf_op jit(solution)/shard_map/ppermute | solution.py:42
  33.9 5.5 %collective-permute-start.11 = (bf16[384,128]{1,0:T(8,128)(2,1)S(1)}, bf16[384,128]{1,0:T(8,128)(2,1)S(1)}, u32[]{:S(2)}, u32[]{:S(2)}) collective-permute-start(bf16[384,128]{1,0:T(8,128)(2,1)S(1)} %slice.18), channel_id=1, source_target_pairs={{0,8},{1,25},{2,10},{3,27},{4,12},{5,29},{6,14},{7,31},{8,16},{9,1... | collective-permute-start | bytes 294920 | tf_op jit(solution)/shard_map/ppermute | solution.py:42
  36.8 5.4 %collective-permute-start.9 = (bf16[640,128]{1,0:T(8,128)(2,1)S(1)}, bf16[640,128]{1,0:T(8,128)(2,1)S(1)}, u32[]{:S(2)}, u32[]{:S(2)}) collective-permute-start(bf16[640,128]{1,0:T(8,128)(2,1)S(1)} %slice.16), channel_id=1, source_target_pairs={{0,8},{1,25},{2,10},{3,27},{4,12},{5,29},{6,14},{7,31},{8,16},{9,1... | collective-permute-start | bytes 491528 | tf_op jit(solution)/shard_map/ppermute | solution.py:42
  37.4 6.7 %collective-permute-start.19 = (bf16[768,128]{1,0:T(8,128)(2,1)S(1)}, bf16[768,128]{1,0:T(8,128)(2,1)S(1)}, u32[]{:S(2)}, u32[]{:S(2)}) collective-permute-start(bf16[768,128]{1,0:T(8,128)(2,1)S(1)} %collective-permute-done.8.rest_9_), channel_id=1, source_target_pairs={{0,1},{1,0},{2,3},{3,2},{4,5},{5,4},{6,7},{7,6},{8,9},{9,8},{10,11... | collective-permute-start | bytes 589832 | tf_op jit(solution)/shard_map/ppermute | solution.py:54
  39.4 4.7 %collective-permute-start.23 = (bf16[384,128]{1,0:T(8,128)(2,1)S(1)}, bf16[384,128]{1,0:T(8,128)(2,1)S(1)}, u32[]{:S(2)}, u32[]{:S(2)}) collective-permute-start(bf16[384,128]{1,0:T(8,128)(2,1)S(1)} %collective-permute-done.12.rest_13_), channel_id=1, source_target_pairs={{0,1},{1,0},{2,3},{3,2},{4,5},{5,4},{6,7},{7,6},{8,9},{9,8},{10,11... | collective-permute-start | bytes 294920 | tf_op jit(solution)/shard_map/ppermute | solution.py:54
  42.2 4.2 %collective-permute-start.18 = (bf16[768,128]{1,0:T(8,128)(2,1)S(1)}, bf16[768,128]{1,0:T(8,128)(2,1)S(1)}, u32[]{:S(2)}, u32[]{:S(2)}) collective-permute-start(bf16[768,128]{1,0:T(8,128)(2,1)S(1)} %collective-permute-done.7.rest_8_), channel_id=1, source_target_pairs={{0,1},{1,0},{2,3},{3,2},{4,5},{5,4},{6,7},{7,6},{8,9},{9,8},{10,11... | collective-permute-start | bytes 589832 | tf_op jit(solution)/shard_map/ppermute | solution.py:54
  42.2 5.5 %collective-permute-start.17 = (bf16[1280,128]{1,0:T(8,128)(2,1)S(1)}, bf16[1280,128]{1,0:T(8,128)(2,1)S(1)}, u32[]{:S(2)}, u32[]{:S(2)}) collective-permute-start(bf16[1280,128]{1,0:T(8,128)(2,1)S(1)} %collective-permute-done.6.rest_7_), channel_id=1, source_target_pairs={{0,1},{1,0},{2,3},{3,2},{4,5},{5,4},{6,7},{7,6},{8,9},{9,8},{10,11... | collective-permute-start | bytes 983048 | tf_op jit(solution)/shard_map/ppermute | solution.py:54
  44.2 3.6 %collective-permute-start.16 = (bf16[1280,128]{1,0:T(8,128)(2,1)S(1)}, bf16[1280,128]{1,0:T(8,128)(2,1)S(1)}, u32[]{:S(2)}, u32[]{:S(2)}) collective-permute-start(bf16[1280,128]{1,0:T(8,128)(2,1)S(1)} %collective-permute-done.5.rest_6_), channel_id=1, source_target_pairs={{0,1},{1,0},{2,3},{3,2},{4,5},{5,4},{6,7},{7,6},{8,9},{9,8},{10,11... | collective-permute-start | bytes 983048 | tf_op jit(solution)/shard_map/ppermute | solution.py:54
  44.2 1.9 %collective-permute-start.22 = (bf16[384,128]{1,0:T(8,128)(2,1)S(1)}, bf16[384,128]{1,0:T(8,128)(2,1)S(1)}, u32[]{:S(2)}, u32[]{:S(2)}) collective-permute-start(bf16[384,128]{1,0:T(8,128)(2,1)S(1)} %collective-permute-done.11.rest_12_), channel_id=1, source_target_pairs={{0,1},{1,0},{2,3},{3,2},{4,5},{5,4},{6,7},{7,6},{8,9},{9,8},{10,11... | collective-permute-start | bytes 294920 | tf_op jit(solution)/shard_map/ppermute | solution.py:54
  46.0 1.4 %collective-permute-start.21 = (bf16[640,128]{1,0:T(8,128)(2,1)S(1)}, bf16[640,128]{1,0:T(8,128)(2,1)S(1)}, u32[]{:S(2)}, u32[]{:S(2)}) collective-permute-start(bf16[640,128]{1,0:T(8,128)(2,1)S(1)} %collective-permute-done.10.rest_11_), channel_id=1, source_target_pairs={{0,1},{1,0},{2,3},{3,2},{4,5},{5,4},{6,7},{7,6},{8,9},{9,8},{10,11... | collective-permute-start | bytes 491528 | tf_op jit(solution)/shard_map/ppermute | solution.py:54
  46.4 1.4 %collective-permute-start.20 = (bf16[640,128]{1,0:T(8,128)(2,1)S(1)}, bf16[640,128]{1,0:T(8,128)(2,1)S(1)}, u32[]{:S(2)}, u32[]{:S(2)}) collective-permute-start(bf16[640,128]{1,0:T(8,128)(2,1)S(1)} %collective-permute-done.9.rest_10_), channel_id=1, source_target_pairs={{0,1},{1,0},{2,3},{3,2},{4,5},{5,4},{6,7},{7,6},{8,9},{9,8},{10,11... | collective-permute-start | bytes 491528 | tf_op jit(solution)/shard_map/ppermute | solution.py:54
  53.4 1.6 %collective-permute-start.24 = (bf16[256,512]{1,0:T(8,128)(2,1)S(1)}, bf16[256,512]{1,0:T(8,128)(2,1)S(1)}, u32[]{:S(2)}, u32[]{:S(2)}) collective-permute-start(bf16[256,512]{1,0:T(8,128)(2,1)S(1)} %get-tuple-element.17.a_ref), channel_id=1, source_target_pairs={{0,1},{1,0},{2,3},{3,2},{4,5},{5,4},{6,7},{7,6},{8,9},{9,8},{10,11... | collective-permute-start | bytes 786440 | tf_op jit(solution)/shard_map/ppermute | solution.py:54
  55.8 8.2 %collective-permute-start.25 = (bf16[128,1024]{1,0:T(8,128)(2,1)S(1)}, bf16[128,1024]{1,0:T(8,128)(2,1)S(1)}, u32[]{:S(2)}, u32[]{:S(2)}) collective-permute-start(bf16[128,1024]{1,0:T(8,128)(2,1)S(1)} %get-tuple-element.20), channel_id=1, source_target_pairs={{0,2},{1,7},{2,4},{3,1},{4,6},{5,3},{6,0},{7,5},{8,10},{9,15},{10,... | collective-permute-start | bytes 786440 | tf_op jit(solution)/shard_map/ppermute | solution.py:48
  58.7 7.1 %collective-permute-start.26 = (bf16[128,1024]{1,0:T(8,128)(2,1)S(1)}, bf16[128,1024]{1,0:T(8,128)(2,1)S(1)}, u32[]{:S(2)}, u32[]{:S(2)}) collective-permute-start(bf16[128,1024]{1,0:T(8,128)(2,1)S(1)} %get-tuple-element.21), channel_id=1, source_target_pairs={{0,6},{1,3},{2,0},{3,5},{4,2},{5,7},{6,4},{7,1},{8,14},{9,11},{10,... | collective-permute-start | bytes 786440 | tf_op jit(solution)/shard_map/ppermute | solution.py:48
  59.4 12.0 %collective-permute-start.28 = (bf16[128,1024]{1,0:T(8,128)(2,1)S(1)}, bf16[128,1024]{1,0:T(8,128)(2,1)S(1)}, u32[]{:S(2)}, u32[]{:S(2)}) collective-permute-start(bf16[128,1024]{1,0:T(8,128)(2,1)S(1)} %get-tuple-element.23), channel_id=1, source_target_pairs={{0,6},{1,3},{2,0},{3,5},{4,2},{5,7},{6,4},{7,1},{8,14},{9,11},{10,... | collective-permute-start | bytes 786440 | tf_op jit(solution)/shard_map/ppermute | solution.py:48
  59.5 11.9 %collective-permute-start.30 = (bf16[128,1024]{1,0:T(8,128)(2,1)S(1)}, bf16[128,1024]{1,0:T(8,128)(2,1)S(1)}, u32[]{:S(2)}, u32[]{:S(2)}) collective-permute-start(bf16[128,1024]{1,0:T(8,128)(2,1)S(1)} %get-tuple-element.25), channel_id=1, source_target_pairs={{0,2},{1,7},{2,4},{3,1},{4,6},{5,3},{6,0},{7,5},{8,10},{9,15},{10,... | collective-permute-start | bytes 786440 | tf_op jit(solution)/shard_map/ppermute | solution.py:48
  66.5 19.9 %copy-start.1 = (f32[1024]{0:T(1024)S(1)}, f32[1024]{0:T(1024)}, u32[]{:S(2)}) copy-start(f32[1024]{0:T(1024)} %param.12) | copy-start | bytes 12292
  66.5 8.6 %collective-permute-start.27 = (bf16[128,1024]{1,0:T(8,128)(2,1)S(1)}, bf16[128,1024]{1,0:T(8,128)(2,1)S(1)}, u32[]{:S(2)}, u32[]{:S(2)}) collective-permute-start(bf16[128,1024]{1,0:T(8,128)(2,1)S(1)} %get-tuple-element.22), channel_id=1, source_target_pairs={{0,2},{1,7},{2,4},{3,1},{4,6},{5,3},{6,0},{7,5},{8,10},{9,15},{10,... | collective-permute-start | bytes 786440 | tf_op jit(solution)/shard_map/ppermute | solution.py:48
  68.2 8.8 %collective-permute-start.29 = (bf16[128,1024]{1,0:T(8,128)(2,1)S(1)}, bf16[128,1024]{1,0:T(8,128)(2,1)S(1)}, u32[]{:S(2)}, u32[]{:S(2)}) collective-permute-start(bf16[128,1024]{1,0:T(8,128)(2,1)S(1)} %get-tuple-element.24), channel_id=1, source_target_pairs={{0,6},{1,3},{2,0},{3,5},{4,2},{5,7},{6,4},{7,1},{8,14},{9,11},{10,... | collective-permute-start | bytes 786440 | tf_op jit(solution)/shard_map/ppermute | solution.py:48
  (1 other events, 17.5 us)

commit v2 on v1

--- a/solution.py
+++ b/solution.py
@@ -54,22 +54,72 @@
     return lax.ppermute(array, AXES, permutation(lambda z, x, y, c: (z, x, y, c + 1)))
 
 
-def gather_pairs(own, own_half):
+def choose(ancestors, tile_of_slot):
+    def kernel(first_ref, second_ref, third_ref, tile_of_slot_ref, out_ref):
+        z, x, c = (lax.axis_index(name) for name in ("z", "x", "c"))
+        sign = 1 - 2 * c
+        slots = lax.broadcasted_iota(jnp.int32, (1, TILES), 1)
+        for n in range(NZ):
+            slot = (lax.rem(z - n * sign + NZ, NZ) * NX + x) * 2 + 1
+            tile = jnp.sum(
+                jnp.where(slots == slot, tile_of_slot_ref[...], 0), axis=1, keepdims=True
+            )
+            for k, ref in enumerate((first_ref, second_ref, third_ref)):
+                named = jnp.where(ref[...] == tile, 1.0, 0.0)
+                named = jnp.max(jnp.max(named, axis=1, keepdims=True), axis=0, keepdims=True)
+                out_ref[k * NZ + n : k * NZ + n + 1, :] = jnp.broadcast_to(named, (1, 128))
+
+    return pl.pallas_call(
+        kernel,
+        out_shape=pltpu.VMEM((3 * NZ, 128), jnp.float32),
+        in_specs=[pl.BlockSpec(memory_space=pltpu.VMEM)] * 4,
+        out_specs=pl.BlockSpec(memory_space=pltpu.VMEM),
+        compiler_params=pltpu.CompilerParams(vmem_limit_bytes=4 << 20),
+        name="choose",
+    )(*ancestors, tile_of_slot.reshape(1, TILES))
+
+
+def select(chosen, arrays, steps):
+    total = sum(array.shape[0] for array in arrays) // 2
+
+    def kernel(chosen_ref, *refs):
+        array_refs, out_refs = refs[: len(arrays)], refs[len(arrays) :]
+        for k, out_ref in enumerate(out_refs):
+            to = 0
+            for ref, n in zip(array_refs, steps):
+                second = chosen_ref[k * NZ + n : k * NZ + n + 1, :]
+                first = jnp.broadcast_to(1.0 - second, (TILE, 128)).astype(jnp.bfloat16)
+                second = jnp.broadcast_to(second, (TILE, 128)).astype(jnp.bfloat16)
+                for row in range(0, ref.shape[0], 2 * TILE):
+                    out_ref[to : to + TILE] = (
+                        ref[row : row + TILE] * first + ref[row + TILE : row + 2 * TILE] * second
+                    )
+                    to += TILE
+
+    return pl.pallas_call(
+        kernel,
+        out_shape=[pltpu.VMEM((total, HEAD), jnp.bfloat16)] * 3,
+        in_specs=[pl.BlockSpec(memory_space=pltpu.VMEM)] * (1 + len(arrays)),
+        out_specs=[pl.BlockSpec(memory_space=pltpu.VMEM)] * 3,
+        compiler_params=pltpu.CompilerParams(vmem_limit_bytes=4 << 20),
+        name="select",
+    )(chosen, *arrays)
+
+
+def gather_pairs(own, own_half, ancestors, tile_of_slot):
+    asked_ahead = along_x(ancestors, -1)
+    asked_back = along_x(ancestors, 1)
+    asked_across = along_x(ancestors, 2)
     near1 = along_z(own, 1)
     near2 = along_z(own, 2)
     near3 = along_z(near1, 2)
     half4 = along_z(lax.dynamic_slice_in_dim(near2, lax.axis_index("c") * 256, 256, 0), 2)
-    group1 = jnp.concatenate([own_half, near1, near2], axis=0)
-    ahead1 = along_x(group1, 1)
-    back1 = along_x(group1, -1)
-    group2 = jnp.concatenate([near3, half4], axis=0)
-    ahead2 = along_x(group2, 1)
-    back2 = along_x(group2, -1)
-    far1 = along_x(ahead1[:640], 1)
-    far1_low = along_x(back1[640:], -1)
-    far2 = along_x(ahead2[:384], 1)
-    far2_low = along_x(back2[384:], -1)
-    arrays = [near1, near2, group2, ahead1, back1, ahead2, back2, far1, far1_low, far2, far2_low]
+    chosen = choose((asked_ahead, asked_back, asked_across), tile_of_slot)
+    arrays = [near1, near2, near3, half4]
+    for parts, steps in (((own_half, near1, near2), (0, 1, 2)), ((near3, half4), (3, 4))):
+        messages = select(chosen, parts, steps)
+        for hops, message in reversed(tuple(zip((1, -1, 2), messages))):
+            arrays.append(along_x(message, hops))
     theirs = []
     for array in arrays:
         theirs.append(other_core(array))
@@ -98,22 +148,18 @@
         in_specs=[pl.BlockSpec(memory_space=pltpu.HBM)],
         out_specs=[pl.BlockSpec(memory_space=pltpu.VMEM)] * 2,
         scratch_shapes=[pltpu.SemaphoreType.DMA((2,))],
+        compiler_params=pltpu.CompilerParams(vmem_limit_bytes=4 << 20),
         name="pick",
     )(pltpu.with_memory_space_constraint(keys_values, pltpu.HBM))
 
 
-def spot(refs, steps, hops, row):
-    near1, near2, group2, ahead1, back1, ahead2, back2, far1, far1_low, far2, far2_low = refs
-    if hops == 0 and steps < 3:
-        return (near1, near2)[steps - 1], row
-    row += {0: 0, 1: 256, 2: 768, 3: 0, 4: 512}[steps]
-    if steps < 3:
-        held, far, cut = (None, ahead1, None, back1)[hops], (far1, far1_low), 640
-    else:
-        held, far, cut = (group2, ahead2, None, back2)[hops], (far2, far2_low), 384
-    if hops == 2:
-        return (far[0], row) if row < cut else (far[1], row - cut)
-    return held, row
+def spot(refs, steps, hops, part):
+    whole, (across1, back1, ahead1, across2, back2, ahead2) = refs[:4], refs[4:]
+    if hops == 0:
+        return whole[steps - 1], (0 if steps == 4 else 256 * part), True
+    row = {0: 0, 1: 128, 2: 384, 3: 0, 4: 256}[steps] + (0 if steps in (0, 4) else 128 * part)
+    first, second = {1: (ahead1, ahead2), 3: (back1, back2), 2: (across1, across2)}[hops]
+    return (first if steps < 3 else second), row, False
 
 
 def attend(query, own, mine, theirs, ancestors, tile_of_slot, weight, weight_other):
@@ -177,47 +223,33 @@
             hops = lax.rem((x - chip % NX) * sign + NX, NX)
             to = pl.multiple_of((i + 1 + jnp.where(i >= ANC, 1, 0)) * TILE, TILE)
 
-            def put(target, source, row):
-                start = pl.multiple_of(row + second * TILE, TILE)
+            def put(target, source, row, both):
+                start = pl.multiple_of(row + second * TILE, TILE) if both else row
                 target[pl.ds(to, TILE)] = source[pl.ds(start, TILE)]
-
-            def put_from(target, refs, n, h, row):
-                (ref0, row0), (ref1, row1) = (spot(refs, n, h, row + r) for r in (0, TILE))
-                if ref0 is ref1:
-                    put(target, ref0, row0)
-                else:
-
-                    @pl.when(second == 0)
-                    def _():
-                        target[pl.ds(to, TILE)] = ref0[row0 : row0 + TILE]
-
-                    @pl.when(second == 1)
-                    def _():
-                        target[pl.ds(to, TILE)] = ref1[row1 : row1 + TILE]
 
             def from_chip(n, h):
                 h_other = (NX - h) % NX
                 if n == 0 and h == 0:
-                    put(keys, own_ref, 0)
-                    put(values, own_ref, 256)
+                    put(keys, own_ref, 0, True)
+                    put(values, own_ref, 256, True)
                 elif n in (0, 4):
 
                     @pl.when(c == 0)
                     def _():
-                        put_from(keys, mine_refs, n, h, 0)
-                        put_from(values, theirs_refs, n, h_other, 0)
+                        put(keys, *spot(mine_refs, n, h, 0))
+                        put(values, *spot(theirs_refs, n, h_other, 1))
 
                     @pl.when(c == 1)
                     def _():
-                        put_from(keys, theirs_refs, n, h_other, 0)
-                        put_from(values, mine_refs, n, h, 0)
+                        put(keys, *spot(theirs_refs, n, h_other, 0))
+                        put(values, *spot(mine_refs, n, h, 1))
 
                 elif n < 4:
-                    put_from(keys, mine_refs, n, h, 0)
-                    put_from(values, mine_refs, n, h, 256)
+                    put(keys, *spot(mine_refs, n, h, 0))
+                    put(values, *spot(mine_refs, n, h, 1))
                 else:
-                    put_from(keys, theirs_refs, NZ - n, h_other, 0)
-                    put_from(values, theirs_refs, NZ - n, h_other, 256)
+                    put(keys, *spot(theirs_refs, NZ - n, h_other, 0))
+                    put(values, *spot(theirs_refs, NZ - n, h_other, 1))
 
             def branch(case, low, high):
                 if high - low == 1:
@@ -434,7 +466,7 @@
     own, own_half = pick(keys_values)
     own = own.reshape(BLOCK, HEAD)
     weight_other = other_core(out_weight)
-    mine, theirs = gather_pairs(own, own_half)
+    mine, theirs = gather_pairs(own, own_half, ancestors, tile_of_slot)
     attended, *weights = attend(
         query, own, mine, theirs, ancestors, tile_of_slot, out_weight, weight_other
     )

time: 87.8 us -> 93.8 us (1.068)
  waiting for transfers between devices: 23.4 us -> 33 us
  starting transfers between devices: 43.2 us -> 39.1 us
    ppermute x8 -> x9, waiting for transfers between devices: 3.78 us -> 15.3 us  [along_x(): lax.ppermute(array, AXES, permutation(lambda z, x, y, c: (z, x + hops * (...]
    ppermute x13 -> x12, starting transfers between devices: 17.4 us -> 10.8 us  [other_core(): lax.ppermute(array, AXES, permutation(lambda z, x, y, c: (z, x, y, c + 1)))]
    ppermute x8 -> x9, starting transfers between devices: 8.85 us -> 11.2 us  [along_x(): lax.ppermute(array, AXES, permutation(lambda z, x, y, c: (z, x + hops * (...]
    ppermute x13 -> x12, waiting for transfers between devices: 4.78 us -> 2.54 us  [other_core(): lax.ppermute(array, AXES, permutation(lambda z, x, y, c: (z, x, y, c + 1)))]
where the time goes in v2:
time: 93.8 us; the launch traced here: 93.7 us
  starting transfers between devices  39.1 us (42%)
  waiting for transfers between devices  33 us (35%)
  Pallas kernels  11.2 us (12%)
  blocking collectives  8.79 us (9%)
  between operations  0.96 us (1%)
    ppermute x9, waiting for transfers between devices, along_x(): lax.ppermute(array, AXES, permutation(lambda z, x, y, c: (z, x + hops * (...  15.3 us
    ppermute x6, waiting for transfers between devices, along_y(): lax.ppermute(array, AXES, permutation(lambda z, x, y, c: (z, x, y + hops...  11.4 us
    ppermute x9, starting transfers between devices, along_x(): lax.ppermute(array, AXES, permutation(lambda z, x, y, c: (z, x + hops * (...  11.2 us
    ppermute x12, starting transfers between devices, other_core(): lax.ppermute(array, AXES, permutation(lambda z, x, y, c: (z, x, y, c + 1)))  10.8 us
    ppermute x4, starting transfers between devices, along_z(): lax.ppermute(array, AXES, permutation(lambda z, x, y, c: (z + hops * (1 -...  9.39 us
    all_to_all x1, blocking collectives, layer(): sums = lax.all_to_all(sums, ('y', 'c'), 0, 0, tiled=True)  8.79 us
    ppermute x6, starting transfers between devices, along_y(): lax.ppermute(array, AXES, permutation(lambda z, x, y, c: (z, x, y + hops...  7.61 us
    pallas_call x1, Pallas kernels, attend(): pl.pallas_call(kernel, out_shape=[pltpu.VMEM((2 * TILE, GROUP * HEAD), jn...  5.39 us
  transfers between devices with their start and end apart: 31, of which 15 were waited for; matrix products, arithmetic and copies ran while one was open for 0% of the time, Pallas kernels for 4%

profile of v2, /device:TPU:1, one launch (start us, length us, event | category | flops | bytes accessed | tf_op | source)
XLA Modules:
  0.0 93.7 jit_solution(5112404529449923942)
XLA Ops:
  0.6 3.3 %collective-permute-start = (bf16[512,8192]{1,0:T(8,128)(2,1)}, bf16[512,8192]{1,0:T(8,128)(2,1)}, u32[]{:S(2)}, u32[]{:S(2)}) collective-permute-start(bf16[512,8192]{1,0:T(8,128)(2,1)} %rest_0_.1), channel_id=1, source_target_pairs={{0,1},{1,0},{2,3},{3,2},{4,5},{5,4},{6,7},{7,6},{8,9},{9,8},{10,11... | collective-permute-start | bytes 25165832 | tf_op jit(solution)/shard_map/ppermute | solution.py:54
  4.9 4.4 %collective-permute-start.2 = (bf16[512,128]{1,0:T(8,128)(2,1)S(1)}, bf16[512,128]{1,0:T(8,128)(2,1)S(1)}, u32[]{:S(2)}, u32[]{:S(2)}) collective-permute-start(bf16[512,128]{1,0:T(8,128)(2,1)S(1)} %bitcast.3), channel_id=1, source_target_pairs={{0,64},{1,193},{2,66},{3,195},{4,68},{5,197},{6,70},{7,199},{8,72}... | collective-permute-start | bytes 393224 | tf_op jit(solution)/shard_map/ppermute | solution.py:36
  10.0 2.6 %collective-permute-done.2.refs_2_.rest_4_ = bf16[512,128]{1,0:T(8,128)(2,1)S(1)} collective-permute-done((bf16[512,128]{1,0:T(8,128)(2,1)S(1)}, bf16[512,128]{1,0:T(8,128)(2,1)S(1)}, u32[]{:S(2)}, u32[]{:S(2)}) %collective-permute-start.2) | collective-permute-done | bytes 131104 | tf_op jit(solution)/shard_map/ppermute | solution.py:36
  12.6 4.0 %collective-permute-start.4 = (bf16[256,128]{1,0:T(8,128)(2,1)S(1)}, bf16[256,128]{1,0:T(8,128)(2,1)S(1)}, u32[]{:S(2)}, u32[]{:S(2)}) collective-permute-start(bf16[256,128]{1,0:T(8,128)(2,1)S(1)} %constant_dynamic-slice_fusion), channel_id=1, source_target_pairs={{0,64},{1,193},{2,66},{3,195},{4,68},{5,197},{6,70},{7,199},{8,72}... | collective-permute-start | bytes 196616 | tf_op jit(solution)/shard_map/ppermute | solution.py:36
  16.8 1.1 %collective-permute-done.4.refs_1_.rest_6_ = bf16[256,128]{1,0:T(8,128)(2,1)S(1)} collective-permute-done((bf16[256,128]{1,0:T(8,128)(2,1)S(1)}, bf16[256,128]{1,0:T(8,128)(2,1)S(1)}, u32[]{:S(2)}, u32[]{:S(2)}) %collective-permute-start.4) | collective-permute-done | bytes 65568 | tf_op jit(solution)/shard_map/ppermute | solution.py:36
  17.9 1.1 %collective-permute-start.17 = (bf16[256,128]{1,0:T(8,128)(2,1)S(1)}, bf16[256,128]{1,0:T(8,128)(2,1)S(1)}, u32[]{:S(2)}, u32[]{:S(2)}) collective-permute-start(bf16[256,128]{1,0:T(8,128)(2,1)S(1)} %collective-permute-done.4.refs_1_.rest_6_), channel_id=1, source_target_pairs={{0,1},{1,0},{2,3},{3,2},{4,5},{5,4},{6,7},{7,6},{8,9},{9,8},{10,11... | collective-permute-start | bytes 196616 | tf_op jit(solution)/shard_map/ppermute | solution.py:54
  19.0 2.5 %collective-permute-start.6 = (s32[2,12]{1,0:T(2,128)}, s32[2,12]{1,0:T(2,128)S(1)}, u32[]{:S(2)}, u32[]{:S(2)}) collective-permute-start(s32[2,12]{1,0:T(2,128)} %ancestors_hbm.1), channel_id=1, source_target_pairs={{0,8},{1,25},{2,10},{3,27},{4,12},{5,29},{6,14},{7,31},{8,16},{9,1... | collective-permute-start | bytes 296 | tf_op jit(solution)/shard_map/ppermute | solution.py:42
  22.8 3.9 %collective-permute-done.5.first_ref = s32[2,12]{1,0:T(2,128)S(1)} collective-permute-done((s32[2,12]{1,0:T(2,128)}, s32[2,12]{1,0:T(2,128)S(1)}, u32[]{:S(2)}, u32[]{:S(2)}) %collective-permute-start.5) | collective-permute-done | bytes 128 | tf_op jit(solution)/shard_map/ppermute | solution.py:42
  26.8 0.9 %collective-permute-start.7 = (s32[2,12]{1,0:T(2,128)}, s32[2,12]{1,0:T(2,128)S(1)}, u32[]{:S(2)}, u32[]{:S(2)}) collective-permute-start(s32[2,12]{1,0:T(2,128)} %ancestors_hbm.1), channel_id=1, source_target_pairs={{0,16},{1,17},{2,18},{3,19},{4,20},{5,21},{6,22},{7,23},{8,24},{9,... | collective-permute-start | bytes 296 | tf_op jit(solution)/shard_map/ppermute | solution.py:42
  27.7 3.2 %collective-permute-done.7.third_ref = s32[2,12]{1,0:T(2,128)S(1)} collective-permute-done((s32[2,12]{1,0:T(2,128)}, s32[2,12]{1,0:T(2,128)S(1)}, u32[]{:S(2)}, u32[]{:S(2)}) %collective-permute-start.7) | collective-permute-done | bytes 128 | tf_op jit(solution)/shard_map/ppermute | solution.py:42
  30.9 2.1 %collective-permute-start.14 = (bf16[512,128]{1,0:T(8,128)(2,1)S(1)}, bf16[512,128]{1,0:T(8,128)(2,1)S(1)}, u32[]{:S(2)}, u32[]{:S(2)}) collective-permute-start(bf16[512,128]{1,0:T(8,128)(2,1)S(1)} %collective-permute-done.1.refs_1_.rest_3_), channel_id=1, source_target_pairs={{0,1},{1,0},{2,3},{3,2},{4,5},{5,4},{6,7},{7,6},{8,9},{9,8},{10,11... | collective-permute-start | bytes 393224 | tf_op jit(solution)/shard_map/ppermute | solution.py:54
  34.1 1.6 %collective-permute-start.8 = (bf16[640,128]{1,0:T(8,128)(2,1)S(1)}, bf16[640,128]{1,0:T(8,128)(2,1)S(1)}, u32[]{:S(2)}, u32[]{:S(2)}) collective-permute-start(bf16[640,128]{1,0:T(8,128)(2,1)S(1)} %get-tuple-element.23), channel_id=1, source_target_pairs={{0,16},{1,17},{2,18},{3,19},{4,20},{5,21},{6,22},{7,23},{8,24},{9,... | collective-permute-start | bytes 491528 | tf_op jit(solution)/shard_map/ppermute | solution.py:42
  35.7 1.5 %collective-permute-start.9 = (bf16[640,128]{1,0:T(8,128)(2,1)S(1)}, bf16[640,128]{1,0:T(8,128)(2,1)S(1)}, u32[]{:S(2)}, u32[]{:S(2)}) collective-permute-start(bf16[640,128]{1,0:T(8,128)(2,1)S(1)} %get-tuple-element.24), channel_id=1, source_target_pairs={{0,24},{1,9},{2,26},{3,11},{4,28},{5,13},{6,30},{7,15},{8,0},{9,17... | collective-permute-start | bytes 491528 | tf_op jit(solution)/shard_map/ppermute | solution.py:42
  37.2 1.2 %collective-permute-start.10 = (bf16[640,128]{1,0:T(8,128)(2,1)S(1)}, bf16[640,128]{1,0:T(8,128)(2,1)S(1)}, u32[]{:S(2)}, u32[]{:S(2)}) collective-permute-start(bf16[640,128]{1,0:T(8,128)(2,1)S(1)} %get-tuple-element.25), channel_id=1, source_target_pairs={{0,8},{1,25},{2,10},{3,27},{4,12},{5,29},{6,14},{7,31},{8,16},{9,1... | collective-permute-start | bytes 491528 | tf_op jit(solution)/shard_map/ppermute | solution.py:42
  39.3 2.2 %collective-permute-done.8.rest_7_ = bf16[640,128]{1,0:T(8,128)(2,1)S(1)} collective-permute-done((bf16[640,128]{1,0:T(8,128)(2,1)S(1)}, bf16[640,128]{1,0:T(8,128)(2,1)S(1)}, u32[]{:S(2)}, u32[]{:S(2)}) %collective-permute-start.8) | collective-permute-done | bytes 163872 | tf_op jit(solution)/shard_map/ppermute | solution.py:42
  41.6 4.0 %collective-permute-done.9.rest_8_ = bf16[640,128]{1,0:T(8,128)(2,1)S(1)} collective-permute-done((bf16[640,128]{1,0:T(8,128)(2,1)S(1)}, bf16[640,128]{1,0:T(8,128)(2,1)S(1)}, u32[]{:S(2)}, u32[]{:S(2)}) %collective-permute-start.9) | collective-permute-done | bytes 163872 | tf_op jit(solution)/shard_map/ppermute | solution.py:42
  46.4 2.1 %collective-permute-start.13 = (bf16[384,128]{1,0:T(8,128)(2,1)S(1)}, bf16[384,128]{1,0:T(8,128)(2,1)S(1)}, u32[]{:S(2)}, u32[]{:S(2)}) collective-permute-start(bf16[384,128]{1,0:T(8,128)(2,1)S(1)} %get-tuple-element.28), channel_id=1, source_target_pairs={{0,8},{1,25},{2,10},{3,27},{4,12},{5,29},{6,14},{7,31},{8,16},{9,1... | collective-permute-start | bytes 294920 | tf_op jit(solution)/shard_map/ppermute | solution.py:42
  49.1 1.1 %collective-permute-done.13.rest_12_ = bf16[384,128]{1,0:T(8,128)(2,1)S(1)} collective-permute-done((bf16[384,128]{1,0:T(8,128)(2,1)S(1)}, bf16[384,128]{1,0:T(8,128)(2,1)S(1)}, u32[]{:S(2)}, u32[]{:S(2)}) %collective-permute-start.13) | collective-permute-done | bytes 98336 | tf_op jit(solution)/shard_map/ppermute | solution.py:42
  50.1 2.1 %collective-permute-start.18 = (bf16[640,128]{1,0:T(8,128)(2,1)S(1)}, bf16[640,128]{1,0:T(8,128)(2,1)S(1)}, u32[]{:S(2)}, u32[]{:S(2)}) collective-permute-start(bf16[640,128]{1,0:T(8,128)(2,1)S(1)} %collective-permute-done.8.rest_7_), channel_id=1, source_target_pairs={{0,1},{1,0},{2,3},{3,2},{4,5},{5,4},{6,7},{7,6},{8,9},{9,8},{10,11... | collective-permute-start | bytes 491528 | tf_op jit(solution)/shard_map/ppermute | solution.py:54
  52.8 1.2 %collective-permute-done.23.rest_22_ = bf16[384,128]{1,0:T(8,128)(2,1)S(1)} collective-permute-done((bf16[384,128]{1,0:T(8,128)(2,1)S(1)}, bf16[384,128]{1,0:T(8,128)(2,1)S(1)}, u32[]{:S(2)}, u32[]{:S(2)}) %collective-permute-start.23) | collective-permute-done | bytes 98336 | tf_op jit(solution)/shard_map/ppermute | solution.py:54
  54.1 5.4 %attend.1 = (bf16[256,512]{1,0:T(8,128)(2,1)S(1)}, bf16[4,512,1024]{2,1,0:T(8,128)(2,1)S(1)}, bf16[4,512,1024]{2,1,0:T(8,128)(2,1)S(1)}) custom-call(s32[2,12]{1,0:T(2,128)} %ancestors_hbm.1, s32[64]{0:T(128)} %tile_of_slot_hbm.1, bf16[256,512]{1,0:T(8,128)(2,1)} %query_hbm.1, bf16[512,8192]{1,0:T(8,128)(2,1)} %rest_0_.1, ...), custom_call_target="tpu_custom_call" | custom-call | tf_op jit(solution)/shard_map/attend/pallas_call | solution.py:315
  59.8 1.3 %collective-permute-done.24.b_ref = bf16[256,512]{1,0:T(8,128)(2,1)S(1)} collective-permute-done((bf16[256,512]{1,0:T(8,128)(2,1)S(1)}, bf16[256,512]{1,0:T(8,128)(2,1)S(1)}, u32[]{:S(2)}, u32[]{:S(2)}) %collective-permute-start.24) | collective-permute-done | bytes 262176 | tf_op jit(solution)/shard_map/ppermute | solution.py:54
  61.8 2.9 %collective-permute-start.25 = (bf16[128,1024]{1,0:T(8,128)(2,1)S(1)}, bf16[128,1024]{1,0:T(8,128)(2,1)S(1)}, u32[]{:S(2)}, u32[]{:S(2)}) collective-permute-start(bf16[128,1024]{1,0:T(8,128)(2,1)S(1)} %get-tuple-element.32), channel_id=1, source_target_pairs={{0,2},{1,7},{2,4},{3,1},{4,6},{5,3},{6,0},{7,5},{8,10},{9,15},{10,... | collective-permute-start | bytes 786440 | tf_op jit(solution)/shard_map/ppermute | solution.py:48
  65.5 3.0 %collective-permute-start.30 = (bf16[128,1024]{1,0:T(8,128)(2,1)S(1)}, bf16[128,1024]{1,0:T(8,128)(2,1)S(1)}, u32[]{:S(2)}, u32[]{:S(2)}) collective-permute-start(bf16[128,1024]{1,0:T(8,128)(2,1)S(1)} %get-tuple-element.37), channel_id=1, source_target_pairs={{0,2},{1,7},{2,4},{3,1},{4,6},{5,3},{6,0},{7,5},{8,10},{9,15},{10,... | collective-permute-start | bytes 786440 | tf_op jit(solution)/shard_map/ppermute | solution.py:48
  68.5 1.5 %collective-permute-done.25.rest_0_ = bf16[128,1024]{1,0:T(8,128)(2,1)S(1)} collective-permute-done((bf16[128,1024]{1,0:T(8,128)(2,1)S(1)}, bf16[128,1024]{1,0:T(8,128)(2,1)S(1)}, u32[]{:S(2)}, u32[]{:S(2)}) %collective-permute-start.25) | collective-permute-done | bytes 262176 | tf_op jit(solution)/shard_map/ppermute | solution.py:48
  70.0 1.8 %collective-permute-done.26.rest_1_ = bf16[128,1024]{1,0:T(8,128)(2,1)S(1)} collective-permute-done((bf16[128,1024]{1,0:T(8,128)(2,1)S(1)}, bf16[128,1024]{1,0:T(8,128)(2,1)S(1)}, u32[]{:S(2)}, u32[]{:S(2)}) %collective-permute-start.26) | collective-permute-done | bytes 262176 | tf_op jit(solution)/shard_map/ppermute | solution.py:48
  72.6 1.7 %collective-permute-start.27 = (bf16[128,1024]{1,0:T(8,128)(2,1)S(1)}, bf16[128,1024]{1,0:T(8,128)(2,1)S(1)}, u32[]{:S(2)}, u32[]{:S(2)}) collective-permute-start(bf16[128,1024]{1,0:T(8,128)(2,1)S(1)} %get-tuple-element.34), channel_id=1, source_target_pairs={{0,2},{1,7},{2,4},{3,1},{4,6},{5,3},{6,0},{7,5},{8,10},{9,15},{10,... | collective-permute-start | bytes 786440 | tf_op jit(solution)/shard_map/ppermute | solution.py:48
  74.9 2.5 %collective-permute-done.28.a0_ref = bf16[128,1024]{1,0:T(8,128)(2,1)S(1)} collective-permute-done((bf16[128,1024]{1,0:T(8,128)(2,1)S(1)}, bf16[128,1024]{1,0:T(8,128)(2,1)S(1)}, u32[]{:S(2)}, u32[]{:S(2)}) %collective-permute-start.28) | collective-permute-done | bytes 262176 | tf_op jit(solution)/shard_map/ppermute | solution.py:48
  77.4 3.7 %collective-permute-done.27.b0_ref = bf16[128,1024]{1,0:T(8,128)(2,1)S(1)} collective-permute-done((bf16[128,1024]{1,0:T(8,128)(2,1)S(1)}, bf16[128,1024]{1,0:T(8,128)(2,1)S(1)}, u32[]{:S(2)}, u32[]{:S(2)}) %collective-permute-start.27) | collective-permute-done | bytes 262176 | tf_op jit(solution)/shard_map/ppermute | solution.py:48
  81.2 1.9 %collective-permute-done.29.a1_ref = bf16[128,1024]{1,0:T(8,128)(2,1)S(1)} collective-permute-done((bf16[128,1024]{1,0:T(8,128)(2,1)S(1)}, bf16[128,1024]{1,0:T(8,128)(2,1)S(1)}, u32[]{:S(2)}, u32[]{:S(2)}) %collective-permute-start.29) | collective-permute-done | bytes 262176 | tf_op jit(solution)/shard_map/ppermute | solution.py:48
  83.7 8.8 %all_to_all.5.sums_ref = f32[8,1,256]{2,1,0:T(1,128)S(1)} all-to-all(f32[8,1,256]{2,1,0:T(1,128)S(1)} %get-tuple-element.39), channel_id=1, replica_groups=mesh['z'=8,'x'=4,'y'=4,'c'=2] {'y','c'}, dimensions={0} | all-to-all | bytes 16384 | tf_op jit(solution)/shard_map/all_to_all | solution.py:485
  92.5 1.0 %normalize.1 = (bf16[256,1024]{1,0:T(8,128)(2,1)}, bf16[256,1024]{1,0:T(8,128)(2,1)}) custom-call(bf16[256,1024]{1,0:T(8,128)(2,1)S(1)} %get-tuple-element.38.hidden_ref, f32[8,1,256]{2,1,0:T(1,128)S(1)} %all_to_all.5.sums_ref, f32[1,1024]{1,0:T(1,128)S(1)} %bitcast.6), custom_call_target="tpu_custom_call" | custom-call | tf_op jit(solution)/shard_map/normalize/pallas_call | solution.py:451
  (49 shorter events, 11.2 us)
Async XLA Ops:
  0.6 53.4 %collective-permute-start = (bf16[512,8192]{1,0:T(8,128)(2,1)}, bf16[512,8192]{1,0:T(8,128)(2,1)}, u32[]{:S(2)}, u32[]{:S(2)}) collective-permute-start(bf16[512,8192]{1,0:T(8,128)(2,1)} %rest_0_.1), channel_id=1, source_target_pairs={{0,1},{1,0},{2,3},{3,2},{4,5},{5,4},{6,7},{7,6},{8,9},{9,8},{10,11... | collective-permute-start | bytes 25165832 | tf_op jit(solution)/shard_map/ppermute | solution.py:54
  4.9 7.7 %collective-permute-start.2 = (bf16[512,128]{1,0:T(8,128)(2,1)S(1)}, bf16[512,128]{1,0:T(8,128)(2,1)S(1)}, u32[]{:S(2)}, u32[]{:S(2)}) collective-permute-start(bf16[512,128]{1,0:T(8,128)(2,1)S(1)} %bitcast.3), channel_id=1, source_target_pairs={{0,64},{1,193},{2,66},{3,195},{4,68},{5,197},{6,70},{7,199},{8,72}... | collective-permute-start | bytes 393224 | tf_op jit(solution)/shard_map/ppermute | solution.py:36
  9.2 7.3 %collective-permute-start.1 = (bf16[512,128]{1,0:T(8,128)(2,1)S(1)}, bf16[512,128]{1,0:T(8,128)(2,1)S(1)}, u32[]{:S(2)}, u32[]{:S(2)}) collective-permute-start(bf16[512,128]{1,0:T(8,128)(2,1)S(1)} %bitcast.4), channel_id=1, source_target_pairs={{0,32},{1,225},{2,34},{3,227},{4,36},{5,229},{6,38},{7,231},{8,40}... | collective-permute-start | bytes 393224 | tf_op jit(solution)/shard_map/ppermute | solution.py:36
  12.6 5.3 %collective-permute-start.4 = (bf16[256,128]{1,0:T(8,128)(2,1)S(1)}, bf16[256,128]{1,0:T(8,128)(2,1)S(1)}, u32[]{:S(2)}, u32[]{:S(2)}) collective-permute-start(bf16[256,128]{1,0:T(8,128)(2,1)S(1)} %constant_dynamic-slice_fusion), channel_id=1, source_target_pairs={{0,64},{1,193},{2,66},{3,195},{4,68},{5,197},{6,70},{7,199},{8,72}... | collective-permute-start | bytes 196616 | tf_op jit(solution)/shard_map/ppermute | solution.py:36
  16.6 19.1 %collective-permute-start.15 = (bf16[512,128]{1,0:T(8,128)(2,1)S(1)}, bf16[512,128]{1,0:T(8,128)(2,1)S(1)}, u32[]{:S(2)}, u32[]{:S(2)}) collective-permute-start(bf16[512,128]{1,0:T(8,128)(2,1)S(1)} %collective-permute-done.2.refs_2_.rest_4_), channel_id=1, source_target_pairs={{0,1},{1,0},{2,3},{3,2},{4,5},{5,4},{6,7},{7,6},{8,9},{9,8},{10,11... | collective-permute-start | bytes 393224 | tf_op jit(solution)/shard_map/ppermute | solution.py:54
  16.6 20.6 %collective-permute-start.3 = (bf16[512,128]{1,0:T(8,128)(2,1)S(1)}, bf16[512,128]{1,0:T(8,128)(2,1)S(1)}, u32[]{:S(2)}, u32[]{:S(2)}) collective-permute-start(bf16[512,128]{1,0:T(8,128)(2,1)S(1)} %collective-permute-done.1.refs_1_.rest_3_), channel_id=1, source_target_pairs={{0,64},{1,193},{2,66},{3,195},{4,68},{5,197},{6,70},{7,199},{8,72}... | collective-permute-start | bytes 393224 | tf_op jit(solution)/shard_map/ppermute | solution.py:36
  17.9 16.2 %collective-permute-start.17 = (bf16[256,128]{1,0:T(8,128)(2,1)S(1)}, bf16[256,128]{1,0:T(8,128)(2,1)S(1)}, u32[]{:S(2)}, u32[]{:S(2)}) collective-permute-start(bf16[256,128]{1,0:T(8,128)(2,1)S(1)} %collective-permute-done.4.refs_1_.rest_6_), channel_id=1, source_target_pairs={{0,1},{1,0},{2,3},{3,2},{4,5},{5,4},{6,7},{7,6},{8,9},{9,8},{10,11... | collective-permute-start | bytes 196616 | tf_op jit(solution)/shard_map/ppermute | solution.py:54
  19.0 3.4 %collective-permute-start.6 = (s32[2,12]{1,0:T(2,128)}, s32[2,12]{1,0:T(2,128)S(1)}, u32[]{:S(2)}, u32[]{:S(2)}) collective-permute-start(s32[2,12]{1,0:T(2,128)} %ancestors_hbm.1), channel_id=1, source_target_pairs={{0,8},{1,25},{2,10},{3,27},{4,12},{5,29},{6,14},{7,31},{8,16},{9,1... | collective-permute-start | bytes 296 | tf_op jit(solution)/shard_map/ppermute | solution.py:42
  22.4 4.4 %collective-permute-start.5 = (s32[2,12]{1,0:T(2,128)}, s32[2,12]{1,0:T(2,128)S(1)}, u32[]{:S(2)}, u32[]{:S(2)}) collective-permute-start(s32[2,12]{1,0:T(2,128)} %ancestors_hbm.1), channel_id=1, source_target_pairs={{0,24},{1,9},{2,26},{3,11},{4,28},{5,13},{6,30},{7,15},{8,0},{9,17... | collective-permute-start | bytes 296 | tf_op jit(solution)/shard_map/ppermute | solution.py:42
  26.8 4.1 %collective-permute-start.7 = (s32[2,12]{1,0:T(2,128)}, s32[2,12]{1,0:T(2,128)S(1)}, u32[]{:S(2)}, u32[]{:S(2)}) collective-permute-start(s32[2,12]{1,0:T(2,128)} %ancestors_hbm.1), channel_id=1, source_target_pairs={{0,16},{1,17},{2,18},{3,19},{4,20},{5,21},{6,22},{7,23},{8,24},{9,... | collective-permute-start | bytes 296 | tf_op jit(solution)/shard_map/ppermute | solution.py:42
  30.9 7.6 %collective-permute-start.14 = (bf16[512,128]{1,0:T(8,128)(2,1)S(1)}, bf16[512,128]{1,0:T(8,128)(2,1)S(1)}, u32[]{:S(2)}, u32[]{:S(2)}) collective-permute-start(bf16[512,128]{1,0:T(8,128)(2,1)S(1)} %collective-permute-done.1.refs_1_.rest_3_), channel_id=1, source_target_pairs={{0,1},{1,0},{2,3},{3,2},{4,5},{5,4},{6,7},{7,6},{8,9},{9,8},{10,11... | collective-permute-start | bytes 393224 | tf_op jit(solution)/shard_map/ppermute | solution.py:54
  34.1 7.4 %collective-permute-start.8 = (bf16[640,128]{1,0:T(8,128)(2,1)S(1)}, bf16[640,128]{1,0:T(8,128)(2,1)S(1)}, u32[]{:S(2)}, u32[]{:S(2)}) collective-permute-start(bf16[640,128]{1,0:T(8,128)(2,1)S(1)} %get-tuple-element.23), channel_id=1, source_target_pairs={{0,16},{1,17},{2,18},{3,19},{4,20},{5,21},{6,22},{7,23},{8,24},{9,... | collective-permute-start | bytes 491528 | tf_op jit(solution)/shard_map/ppermute | solution.py:42
  35.7 9.9 %collective-permute-start.9 = (bf16[640,128]{1,0:T(8,128)(2,1)S(1)}, bf16[640,128]{1,0:T(8,128)(2,1)S(1)}, u32[]{:S(2)}, u32[]{:S(2)}) collective-permute-start(bf16[640,128]{1,0:T(8,128)(2,1)S(1)} %get-tuple-element.24), channel_id=1, source_target_pairs={{0,24},{1,9},{2,26},{3,11},{4,28},{5,13},{6,30},{7,15},{8,0},{9,17... | collective-permute-start | bytes 491528 | tf_op jit(solution)/shard_map/ppermute | solution.py:42
  37.2 9.2 %collective-permute-start.10 = (bf16[640,128]{1,0:T(8,128)(2,1)S(1)}, bf16[640,128]{1,0:T(8,128)(2,1)S(1)}, u32[]{:S(2)}, u32[]{:S(2)}) collective-permute-start(bf16[640,128]{1,0:T(8,128)(2,1)S(1)} %get-tuple-element.25), channel_id=1, source_target_pairs={{0,8},{1,25},{2,10},{3,27},{4,12},{5,29},{6,14},{7,31},{8,16},{9,1... | collective-permute-start | bytes 491528 | tf_op jit(solution)/shard_map/ppermute | solution.py:42
  38.5 10.0 %collective-permute-start.11 = (bf16[384,128]{1,0:T(8,128)(2,1)S(1)}, bf16[384,128]{1,0:T(8,128)(2,1)S(1)}, u32[]{:S(2)}, u32[]{:S(2)}) collective-permute-start(bf16[384,128]{1,0:T(8,128)(2,1)S(1)} %get-tuple-element.26), channel_id=1, source_target_pairs={{0,16},{1,17},{2,18},{3,19},{4,20},{5,21},{6,22},{7,23},{8,24},{9,... | collective-permute-start | bytes 294920 | tf_op jit(solution)/shard_map/ppermute | solution.py:42
  41.5 7.1 %collective-permute-start.12 = (bf16[384,128]{1,0:T(8,128)(2,1)S(1)}, bf16[384,128]{1,0:T(8,128)(2,1)S(1)}, u32[]{:S(2)}, u32[]{:S(2)}) collective-permute-start(bf16[384,128]{1,0:T(8,128)(2,1)S(1)} %get-tuple-element.27), channel_id=1, source_target_pairs={{0,24},{1,9},{2,26},{3,11},{4,28},{5,13},{6,30},{7,15},{8,0},{9,17... | collective-permute-start | bytes 294920 | tf_op jit(solution)/shard_map/ppermute | solution.py:42
  45.6 6.6 %collective-permute-start.16 = (bf16[512,128]{1,0:T(8,128)(2,1)S(1)}, bf16[512,128]{1,0:T(8,128)(2,1)S(1)}, u32[]{:S(2)}, u32[]{:S(2)}) collective-permute-start(bf16[512,128]{1,0:T(8,128)(2,1)S(1)} %collective-permute-done.3.refs_0_.rest_5_), channel_id=1, source_target_pairs={{0,1},{1,0},{2,3},{3,2},{4,5},{5,4},{6,7},{7,6},{8,9},{9,8},{10,11... | collective-permute-start | bytes 393224 | tf_op jit(solution)/shard_map/ppermute | solution.py:54
  46.4 3.7 %collective-permute-start.13 = (bf16[384,128]{1,0:T(8,128)(2,1)S(1)}, bf16[384,128]{1,0:T(8,128)(2,1)S(1)}, u32[]{:S(2)}, u32[]{:S(2)}) collective-permute-start(bf16[384,128]{1,0:T(8,128)(2,1)S(1)} %get-tuple-element.28), channel_id=1, source_target_pairs={{0,8},{1,25},{2,10},{3,27},{4,12},{5,29},{6,14},{7,31},{8,16},{9,1... | collective-permute-start | bytes 294920 | tf_op jit(solution)/shard_map/ppermute | solution.py:42
  48.5 3.7 %collective-permute-start.21 = (bf16[384,128]{1,0:T(8,128)(2,1)S(1)}, bf16[384,128]{1,0:T(8,128)(2,1)S(1)}, u32[]{:S(2)}, u32[]{:S(2)}) collective-permute-start(bf16[384,128]{1,0:T(8,128)(2,1)S(1)} %collective-permute-done.11.rest_10_), channel_id=1, source_target_pairs={{0,1},{1,0},{2,3},{3,2},{4,5},{5,4},{6,7},{7,6},{8,9},{9,8},{10,11... | collective-permute-start | bytes 294920 | tf_op jit(solution)/shard_map/ppermute | solution.py:54
  48.5 4.2 %collective-permute-start.22 = (bf16[384,128]{1,0:T(8,128)(2,1)S(1)}, bf16[384,128]{1,0:T(8,128)(2,1)S(1)}, u32[]{:S(2)}, u32[]{:S(2)}) collective-permute-start(bf16[384,128]{1,0:T(8,128)(2,1)S(1)} %collective-permute-done.12.rest_11_), channel_id=1, source_target_pairs={{0,1},{1,0},{2,3},{3,2},{4,5},{5,4},{6,7},{7,6},{8,9},{9,8},{10,11... | collective-permute-start | bytes 294920 | tf_op jit(solution)/shard_map/ppermute | solution.py:54
  50.1 3.9 %collective-permute-start.18 = (bf16[640,128]{1,0:T(8,128)(2,1)S(1)}, bf16[640,128]{1,0:T(8,128)(2,1)S(1)}, u32[]{:S(2)}, u32[]{:S(2)}) collective-permute-start(bf16[640,128]{1,0:T(8,128)(2,1)S(1)} %collective-permute-done.8.rest_7_), channel_id=1, source_target_pairs={{0,1},{1,0},{2,3},{3,2},{4,5},{5,4},{6,7},{7,6},{8,9},{9,8},{10,11... | collective-permute-start | bytes 491528 | tf_op jit(solution)/shard_map/ppermute | solution.py:54
  52.2 1.8 %collective-permute-start.19 = (bf16[640,128]{1,0:T(8,128)(2,1)S(1)}, bf16[640,128]{1,0:T(8,128)(2,1)S(1)}, u32[]{:S(2)}, u32[]{:S(2)}) collective-permute-start(bf16[640,128]{1,0:T(8,128)(2,1)S(1)} %collective-permute-done.9.rest_8_), channel_id=1, source_target_pairs={{0,1},{1,0},{2,3},{3,2},{4,5},{5,4},{6,7},{7,6},{8,9},{9,8},{10,11... | collective-permute-start | bytes 491528 | tf_op jit(solution)/shard_map/ppermute | solution.py:54
  52.2 1.8 %collective-permute-start.20 = (bf16[640,128]{1,0:T(8,128)(2,1)S(1)}, bf16[640,128]{1,0:T(8,128)(2,1)S(1)}, u32[]{:S(2)}, u32[]{:S(2)}) collective-permute-start(bf16[640,128]{1,0:T(8,128)(2,1)S(1)} %collective-permute-done.10.rest_9_), channel_id=1, source_target_pairs={{0,1},{1,0},{2,3},{3,2},{4,5},{5,4},{6,7},{7,6},{8,9},{9,8},{10,11... | collective-permute-start | bytes 491528 | tf_op jit(solution)/shard_map/ppermute | solution.py:54
  52.8 1.3 %collective-permute-start.23 = (bf16[384,128]{1,0:T(8,128)(2,1)S(1)}, bf16[384,128]{1,0:T(8,128)(2,1)S(1)}, u32[]{:S(2)}, u32[]{:S(2)}) collective-permute-start(bf16[384,128]{1,0:T(8,128)(2,1)S(1)} %collective-permute-done.13.rest_12_), channel_id=1, source_target_pairs={{0,1},{1,0},{2,3},{3,2},{4,5},{5,4},{6,7},{7,6},{8,9},{9,8},{10,11... | collective-permute-start | bytes 294920 | tf_op jit(solution)/shard_map/ppermute | solution.py:54
  59.5 1.6 %collective-permute-start.24 = (bf16[256,512]{1,0:T(8,128)(2,1)S(1)}, bf16[256,512]{1,0:T(8,128)(2,1)S(1)}, u32[]{:S(2)}, u32[]{:S(2)}) collective-permute-start(bf16[256,512]{1,0:T(8,128)(2,1)S(1)} %get-tuple-element.29.a_ref), channel_id=1, source_target_pairs={{0,1},{1,0},{2,3},{3,2},{4,5},{5,4},{6,7},{7,6},{8,9},{9,8},{10,11... | collective-permute-start | bytes 786440 | tf_op jit(solution)/shard_map/ppermute | solution.py:54
  61.8 8.2 %collective-permute-start.25 = (bf16[128,1024]{1,0:T(8,128)(2,1)S(1)}, bf16[128,1024]{1,0:T(8,128)(2,1)S(1)}, u32[]{:S(2)}, u32[]{:S(2)}) collective-permute-start(bf16[128,1024]{1,0:T(8,128)(2,1)S(1)} %get-tuple-element.32), channel_id=1, source_target_pairs={{0,2},{1,7},{2,4},{3,1},{4,6},{5,3},{6,0},{7,5},{8,10},{9,15},{10,... | collective-permute-start | bytes 786440 | tf_op jit(solution)/shard_map/ppermute | solution.py:48
  64.7 7.1 %collective-permute-start.26 = (bf16[128,1024]{1,0:T(8,128)(2,1)S(1)}, bf16[128,1024]{1,0:T(8,128)(2,1)S(1)}, u32[]{:S(2)}, u32[]{:S(2)}) collective-permute-start(bf16[128,1024]{1,0:T(8,128)(2,1)S(1)} %get-tuple-element.33), channel_id=1, source_target_pairs={{0,6},{1,3},{2,0},{3,5},{4,2},{5,7},{6,4},{7,1},{8,14},{9,11},{10,... | collective-permute-start | bytes 786440 | tf_op jit(solution)/shard_map/ppermute | solution.py:48
  65.4 12.0 %collective-permute-start.28 = (bf16[128,1024]{1,0:T(8,128)(2,1)S(1)}, bf16[128,1024]{1,0:T(8,128)(2,1)S(1)}, u32[]{:S(2)}, u32[]{:S(2)}) collective-permute-start(bf16[128,1024]{1,0:T(8,128)(2,1)S(1)} %get-tuple-element.35), channel_id=1, source_target_pairs={{0,6},{1,3},{2,0},{3,5},{4,2},{5,7},{6,4},{7,1},{8,14},{9,11},{10,... | collective-permute-start | bytes 786440 | tf_op jit(solution)/shard_map/ppermute | solution.py:48
  65.5 11.9 %collective-permute-start.30 = (bf16[128,1024]{1,0:T(8,128)(2,1)S(1)}, bf16[128,1024]{1,0:T(8,128)(2,1)S(1)}, u32[]{:S(2)}, u32[]{:S(2)}) collective-permute-start(bf16[128,1024]{1,0:T(8,128)(2,1)S(1)} %get-tuple-element.37), channel_id=1, source_target_pairs={{0,2},{1,7},{2,4},{3,1},{4,6},{5,3},{6,0},{7,5},{8,10},{9,15},{10,... | collective-permute-start | bytes 786440 | tf_op jit(solution)/shard_map/ppermute | solution.py:48
  72.6 19.9 %copy-start.1 = (f32[1024]{0:T(1024)S(1)}, f32[1024]{0:T(1024)}, u32[]{:S(2)}) copy-start(f32[1024]{0:T(1024)} %param.12) | copy-start | bytes 12292
  72.6 8.6 %collective-permute-start.27 = (bf16[128,1024]{1,0:T(8,128)(2,1)S(1)}, bf16[128,1024]{1,0:T(8,128)(2,1)S(1)}, u32[]{:S(2)}, u32[]{:S(2)}) collective-permute-start(bf16[128,1024]{1,0:T(8,128)(2,1)S(1)} %get-tuple-element.34), channel_id=1, source_target_pairs={{0,2},{1,7},{2,4},{3,1},{4,6},{5,3},{6,0},{7,5},{8,10},{9,15},{10,... | collective-permute-start | bytes 786440 | tf_op jit(solution)/shard_map/ppermute | solution.py:48
  74.2 8.8 %collective-permute-start.29 = (bf16[128,1024]{1,0:T(8,128)(2,1)S(1)}, bf16[128,1024]{1,0:T(8,128)(2,1)S(1)}, u32[]{:S(2)}, u32[]{:S(2)}) collective-permute-start(bf16[128,1024]{1,0:T(8,128)(2,1)S(1)} %get-tuple-element.36), channel_id=1, source_target_pairs={{0,6},{1,3},{2,0},{3,5},{4,2},{5,7},{6,4},{7,1},{8,14},{9,11},{10,... | collective-permute-start | bytes 786440 | tf_op jit(solution)/shard_map/ppermute | solution.py:48
  (2 other events, 18.2 us)

commit v3 on v2

--- a/solution.py
+++ b/solution.py
@@ -76,7 +76,7 @@
         out_specs=pl.BlockSpec(memory_space=pltpu.VMEM),
         compiler_params=pltpu.CompilerParams(vmem_limit_bytes=4 << 20),
         name="choose",
-    )(*ancestors, tile_of_slot.reshape(1, TILES))
+    )(*ancestors, tile_of_slot)
 
 
 def select(chosen, arrays, steps):
@@ -126,13 +126,15 @@
     return arrays, theirs
 
 
-def pick(keys_values):
-    def kernel(all_ref, block_ref, half_ref, sems):
+def pick(keys_values, ancestors, tile_of_slot):
+    def kernel(all_ref, anc_hbm, tiles_hbm, block_ref, half_ref, anc_ref, tiles_ref, sems):
         y, c = lax.axis_index("y"), lax.axis_index("c")
         head = all_ref.at[:, :, pl.ds(pl.multiple_of(y * HEAD, HEAD), HEAD)]
         copies = [
             pltpu.make_async_copy(head, block_ref, sems.at[0]),
             pltpu.make_async_copy(head.at[c], half_ref, sems.at[1]),
+            pltpu.make_async_copy(anc_hbm, anc_ref, sems.at[2]),
+            pltpu.make_async_copy(tiles_hbm, tiles_ref, sems.at[3]),
         ]
         for copy in copies:
             copy.start()
@@ -144,13 +146,20 @@
         out_shape=[
             pltpu.VMEM((2, 256, HEAD), jnp.bfloat16),
             pltpu.VMEM((256, HEAD), jnp.bfloat16),
+            pltpu.VMEM((2, ANC), jnp.int32),
+            pltpu.VMEM((1, TILES), jnp.int32),
         ],
-        in_specs=[pl.BlockSpec(memory_space=pltpu.HBM)],
-        out_specs=[pl.BlockSpec(memory_space=pltpu.VMEM)] * 2,
-        scratch_shapes=[pltpu.SemaphoreType.DMA((2,))],
+        in_specs=[pl.BlockSpec(memory_space=pltpu.HBM)] * 3,
+        out_specs=[pl.BlockSpec(memory_space=pltpu.VMEM)] * 4,
+        scratch_shapes=[pltpu.SemaphoreType.DMA((4,))],
         compiler_params=pltpu.CompilerParams(vmem_limit_bytes=4 << 20),
         name="pick",
-    )(pltpu.with_memory_space_constraint(keys_values, pltpu.HBM))
+    )(
+        *(
+            pltpu.with_memory_space_constraint(array, pltpu.HBM)
+            for array in (keys_values, ancestors, tile_of_slot.reshape(1, TILES))
+        )
+    )
 
 
 def spot(refs, steps, hops, part):
@@ -167,8 +176,9 @@
     keys_total = (ANC + 1) * TILE
     count = len(mine)
 
-    def kernel(ancestors_hbm, tile_of_slot_hbm, query_hbm, *rest):
-        weight_refs, own_ref, rest = rest[:2], rest[2], rest[3:]
+    def kernel(query_hbm, *rest):
+        weight_refs, rest = rest[:2], rest[2:]
+        (ancestors_vmem, tile_of_slot_vmem, own_ref), rest = rest[:3], rest[3:]
         mine_refs, theirs_refs = rest[:count], rest[count : 2 * count]
         out_ref, *loaded_refs = rest[2 * count : 2 * count + 3]
         keys, values, scores, weights, bias, query_ref = rest[2 * count + 3 : 2 * count + 9]
@@ -176,8 +186,8 @@
         z, x, y, c = (lax.axis_index(name) for name in AXES)
         sign = 1 - 2 * c
         copies = [
-            pltpu.make_async_copy(ancestors_hbm, ancestors_ref, sems.at[0]),
-            pltpu.make_async_copy(tile_of_slot_hbm, tile_of_slot_ref, sems.at[1]),
+            pltpu.make_async_copy(ancestors_vmem, ancestors_ref, sems.at[0]),
+            pltpu.make_async_copy(tile_of_slot_vmem, tile_of_slot_ref, sems.at[1]),
             pltpu.make_async_copy(query_hbm, query_ref, sems.at[2]),
         ]
         for copy in copies:
@@ -196,7 +206,7 @@
         for copy in copies[:2]:
             copy.wait()
         for s in range(TILES):
-            slot_of[tile_of_slot_ref[s]] = s
+            slot_of[tile_of_slot_ref[0, s]] = s
         for t in range(2):
             start = t * keys_total
             keys[start : start + TILE] = own_ref[t * TILE : (t + 1) * TILE]
@@ -319,8 +329,8 @@
             pltpu.VMEM((NY, 512, 1024), jnp.bfloat16),
             pltpu.VMEM((NY, 512, 1024), jnp.bfloat16),
         ],
-        in_specs=[pl.BlockSpec(memory_space=pltpu.HBM)] * 5
-        + [pl.BlockSpec(memory_space=pltpu.VMEM)] * (1 + 2 * count),
+        in_specs=[pl.BlockSpec(memory_space=pltpu.HBM)] * 3
+        + [pl.BlockSpec(memory_space=pltpu.VMEM)] * (3 + 2 * count),
         out_specs=[pl.BlockSpec(memory_space=pltpu.VMEM)] * 3,
         scratch_shapes=[
             pltpu.VMEM((2 * keys_total, HEAD), jnp.bfloat16),
@@ -330,7 +340,7 @@
             pltpu.VMEM((2, 8, keys_total), jnp.float32),
             pltpu.VMEM((2 * TILE, GROUP * HEAD), jnp.bfloat16),
             pltpu.SMEM((2, ANC), jnp.int32),
-            pltpu.SMEM((TILES,), jnp.int32),
+            pltpu.SMEM((1, TILES), jnp.int32),
             pltpu.SMEM((TILES,), jnp.int32),
             pltpu.SMEM((2 * ANC,), jnp.int32),
             pltpu.SemaphoreType.DMA((4,)),
@@ -340,8 +350,10 @@
     )(
         *(
             pltpu.with_memory_space_constraint(array, pltpu.HBM)
-            for array in (ancestors, tile_of_slot, query, weight, weight_other)
+            for array in (query, weight, weight_other)
         ),
+        ancestors,
+        tile_of_slot,
         own,
         *mine,
         *theirs,
@@ -463,22 +475,24 @@
 
 
 def layer(query, keys_values, ancestors, tile_of_slot, residual, norm_gain, out_weight):
-    own, own_half = pick(keys_values)
+    own, own_half, anc_here, tiles_here = pick(keys_values, ancestors, tile_of_slot)
     own = own.reshape(BLOCK, HEAD)
     weight_other = other_core(out_weight)
-    mine, theirs = gather_pairs(own, own_half, ancestors, tile_of_slot)
+    mine, theirs = gather_pairs(own, own_half, ancestors, tiles_here)
     attended, *weights = attend(
-        query, own, mine, theirs, ancestors, tile_of_slot, out_weight, weight_other
+        query, own, mine, theirs, anc_here, tiles_here, out_weight, weight_other
     )
     args = (attended, other_core(attended), *weights)
-    across0, across1 = project(*args, [(2, 0), (2, 1)])
+    (across0,) = project(*args, [(2, 0)])
     relay_ahead = along_y(across0, 1)
+    (across1,) = project(*args, [(2, 1)])
     relay_back = along_y(across1, -1)
     direct1, direct0 = project(*args, [(1, 1), (3, 0)])
     from_back1 = along_y(direct1, 1)
     from_ahead0 = along_y(direct0, -1)
-    joined0, joined1 = project(*args, [(1, 0), (3, 1)], (relay_ahead, relay_back))
+    (joined0,) = project(*args, [(1, 0)], (relay_ahead,))
     from_back0 = along_y(joined0, 1)
+    (joined1,) = project(*args, [(3, 1)], (relay_back,))
     from_ahead1 = along_y(joined1, -1)
     (here,) = project(*args, [(0, None)], (), jnp.float32)
     hidden, sums = finish(here, from_back0, from_ahead0, from_ahead1, from_back1, residual)

time: 93.8 us -> 93.5 us (level)
  waiting for transfers between devices: 33 us -> 30.3 us
  starting transfers between devices: 39.1 us -> 41.8 us
    ppermute x6, waiting for transfers between devices: 11.4 us -> 8.8 us  [along_y(): lax.ppermute(array, AXES, permutation(lambda z, x, y, c: (z, x, y + hops...]
    ppermute x6, starting transfers between devices: 7.61 us -> 9.57 us  [along_y(): lax.ppermute(array, AXES, permutation(lambda z, x, y, c: (z, x, y + hops...]
    ppermute x12, starting transfers between devices: 10.8 us -> 12.7 us  [other_core(): lax.ppermute(array, AXES, permutation(lambda z, x, y, c: (z, x, y, c + 1)))]
    ppermute x9, starting transfers between devices: 11.2 us -> 10.1 us  [along_x(): lax.ppermute(array, AXES, permutation(lambda z, x, y, c: (z, x + hops * (...]
    pallas_call x4 -> x6, Pallas kernels: 2.86 us -> 3.24 us  [project(): pl.pallas_call(kernel, out_shape=[jax.ShapeDtypeStruct((rows, 1024), dtyp...]
  transfers between devices with their start and end apart: 31 -> 31, of which waited for: 15 -> 14; matrix products, arithmetic and copies ran while one was open for 0% -> 0% of each run, Pallas kernels for 4% -> 4%
where the time goes in v3:
time: 93.5 us; the launch traced here: 93.3 us
  starting transfers between devices  41.8 us (45%)
  waiting for transfers between devices  30.3 us (32%)
  Pallas kernels  11.5 us (12%)
  blocking collectives  8.79 us (9%)
  between operations  0.99 us (1%)
    ppermute x9, waiting for transfers between devices, along_x(): lax.ppermute(array, AXES, permutation(lambda z, x, y, c: (z, x + hops * (...  15.3 us
    ppermute x12, starting transfers between devices, other_core(): lax.ppermute(array, AXES, permutation(lambda z, x, y, c: (z, x, y, c + 1)))  12.7 us
    ppermute x9, starting transfers between devices, along_x(): lax.ppermute(array, AXES, permutation(lambda z, x, y, c: (z, x + hops * (...  10.1 us
    ppermute x6, starting transfers between devices, along_y(): lax.ppermute(array, AXES, permutation(lambda z, x, y, c: (z, x, y + hops...  9.57 us
    ppermute x4, starting transfers between devices, along_z(): lax.ppermute(array, AXES, permutation(lambda z, x, y, c: (z + hops * (1 -...  9.39 us
    ppermute x6, waiting for transfers between devices, along_y(): lax.ppermute(array, AXES, permutation(lambda z, x, y, c: (z, x, y + hops...  8.8 us
    all_to_all x1, blocking collectives, layer(): sums = lax.all_to_all(sums, ('y', 'c'), 0, 0, tiled=True)  8.79 us
    pallas_call x1, Pallas kernels, attend(): pl.pallas_call(kernel, out_shape=[pltpu.VMEM((2 * TILE, GROUP * HEAD), jn...  5.24 us
  transfers between devices with their start and end apart: 31, of which 14 were waited for; matrix products, arithmetic and copies ran while one was open for 0% of the time, Pallas kernels for 4%

profile of v3, /device:TPU:1, one launch (start us, length us, event | category | flops | bytes accessed | tf_op | source)
XLA Modules:
  0.0 93.3 jit_solution(17974635854678624539)
XLA Ops:
  0.6 3.3 %collective-permute-start = (bf16[512,8192]{1,0:T(8,128)(2,1)}, bf16[512,8192]{1,0:T(8,128)(2,1)}, u32[]{:S(2)}, u32[]{:S(2)}) collective-permute-start(bf16[512,8192]{1,0:T(8,128)(2,1)} %rest_0_.1), channel_id=1, source_target_pairs={{0,1},{1,0},{2,3},{3,2},{4,5},{5,4},{6,7},{7,6},{8,9},{9,8},{10,11... | collective-permute-start | bytes 25165832 | tf_op jit(solution)/shard_map/ppermute | solution.py:54
  3.9 1.0 %pick.1 = (bf16[2,256,128]{2,1,0:T(8,128)(2,1)S(1)}, bf16[256,128]{1,0:T(8,128)(2,1)S(1)}, s32[2,12]{1,0:T(2,128)S(1)}, s32[1,64]{1,0:T(1,128)S(1)}) custom-call(bf16[2,256,512]{2,1,0:T(8,128)(2,1)} %all_ref.1, s32[2,12]{1,0:T(2,128)} %anc_hbm.1, s32[1,64]{1,0:T(1,128)} %bitcast.7), custom_call_target="tpu_custom_call" | custom-call | tf_op jit(solution)/shard_map/pick/pallas_call | solution.py:144
  4.9 4.4 %collective-permute-start.2 = (bf16[512,128]{1,0:T(8,128)(2,1)S(1)}, bf16[512,128]{1,0:T(8,128)(2,1)S(1)}, u32[]{:S(2)}, u32[]{:S(2)}) collective-permute-start(bf16[512,128]{1,0:T(8,128)(2,1)S(1)} %bitcast.3), channel_id=1, source_target_pairs={{0,64},{1,193},{2,66},{3,195},{4,68},{5,197},{6,70},{7,199},{8,72}... | collective-permute-start | bytes 393224 | tf_op jit(solution)/shard_map/ppermute | solution.py:36
  10.0 2.6 %collective-permute-done.2.refs_2_.rest_6_ = bf16[512,128]{1,0:T(8,128)(2,1)S(1)} collective-permute-done((bf16[512,128]{1,0:T(8,128)(2,1)S(1)}, bf16[512,128]{1,0:T(8,128)(2,1)S(1)}, u32[]{:S(2)}, u32[]{:S(2)}) %collective-permute-start.2) | collective-permute-done | bytes 131104 | tf_op jit(solution)/shard_map/ppermute | solution.py:36
  12.6 4.0 %collective-permute-start.4 = (bf16[256,128]{1,0:T(8,128)(2,1)S(1)}, bf16[256,128]{1,0:T(8,128)(2,1)S(1)}, u32[]{:S(2)}, u32[]{:S(2)}) collective-permute-start(bf16[256,128]{1,0:T(8,128)(2,1)S(1)} %constant_dynamic-slice_fusion), channel_id=1, source_target_pairs={{0,64},{1,193},{2,66},{3,195},{4,68},{5,197},{6,70},{7,199},{8,72}... | collective-permute-start | bytes 196616 | tf_op jit(solution)/shard_map/ppermute | solution.py:36
  16.9 1.1 %collective-permute-done.4.refs_1_.rest_8_ = bf16[256,128]{1,0:T(8,128)(2,1)S(1)} collective-permute-done((bf16[256,128]{1,0:T(8,128)(2,1)S(1)}, bf16[256,128]{1,0:T(8,128)(2,1)S(1)}, u32[]{:S(2)}, u32[]{:S(2)}) %collective-permute-start.4) | collective-permute-done | bytes 65568 | tf_op jit(solution)/shard_map/ppermute | solution.py:36
  17.9 1.1 %collective-permute-start.17 = (bf16[256,128]{1,0:T(8,128)(2,1)S(1)}, bf16[256,128]{1,0:T(8,128)(2,1)S(1)}, u32[]{:S(2)}, u32[]{:S(2)}) collective-permute-start(bf16[256,128]{1,0:T(8,128)(2,1)S(1)} %collective-permute-done.4.refs_1_.rest_8_), channel_id=1, source_target_pairs={{0,1},{1,0},{2,3},{3,2},{4,5},{5,4},{6,7},{7,6},{8,9},{9,8},{10,11... | collective-permute-start | bytes 196616 | tf_op jit(solution)/shard_map/ppermute | solution.py:54
  19.0 1.2 %collective-permute-start.5 = (s32[2,12]{1,0:T(2,128)}, s32[2,12]{1,0:T(2,128)S(1)}, u32[]{:S(2)}, u32[]{:S(2)}) collective-permute-start(s32[2,12]{1,0:T(2,128)} %anc_hbm.1), channel_id=1, source_target_pairs={{0,24},{1,9},{2,26},{3,11},{4,28},{5,13},{6,30},{7,15},{8,0},{9,17... | collective-permute-start | bytes 296 | tf_op jit(solution)/shard_map/ppermute | solution.py:42
  20.2 2.9 %collective-permute-done.5.first_ref = s32[2,12]{1,0:T(2,128)S(1)} collective-permute-done((s32[2,12]{1,0:T(2,128)}, s32[2,12]{1,0:T(2,128)S(1)}, u32[]{:S(2)}, u32[]{:S(2)}) %collective-permute-start.5) | collective-permute-done | bytes 128 | tf_op jit(solution)/shard_map/ppermute | solution.py:42
  23.2 1.2 %collective-permute-start.7 = (s32[2,12]{1,0:T(2,128)}, s32[2,12]{1,0:T(2,128)S(1)}, u32[]{:S(2)}, u32[]{:S(2)}) collective-permute-start(s32[2,12]{1,0:T(2,128)} %anc_hbm.1), channel_id=1, source_target_pairs={{0,16},{1,17},{2,18},{3,19},{4,20},{5,21},{6,22},{7,23},{8,24},{9,... | collective-permute-start | bytes 296 | tf_op jit(solution)/shard_map/ppermute | solution.py:42
  24.4 2.9 %collective-permute-done.7.third_ref = s32[2,12]{1,0:T(2,128)S(1)} collective-permute-done((s32[2,12]{1,0:T(2,128)}, s32[2,12]{1,0:T(2,128)S(1)}, u32[]{:S(2)}, u32[]{:S(2)}) %collective-permute-start.7) | collective-permute-done | bytes 128 | tf_op jit(solution)/shard_map/ppermute | solution.py:42
  27.3 1.0 %collective-permute-start.6 = (s32[2,12]{1,0:T(2,128)}, s32[2,12]{1,0:T(2,128)S(1)}, u32[]{:S(2)}, u32[]{:S(2)}) collective-permute-start(s32[2,12]{1,0:T(2,128)} %anc_hbm.1), channel_id=1, source_target_pairs={{0,8},{1,25},{2,10},{3,27},{4,12},{5,29},{6,14},{7,31},{8,16},{9,1... | collective-permute-start | bytes 296 | tf_op jit(solution)/shard_map/ppermute | solution.py:42
  28.3 1.7 %collective-permute-done.6.second_ref = s32[2,12]{1,0:T(2,128)S(1)} collective-permute-done((s32[2,12]{1,0:T(2,128)}, s32[2,12]{1,0:T(2,128)S(1)}, u32[]{:S(2)}, u32[]{:S(2)}) %collective-permute-start.6) | collective-permute-done | bytes 128 | tf_op jit(solution)/shard_map/ppermute | solution.py:42
  29.9 3.9 %collective-permute-start.14 = (bf16[512,128]{1,0:T(8,128)(2,1)S(1)}, bf16[512,128]{1,0:T(8,128)(2,1)S(1)}, u32[]{:S(2)}, u32[]{:S(2)}) collective-permute-start(bf16[512,128]{1,0:T(8,128)(2,1)S(1)} %collective-permute-done.1.refs_1_.rest_5_), channel_id=1, source_target_pairs={{0,1},{1,0},{2,3},{3,2},{4,5},{5,4},{6,7},{7,6},{8,9},{9,8},{10,11... | collective-permute-start | bytes 393224 | tf_op jit(solution)/shard_map/ppermute | solution.py:54
  34.2 1.0 %collective-permute-start.8 = (bf16[640,128]{1,0:T(8,128)(2,1)S(1)}, bf16[640,128]{1,0:T(8,128)(2,1)S(1)}, u32[]{:S(2)}, u32[]{:S(2)}) collective-permute-start(bf16[640,128]{1,0:T(8,128)(2,1)S(1)} %get-tuple-element.23), channel_id=1, source_target_pairs={{0,16},{1,17},{2,18},{3,19},{4,20},{5,21},{6,22},{7,23},{8,24},{9,... | collective-permute-start | bytes 491528 | tf_op jit(solution)/shard_map/ppermute | solution.py:42
  35.2 1.4 %collective-permute-start.9 = (bf16[640,128]{1,0:T(8,128)(2,1)S(1)}, bf16[640,128]{1,0:T(8,128)(2,1)S(1)}, u32[]{:S(2)}, u32[]{:S(2)}) collective-permute-start(bf16[640,128]{1,0:T(8,128)(2,1)S(1)} %get-tuple-element.24), channel_id=1, source_target_pairs={{0,24},{1,9},{2,26},{3,11},{4,28},{5,13},{6,30},{7,15},{8,0},{9,17... | collective-permute-start | bytes 491528 | tf_op jit(solution)/shard_map/ppermute | solution.py:42
  36.6 1.3 %collective-permute-start.10 = (bf16[640,128]{1,0:T(8,128)(2,1)S(1)}, bf16[640,128]{1,0:T(8,128)(2,1)S(1)}, u32[]{:S(2)}, u32[]{:S(2)}) collective-permute-start(bf16[640,128]{1,0:T(8,128)(2,1)S(1)} %get-tuple-element.25), channel_id=1, source_target_pairs={{0,8},{1,25},{2,10},{3,27},{4,12},{5,29},{6,14},{7,31},{8,16},{9,1... | collective-permute-start | bytes 491528 | tf_op jit(solution)/shard_map/ppermute | solution.py:42
  38.9 2.7 %collective-permute-done.8.rest_9_ = bf16[640,128]{1,0:T(8,128)(2,1)S(1)} collective-permute-done((bf16[640,128]{1,0:T(8,128)(2,1)S(1)}, bf16[640,128]{1,0:T(8,128)(2,1)S(1)}, u32[]{:S(2)}, u32[]{:S(2)}) %collective-permute-start.8) | collective-permute-done | bytes 163872 | tf_op jit(solution)/shard_map/ppermute | solution.py:42
  41.6 4.2 %collective-permute-done.9.rest_10_ = bf16[640,128]{1,0:T(8,128)(2,1)S(1)} collective-permute-done((bf16[640,128]{1,0:T(8,128)(2,1)S(1)}, bf16[640,128]{1,0:T(8,128)(2,1)S(1)}, u32[]{:S(2)}, u32[]{:S(2)}) %collective-permute-start.9) | collective-permute-done | bytes 163872 | tf_op jit(solution)/shard_map/ppermute | solution.py:42
  45.8 2.1 %collective-permute-start.13 = (bf16[384,128]{1,0:T(8,128)(2,1)S(1)}, bf16[384,128]{1,0:T(8,128)(2,1)S(1)}, u32[]{:S(2)}, u32[]{:S(2)}) collective-permute-start(bf16[384,128]{1,0:T(8,128)(2,1)S(1)} %get-tuple-element.28), channel_id=1, source_target_pairs={{0,8},{1,25},{2,10},{3,27},{4,12},{5,29},{6,14},{7,31},{8,16},{9,1... | collective-permute-start | bytes 294920 | tf_op jit(solution)/shard_map/ppermute | solution.py:42
  49.5 2.8 %collective-permute-start.18 = (bf16[640,128]{1,0:T(8,128)(2,1)S(1)}, bf16[640,128]{1,0:T(8,128)(2,1)S(1)}, u32[]{:S(2)}, u32[]{:S(2)}) collective-permute-start(bf16[640,128]{1,0:T(8,128)(2,1)S(1)} %collective-permute-done.8.rest_9_), channel_id=1, source_target_pairs={{0,1},{1,0},{2,3},{3,2},{4,5},{5,4},{6,7},{7,6},{8,9},{9,8},{10,11... | collective-permute-start | bytes 491528 | tf_op jit(solution)/shard_map/ppermute | solution.py:54
  52.9 1.2 %collective-permute-done.23.rest_24_ = bf16[384,128]{1,0:T(8,128)(2,1)S(1)} collective-permute-done((bf16[384,128]{1,0:T(8,128)(2,1)S(1)}, bf16[384,128]{1,0:T(8,128)(2,1)S(1)}, u32[]{:S(2)}, u32[]{:S(2)}) %collective-permute-start.23) | collective-permute-done | bytes 98336 | tf_op jit(solution)/shard_map/ppermute | solution.py:54
  54.1 5.2 %attend.1 = (bf16[256,512]{1,0:T(8,128)(2,1)S(1)}, bf16[4,512,1024]{2,1,0:T(8,128)(2,1)S(1)}, bf16[4,512,1024]{2,1,0:T(8,128)(2,1)S(1)}) custom-call(bf16[256,512]{1,0:T(8,128)(2,1)} %query_hbm.1, bf16[512,8192]{1,0:T(8,128)(2,1)} %rest_0_.1, bf16[512,8192]{1,0:T(8,128)(2,1)} %collective-permute-done.rest_1_, s32[2,12]{1,0:T(2,128)S(1)} %get-tuple-element.19.rest_2_, ...), custom_call_target="tpu_custom_call" | custom-call | tf_op jit(solution)/shard_map/attend/pallas_call | solution.py:325
  59.7 1.3 %collective-permute-done.24.b_ref = bf16[256,512]{1,0:T(8,128)(2,1)S(1)} collective-permute-done((bf16[256,512]{1,0:T(8,128)(2,1)S(1)}, bf16[256,512]{1,0:T(8,128)(2,1)S(1)}, u32[]{:S(2)}, u32[]{:S(2)}) %collective-permute-start.24) | collective-permute-done | bytes 262176 | tf_op jit(solution)/shard_map/ppermute | solution.py:54
  61.5 2.9 %collective-permute-start.25 = (bf16[128,1024]{1,0:T(8,128)(2,1)S(1)}, bf16[128,1024]{1,0:T(8,128)(2,1)S(1)}, u32[]{:S(2)}, u32[]{:S(2)}) collective-permute-start(bf16[128,1024]{1,0:T(8,128)(2,1)S(1)} %project.7), channel_id=1, source_target_pairs={{0,2},{1,7},{2,4},{3,1},{4,6},{5,3},{6,0},{7,5},{8,10},{9,15},{10,... | collective-permute-start | bytes 786440 | tf_op jit(solution)/shard_map/ppermute | solution.py:48
  65.7 2.7 %collective-permute-start.30 = (bf16[128,1024]{1,0:T(8,128)(2,1)S(1)}, bf16[128,1024]{1,0:T(8,128)(2,1)S(1)}, u32[]{:S(2)}, u32[]{:S(2)}) collective-permute-start(bf16[128,1024]{1,0:T(8,128)(2,1)S(1)} %get-tuple-element.33), channel_id=1, source_target_pairs={{0,2},{1,7},{2,4},{3,1},{4,6},{5,3},{6,0},{7,5},{8,10},{9,15},{10,... | collective-permute-start | bytes 786440 | tf_op jit(solution)/shard_map/ppermute | solution.py:48
  69.6 3.7 %collective-permute-start.26 = (bf16[128,1024]{1,0:T(8,128)(2,1)S(1)}, bf16[128,1024]{1,0:T(8,128)(2,1)S(1)}, u32[]{:S(2)}, u32[]{:S(2)}) collective-permute-start(bf16[128,1024]{1,0:T(8,128)(2,1)S(1)} %project.8), channel_id=1, source_target_pairs={{0,2},{1,7},{2,4},{3,1},{4,6},{5,3},{6,0},{7,5},{8,10},{9,15},{10,... | collective-permute-start | bytes 786440 | tf_op jit(solution)/shard_map/ppermute | solution.py:48
  74.6 2.0 %collective-permute-done.27.a0_ref = bf16[128,1024]{1,0:T(8,128)(2,1)S(1)} collective-permute-done((bf16[128,1024]{1,0:T(8,128)(2,1)S(1)}, bf16[128,1024]{1,0:T(8,128)(2,1)S(1)}, u32[]{:S(2)}, u32[]{:S(2)}) %collective-permute-start.27) | collective-permute-done | bytes 262176 | tf_op jit(solution)/shard_map/ppermute | solution.py:48
  76.6 3.8 %collective-permute-done.26.b0_ref = bf16[128,1024]{1,0:T(8,128)(2,1)S(1)} collective-permute-done((bf16[128,1024]{1,0:T(8,128)(2,1)S(1)}, bf16[128,1024]{1,0:T(8,128)(2,1)S(1)}, u32[]{:S(2)}, u32[]{:S(2)}) %collective-permute-start.26) | collective-permute-done | bytes 262176 | tf_op jit(solution)/shard_map/ppermute | solution.py:48
  80.4 2.4 %collective-permute-done.29.a1_ref = bf16[128,1024]{1,0:T(8,128)(2,1)S(1)} collective-permute-done((bf16[128,1024]{1,0:T(8,128)(2,1)S(1)}, bf16[128,1024]{1,0:T(8,128)(2,1)S(1)}, u32[]{:S(2)}, u32[]{:S(2)}) %collective-permute-start.29) | collective-permute-done | bytes 262176 | tf_op jit(solution)/shard_map/ppermute | solution.py:48
  83.3 8.8 %all_to_all.5.sums_ref = f32[8,1,256]{2,1,0:T(1,128)S(1)} all-to-all(f32[8,1,256]{2,1,0:T(1,128)S(1)} %get-tuple-element.35), channel_id=1, replica_groups=mesh['z'=8,'x'=4,'y'=4,'c'=2] {'y','c'}, dimensions={0} | all-to-all | bytes 16384 | tf_op jit(solution)/shard_map/all_to_all | solution.py:499
  92.1 1.0 %normalize.1 = (bf16[256,1024]{1,0:T(8,128)(2,1)}, bf16[256,1024]{1,0:T(8,128)(2,1)}) custom-call(bf16[256,1024]{1,0:T(8,128)(2,1)S(1)} %get-tuple-element.34.hidden_ref, f32[8,1,256]{2,1,0:T(1,128)S(1)} %all_to_all.5.sums_ref, f32[1,1024]{1,0:T(1,128)S(1)} %bitcast.6), custom_call_target="tpu_custom_call" | custom-call | tf_op jit(solution)/shard_map/normalize/pallas_call | solution.py:463
  (49 shorter events, 9.7 us)
Async XLA Ops:
  0.6 53.5 %collective-permute-start = (bf16[512,8192]{1,0:T(8,128)(2,1)}, bf16[512,8192]{1,0:T(8,128)(2,1)}, u32[]{:S(2)}, u32[]{:S(2)}) collective-permute-start(bf16[512,8192]{1,0:T(8,128)(2,1)} %rest_0_.1), channel_id=1, source_target_pairs={{0,1},{1,0},{2,3},{3,2},{4,5},{5,4},{6,7},{7,6},{8,9},{9,8},{10,11... | collective-permute-start | bytes 25165832 | tf_op jit(solution)/shard_map/ppermute | solution.py:54
  4.9 7.7 %collective-permute-start.2 = (bf16[512,128]{1,0:T(8,128)(2,1)S(1)}, bf16[512,128]{1,0:T(8,128)(2,1)S(1)}, u32[]{:S(2)}, u32[]{:S(2)}) collective-permute-start(bf16[512,128]{1,0:T(8,128)(2,1)S(1)} %bitcast.3), channel_id=1, source_target_pairs={{0,64},{1,193},{2,66},{3,195},{4,68},{5,197},{6,70},{7,199},{8,72}... | collective-permute-start | bytes 393224 | tf_op jit(solution)/shard_map/ppermute | solution.py:36
  9.3 7.3 %collective-permute-start.1 = (bf16[512,128]{1,0:T(8,128)(2,1)S(1)}, bf16[512,128]{1,0:T(8,128)(2,1)S(1)}, u32[]{:S(2)}, u32[]{:S(2)}) collective-permute-start(bf16[512,128]{1,0:T(8,128)(2,1)S(1)} %bitcast.4), channel_id=1, source_target_pairs={{0,32},{1,225},{2,34},{3,227},{4,36},{5,229},{6,38},{7,231},{8,40}... | collective-permute-start | bytes 393224 | tf_op jit(solution)/shard_map/ppermute | solution.py:36
  12.6 5.3 %collective-permute-start.4 = (bf16[256,128]{1,0:T(8,128)(2,1)S(1)}, bf16[256,128]{1,0:T(8,128)(2,1)S(1)}, u32[]{:S(2)}, u32[]{:S(2)}) collective-permute-start(bf16[256,128]{1,0:T(8,128)(2,1)S(1)} %constant_dynamic-slice_fusion), channel_id=1, source_target_pairs={{0,64},{1,193},{2,66},{3,195},{4,68},{5,197},{6,70},{7,199},{8,72}... | collective-permute-start | bytes 196616 | tf_op jit(solution)/shard_map/ppermute | solution.py:36
  16.6 18.6 %collective-permute-start.15 = (bf16[512,128]{1,0:T(8,128)(2,1)S(1)}, bf16[512,128]{1,0:T(8,128)(2,1)S(1)}, u32[]{:S(2)}, u32[]{:S(2)}) collective-permute-start(bf16[512,128]{1,0:T(8,128)(2,1)S(1)} %collective-permute-done.2.refs_2_.rest_6_), channel_id=1, source_target_pairs={{0,1},{1,0},{2,3},{3,2},{4,5},{5,4},{6,7},{7,6},{8,9},{9,8},{10,11... | collective-permute-start | bytes 393224 | tf_op jit(solution)/shard_map/ppermute | solution.py:54
  16.6 20.0 %collective-permute-start.3 = (bf16[512,128]{1,0:T(8,128)(2,1)S(1)}, bf16[512,128]{1,0:T(8,128)(2,1)S(1)}, u32[]{:S(2)}, u32[]{:S(2)}) collective-permute-start(bf16[512,128]{1,0:T(8,128)(2,1)S(1)} %collective-permute-done.1.refs_1_.rest_5_), channel_id=1, source_target_pairs={{0,64},{1,193},{2,66},{3,195},{4,68},{5,197},{6,70},{7,199},{8,72}... | collective-permute-start | bytes 393224 | tf_op jit(solution)/shard_map/ppermute | solution.py:36
  17.9 16.2 %collective-permute-start.17 = (bf16[256,128]{1,0:T(8,128)(2,1)S(1)}, bf16[256,128]{1,0:T(8,128)(2,1)S(1)}, u32[]{:S(2)}, u32[]{:S(2)}) collective-permute-start(bf16[256,128]{1,0:T(8,128)(2,1)S(1)} %collective-permute-done.4.refs_1_.rest_8_), channel_id=1, source_target_pairs={{0,1},{1,0},{2,3},{3,2},{4,5},{5,4},{6,7},{7,6},{8,9},{9,8},{10,11... | collective-permute-start | bytes 196616 | tf_op jit(solution)/shard_map/ppermute | solution.py:54
  19.0 4.1 %collective-permute-start.5 = (s32[2,12]{1,0:T(2,128)}, s32[2,12]{1,0:T(2,128)S(1)}, u32[]{:S(2)}, u32[]{:S(2)}) collective-permute-start(s32[2,12]{1,0:T(2,128)} %anc_hbm.1), channel_id=1, source_target_pairs={{0,24},{1,9},{2,26},{3,11},{4,28},{5,13},{6,30},{7,15},{8,0},{9,17... | collective-permute-start | bytes 296 | tf_op jit(solution)/shard_map/ppermute | solution.py:42
  23.2 4.1 %collective-permute-start.7 = (s32[2,12]{1,0:T(2,128)}, s32[2,12]{1,0:T(2,128)S(1)}, u32[]{:S(2)}, u32[]{:S(2)}) collective-permute-start(s32[2,12]{1,0:T(2,128)} %anc_hbm.1), channel_id=1, source_target_pairs={{0,16},{1,17},{2,18},{3,19},{4,20},{5,21},{6,22},{7,23},{8,24},{9,... | collective-permute-start | bytes 296 | tf_op jit(solution)/shard_map/ppermute | solution.py:42
  27.3 2.6 %collective-permute-start.6 = (s32[2,12]{1,0:T(2,128)}, s32[2,12]{1,0:T(2,128)S(1)}, u32[]{:S(2)}, u32[]{:S(2)}) collective-permute-start(s32[2,12]{1,0:T(2,128)} %anc_hbm.1), channel_id=1, source_target_pairs={{0,8},{1,25},{2,10},{3,27},{4,12},{5,29},{6,14},{7,31},{8,16},{9,1... | collective-permute-start | bytes 296 | tf_op jit(solution)/shard_map/ppermute | solution.py:42
  29.9 8.1 %collective-permute-start.14 = (bf16[512,128]{1,0:T(8,128)(2,1)S(1)}, bf16[512,128]{1,0:T(8,128)(2,1)S(1)}, u32[]{:S(2)}, u32[]{:S(2)}) collective-permute-start(bf16[512,128]{1,0:T(8,128)(2,1)S(1)} %collective-permute-done.1.refs_1_.rest_5_), channel_id=1, source_target_pairs={{0,1},{1,0},{2,3},{3,2},{4,5},{5,4},{6,7},{7,6},{8,9},{9,8},{10,11... | collective-permute-start | bytes 393224 | tf_op jit(solution)/shard_map/ppermute | solution.py:54
  34.2 7.4 %collective-permute-start.8 = (bf16[640,128]{1,0:T(8,128)(2,1)S(1)}, bf16[640,128]{1,0:T(8,128)(2,1)S(1)}, u32[]{:S(2)}, u32[]{:S(2)}) collective-permute-start(bf16[640,128]{1,0:T(8,128)(2,1)S(1)} %get-tuple-element.23), channel_id=1, source_target_pairs={{0,16},{1,17},{2,18},{3,19},{4,20},{5,21},{6,22},{7,23},{8,24},{9,... | collective-permute-start | bytes 491528 | tf_op jit(solution)/shard_map/ppermute | solution.py:42
  35.2 10.5 %collective-permute-start.9 = (bf16[640,128]{1,0:T(8,128)(2,1)S(1)}, bf16[640,128]{1,0:T(8,128)(2,1)S(1)}, u32[]{:S(2)}, u32[]{:S(2)}) collective-permute-start(bf16[640,128]{1,0:T(8,128)(2,1)S(1)} %get-tuple-element.24), channel_id=1, source_target_pairs={{0,24},{1,9},{2,26},{3,11},{4,28},{5,13},{6,30},{7,15},{8,0},{9,17... | collective-permute-start | bytes 491528 | tf_op jit(solution)/shard_map/ppermute | solution.py:42
  36.6 9.2 %collective-permute-start.10 = (bf16[640,128]{1,0:T(8,128)(2,1)S(1)}, bf16[640,128]{1,0:T(8,128)(2,1)S(1)}, u32[]{:S(2)}, u32[]{:S(2)}) collective-permute-start(bf16[640,128]{1,0:T(8,128)(2,1)S(1)} %get-tuple-element.25), channel_id=1, source_target_pairs={{0,8},{1,25},{2,10},{3,27},{4,12},{5,29},{6,14},{7,31},{8,16},{9,1... | collective-permute-start | bytes 491528 | tf_op jit(solution)/shard_map/ppermute | solution.py:42
  38.0 9.9 %collective-permute-start.11 = (bf16[384,128]{1,0:T(8,128)(2,1)S(1)}, bf16[384,128]{1,0:T(8,128)(2,1)S(1)}, u32[]{:S(2)}, u32[]{:S(2)}) collective-permute-start(bf16[384,128]{1,0:T(8,128)(2,1)S(1)} %get-tuple-element.26), channel_id=1, source_target_pairs={{0,16},{1,17},{2,18},{3,19},{4,20},{5,21},{6,22},{7,23},{8,24},{9,... | collective-permute-start | bytes 294920 | tf_op jit(solution)/shard_map/ppermute | solution.py:42
  41.6 7.0 %collective-permute-start.12 = (bf16[384,128]{1,0:T(8,128)(2,1)S(1)}, bf16[384,128]{1,0:T(8,128)(2,1)S(1)}, u32[]{:S(2)}, u32[]{:S(2)}) collective-permute-start(bf16[384,128]{1,0:T(8,128)(2,1)S(1)} %get-tuple-element.27), channel_id=1, source_target_pairs={{0,24},{1,9},{2,26},{3,11},{4,28},{5,13},{6,30},{7,15},{8,0},{9,17... | collective-permute-start | bytes 294920 | tf_op jit(solution)/shard_map/ppermute | solution.py:42
  45.7 6.6 %collective-permute-start.16 = (bf16[512,128]{1,0:T(8,128)(2,1)S(1)}, bf16[512,128]{1,0:T(8,128)(2,1)S(1)}, u32[]{:S(2)}, u32[]{:S(2)}) collective-permute-start(bf16[512,128]{1,0:T(8,128)(2,1)S(1)} %collective-permute-done.3.refs_0_.rest_7_), channel_id=1, source_target_pairs={{0,1},{1,0},{2,3},{3,2},{4,5},{5,4},{6,7},{7,6},{8,9},{9,8},{10,11... | collective-permute-start | bytes 393224 | tf_op jit(solution)/shard_map/ppermute | solution.py:54
  45.8 3.7 %collective-permute-start.13 = (bf16[384,128]{1,0:T(8,128)(2,1)S(1)}, bf16[384,128]{1,0:T(8,128)(2,1)S(1)}, u32[]{:S(2)}, u32[]{:S(2)}) collective-permute-start(bf16[384,128]{1,0:T(8,128)(2,1)S(1)} %get-tuple-element.28), channel_id=1, source_target_pairs={{0,8},{1,25},{2,10},{3,27},{4,12},{5,29},{6,14},{7,31},{8,16},{9,1... | collective-permute-start | bytes 294920 | tf_op jit(solution)/shard_map/ppermute | solution.py:42
  47.9 4.4 %collective-permute-start.21 = (bf16[384,128]{1,0:T(8,128)(2,1)S(1)}, bf16[384,128]{1,0:T(8,128)(2,1)S(1)}, u32[]{:S(2)}, u32[]{:S(2)}) collective-permute-start(bf16[384,128]{1,0:T(8,128)(2,1)S(1)} %collective-permute-done.11.rest_12_), channel_id=1, source_target_pairs={{0,1},{1,0},{2,3},{3,2},{4,5},{5,4},{6,7},{7,6},{8,9},{9,8},{10,11... | collective-permute-start | bytes 294920 | tf_op jit(solution)/shard_map/ppermute | solution.py:54
  48.6 4.3 %collective-permute-start.22 = (bf16[384,128]{1,0:T(8,128)(2,1)S(1)}, bf16[384,128]{1,0:T(8,128)(2,1)S(1)}, u32[]{:S(2)}, u32[]{:S(2)}) collective-permute-start(bf16[384,128]{1,0:T(8,128)(2,1)S(1)} %collective-permute-done.12.rest_13_), channel_id=1, source_target_pairs={{0,1},{1,0},{2,3},{3,2},{4,5},{5,4},{6,7},{7,6},{8,9},{9,8},{10,11... | collective-permute-start | bytes 294920 | tf_op jit(solution)/shard_map/ppermute | solution.py:54
  49.5 4.6 %collective-permute-start.18 = (bf16[640,128]{1,0:T(8,128)(2,1)S(1)}, bf16[640,128]{1,0:T(8,128)(2,1)S(1)}, u32[]{:S(2)}, u32[]{:S(2)}) collective-permute-start(bf16[640,128]{1,0:T(8,128)(2,1)S(1)} %collective-permute-done.8.rest_9_), channel_id=1, source_target_pairs={{0,1},{1,0},{2,3},{3,2},{4,5},{5,4},{6,7},{7,6},{8,9},{9,8},{10,11... | collective-permute-start | bytes 491528 | tf_op jit(solution)/shard_map/ppermute | solution.py:54
  52.3 1.8 %collective-permute-start.19 = (bf16[640,128]{1,0:T(8,128)(2,1)S(1)}, bf16[640,128]{1,0:T(8,128)(2,1)S(1)}, u32[]{:S(2)}, u32[]{:S(2)}) collective-permute-start(bf16[640,128]{1,0:T(8,128)(2,1)S(1)} %collective-permute-done.9.rest_10_), channel_id=1, source_target_pairs={{0,1},{1,0},{2,3},{3,2},{4,5},{5,4},{6,7},{7,6},{8,9},{9,8},{10,11... | collective-permute-start | bytes 491528 | tf_op jit(solution)/shard_map/ppermute | solution.py:54
  52.3 1.8 %collective-permute-start.20 = (bf16[640,128]{1,0:T(8,128)(2,1)S(1)}, bf16[640,128]{1,0:T(8,128)(2,1)S(1)}, u32[]{:S(2)}, u32[]{:S(2)}) collective-permute-start(bf16[640,128]{1,0:T(8,128)(2,1)S(1)} %collective-permute-done.10.rest_11_), channel_id=1, source_target_pairs={{0,1},{1,0},{2,3},{3,2},{4,5},{5,4},{6,7},{7,6},{8,9},{9,8},{10,11... | collective-permute-start | bytes 491528 | tf_op jit(solution)/shard_map/ppermute | solution.py:54
  52.8 1.3 %collective-permute-start.23 = (bf16[384,128]{1,0:T(8,128)(2,1)S(1)}, bf16[384,128]{1,0:T(8,128)(2,1)S(1)}, u32[]{:S(2)}, u32[]{:S(2)}) collective-permute-start(bf16[384,128]{1,0:T(8,128)(2,1)S(1)} %collective-permute-done.13.rest_14_), channel_id=1, source_target_pairs={{0,1},{1,0},{2,3},{3,2},{4,5},{5,4},{6,7},{7,6},{8,9},{9,8},{10,11... | collective-permute-start | bytes 294920 | tf_op jit(solution)/shard_map/ppermute | solution.py:54
  59.4 1.6 %collective-permute-start.24 = (bf16[256,512]{1,0:T(8,128)(2,1)S(1)}, bf16[256,512]{1,0:T(8,128)(2,1)S(1)}, u32[]{:S(2)}, u32[]{:S(2)}) collective-permute-start(bf16[256,512]{1,0:T(8,128)(2,1)S(1)} %get-tuple-element.29.a_ref), channel_id=1, source_target_pairs={{0,1},{1,0},{2,3},{3,2},{4,5},{5,4},{6,7},{7,6},{8,9},{9,8},{10,11... | collective-permute-start | bytes 786440 | tf_op jit(solution)/shard_map/ppermute | solution.py:54
  61.5 7.6 %collective-permute-start.25 = (bf16[128,1024]{1,0:T(8,128)(2,1)S(1)}, bf16[128,1024]{1,0:T(8,128)(2,1)S(1)}, u32[]{:S(2)}, u32[]{:S(2)}) collective-permute-start(bf16[128,1024]{1,0:T(8,128)(2,1)S(1)} %project.7), channel_id=1, source_target_pairs={{0,2},{1,7},{2,4},{3,1},{4,6},{5,3},{6,0},{7,5},{8,10},{9,15},{10,... | collective-permute-start | bytes 786440 | tf_op jit(solution)/shard_map/ppermute | solution.py:48
  64.8 8.5 %collective-permute-start.28 = (bf16[128,1024]{1,0:T(8,128)(2,1)S(1)}, bf16[128,1024]{1,0:T(8,128)(2,1)S(1)}, u32[]{:S(2)}, u32[]{:S(2)}) collective-permute-start(bf16[128,1024]{1,0:T(8,128)(2,1)S(1)} %project.10), channel_id=1, source_target_pairs={{0,6},{1,3},{2,0},{3,5},{4,2},{5,7},{6,4},{7,1},{8,14},{9,11},{10,... | collective-permute-start | bytes 786440 | tf_op jit(solution)/shard_map/ppermute | solution.py:48
  65.6 10.9 %collective-permute-start.27 = (bf16[128,1024]{1,0:T(8,128)(2,1)S(1)}, bf16[128,1024]{1,0:T(8,128)(2,1)S(1)}, u32[]{:S(2)}, u32[]{:S(2)}) collective-permute-start(bf16[128,1024]{1,0:T(8,128)(2,1)S(1)} %get-tuple-element.32), channel_id=1, source_target_pairs={{0,6},{1,3},{2,0},{3,5},{4,2},{5,7},{6,4},{7,1},{8,14},{9,11},{10,... | collective-permute-start | bytes 786440 | tf_op jit(solution)/shard_map/ppermute | solution.py:48
  65.7 10.8 %collective-permute-start.30 = (bf16[128,1024]{1,0:T(8,128)(2,1)S(1)}, bf16[128,1024]{1,0:T(8,128)(2,1)S(1)}, u32[]{:S(2)}, u32[]{:S(2)}) collective-permute-start(bf16[128,1024]{1,0:T(8,128)(2,1)S(1)} %get-tuple-element.33), channel_id=1, source_target_pairs={{0,2},{1,7},{2,4},{3,1},{4,6},{5,3},{6,0},{7,5},{8,10},{9,15},{10,... | collective-permute-start | bytes 786440 | tf_op jit(solution)/shard_map/ppermute | solution.py:48
  69.6 10.8 %collective-permute-start.26 = (bf16[128,1024]{1,0:T(8,128)(2,1)S(1)}, bf16[128,1024]{1,0:T(8,128)(2,1)S(1)}, u32[]{:S(2)}, u32[]{:S(2)}) collective-permute-start(bf16[128,1024]{1,0:T(8,128)(2,1)S(1)} %project.8), channel_id=1, source_target_pairs={{0,2},{1,7},{2,4},{3,1},{4,6},{5,3},{6,0},{7,5},{8,10},{9,15},{10,... | collective-permute-start | bytes 786440 | tf_op jit(solution)/shard_map/ppermute | solution.py:48
  73.8 18.4 %copy-start.1 = (f32[1024]{0:T(1024)S(1)}, f32[1024]{0:T(1024)}, u32[]{:S(2)}) copy-start(f32[1024]{0:T(1024)} %param.12) | copy-start | bytes 12292
  73.8 8.9 %collective-permute-start.29 = (bf16[128,1024]{1,0:T(8,128)(2,1)S(1)}, bf16[128,1024]{1,0:T(8,128)(2,1)S(1)}, u32[]{:S(2)}, u32[]{:S(2)}) collective-permute-start(bf16[128,1024]{1,0:T(8,128)(2,1)S(1)} %project.11), channel_id=1, source_target_pairs={{0,6},{1,3},{2,0},{3,5},{4,2},{5,7},{6,4},{7,1},{8,14},{9,11},{10,... | collective-permute-start | bytes 786440 | tf_op jit(solution)/shard_map/ppermute | solution.py:48
  (1 other events, 13.1 us)

commit v4 on v3

--- a/solution.py
+++ b/solution.py
@@ -108,7 +108,7 @@
 
 def gather_pairs(own, own_half, ancestors, tile_of_slot):
     asked_ahead = along_x(ancestors, -1)
-    asked_back = along_x(ancestors, 1)
+    asked_back = other_core(asked_ahead)
     asked_across = along_x(ancestors, 2)
     near1 = along_z(own, 1)
     near2 = along_z(own, 2)
@@ -487,8 +487,9 @@
     relay_ahead = along_y(across0, 1)
     (across1,) = project(*args, [(2, 1)])
     relay_back = along_y(across1, -1)
-    direct1, direct0 = project(*args, [(1, 1), (3, 0)])
+    (direct1,) = project(*args, [(1, 1)])
     from_back1 = along_y(direct1, 1)
+    (direct0,) = project(*args, [(3, 0)])
     from_ahead0 = along_y(direct0, -1)
     (joined0,) = project(*args, [(1, 0)], (relay_ahead,))
     from_back0 = along_y(joined0, 1)

time: 93.5 us -> 90.6 us (0.969)
  waiting for transfers between devices: 30.3 us -> 25 us
  starting transfers between devices: 41.8 us -> 44 us
    ppermute x9 -> x8, waiting for transfers between devices: 15.3 us -> 9.42 us  [along_x(): lax.ppermute(array, AXES, permutation(lambda z, x, y, c: (z, x + hops * (...]
    ppermute x9 -> x8, starting transfers between devices: 10.1 us -> 12.8 us  [along_x(): lax.ppermute(array, AXES, permutation(lambda z, x, y, c: (z, x + hops * (...]
    ppermute x12 -> x13, waiting for transfers between devices: 2.54 us -> 3.36 us  [other_core(): lax.ppermute(array, AXES, permutation(lambda z, x, y, c: (z, x, y, c + 1)))]
    ppermute x12 -> x13, starting transfers between devices: 12.7 us -> 12.2 us  [other_core(): lax.ppermute(array, AXES, permutation(lambda z, x, y, c: (z, x, y, c + 1)))]
    pallas_call x6 -> x7, Pallas kernels: 3.24 us -> 3.41 us  [project(): pl.pallas_call(kernel, out_shape=[jax.ShapeDtypeStruct((rows, 1024), dtyp...]
  transfers between devices with their start and end apart: 31 -> 31, of which waited for: 14 -> 14; matrix products, arithmetic and copies ran while one was open for 0% -> 0% of each run, Pallas kernels for 4% -> 5%
where the time goes in v4:
time: 90.6 us; the launch traced here: 90.5 us
  starting transfers between devices  44 us (49%)
  waiting for transfers between devices  25 us (28%)
  Pallas kernels  11.6 us (13%)
  blocking collectives  8.8 us (10%)
  between operations  1 us (1%)
    ppermute x8, starting transfers between devices, along_x(): lax.ppermute(array, AXES, permutation(lambda z, x, y, c: (z, x + hops * (...  12.8 us
    ppermute x13, starting transfers between devices, other_core(): lax.ppermute(array, AXES, permutation(lambda z, x, y, c: (z, x, y, c + 1)))  12.2 us
    ppermute x6, starting transfers between devices, along_y(): lax.ppermute(array, AXES, permutation(lambda z, x, y, c: (z, x, y + hops...  9.58 us
    ppermute x8, waiting for transfers between devices, along_x(): lax.ppermute(array, AXES, permutation(lambda z, x, y, c: (z, x + hops * (...  9.42 us
    ppermute x4, starting transfers between devices, along_z(): lax.ppermute(array, AXES, permutation(lambda z, x, y, c: (z + hops * (1 -...  9.39 us
    all_to_all x1, blocking collectives, layer(): sums = lax.all_to_all(sums, ('y', 'c'), 0, 0, tiled=True)  8.8 us
    ppermute x6, waiting for transfers between devices, along_y(): lax.ppermute(array, AXES, permutation(lambda z, x, y, c: (z, x, y + hops...  8.6 us
    pallas_call x1, Pallas kernels, attend(): pl.pallas_call(kernel, out_shape=[pltpu.VMEM((2 * TILE, GROUP * HEAD), jn...  5.25 us
  transfers between devices with their start and end apart: 31, of which 14 were waited for; matrix products, arithmetic and copies ran while one was open for 0% of the time, Pallas kernels for 5%

profile of v4, /device:TPU:1, one launch (start us, length us, event | category | flops | bytes accessed | tf_op | source)
XLA Modules:
  0.0 90.5 jit_solution(12220997348222665049)
XLA Ops:
  0.6 3.3 %collective-permute-start = (bf16[512,8192]{1,0:T(8,128)(2,1)}, bf16[512,8192]{1,0:T(8,128)(2,1)}, u32[]{:S(2)}, u32[]{:S(2)}) collective-permute-start(bf16[512,8192]{1,0:T(8,128)(2,1)} %rest_0_.1), channel_id=1, source_target_pairs={{0,1},{1,0},{2,3},{3,2},{4,5},{5,4},{6,7},{7,6},{8,9},{9,8},{10,11... | collective-permute-start | bytes 25165832 | tf_op jit(solution)/shard_map/ppermute | solution.py:54
  3.9 1.0 %pick.1 = (bf16[2,256,128]{2,1,0:T(8,128)(2,1)S(1)}, bf16[256,128]{1,0:T(8,128)(2,1)S(1)}, s32[2,12]{1,0:T(2,128)S(1)}, s32[1,64]{1,0:T(1,128)S(1)}) custom-call(bf16[2,256,512]{2,1,0:T(8,128)(2,1)} %all_ref.1, s32[2,12]{1,0:T(2,128)} %anc_hbm.1, s32[1,64]{1,0:T(1,128)} %bitcast.7), custom_call_target="tpu_custom_call" | custom-call | tf_op jit(solution)/shard_map/pick/pallas_call | solution.py:144
  4.9 4.4 %collective-permute-start.2 = (bf16[512,128]{1,0:T(8,128)(2,1)S(1)}, bf16[512,128]{1,0:T(8,128)(2,1)S(1)}, u32[]{:S(2)}, u32[]{:S(2)}) collective-permute-start(bf16[512,128]{1,0:T(8,128)(2,1)S(1)} %bitcast.3), channel_id=1, source_target_pairs={{0,64},{1,193},{2,66},{3,195},{4,68},{5,197},{6,70},{7,199},{8,72}... | collective-permute-start | bytes 393224 | tf_op jit(solution)/shard_map/ppermute | solution.py:36
  10.0 2.6 %collective-permute-done.2.refs_2_.rest_6_ = bf16[512,128]{1,0:T(8,128)(2,1)S(1)} collective-permute-done((bf16[512,128]{1,0:T(8,128)(2,1)S(1)}, bf16[512,128]{1,0:T(8,128)(2,1)S(1)}, u32[]{:S(2)}, u32[]{:S(2)}) %collective-permute-start.2) | collective-permute-done | bytes 131104 | tf_op jit(solution)/shard_map/ppermute | solution.py:36
  12.6 4.0 %collective-permute-start.4 = (bf16[256,128]{1,0:T(8,128)(2,1)S(1)}, bf16[256,128]{1,0:T(8,128)(2,1)S(1)}, u32[]{:S(2)}, u32[]{:S(2)}) collective-permute-start(bf16[256,128]{1,0:T(8,128)(2,1)S(1)} %constant_dynamic-slice_fusion), channel_id=1, source_target_pairs={{0,64},{1,193},{2,66},{3,195},{4,68},{5,197},{6,70},{7,199},{8,72}... | collective-permute-start | bytes 196616 | tf_op jit(solution)/shard_map/ppermute | solution.py:36
  16.9 1.1 %collective-permute-done.4.refs_1_.rest_8_ = bf16[256,128]{1,0:T(8,128)(2,1)S(1)} collective-permute-done((bf16[256,128]{1,0:T(8,128)(2,1)S(1)}, bf16[256,128]{1,0:T(8,128)(2,1)S(1)}, u32[]{:S(2)}, u32[]{:S(2)}) %collective-permute-start.4) | collective-permute-done | bytes 65568 | tf_op jit(solution)/shard_map/ppermute | solution.py:36
  17.9 1.1 %collective-permute-start.17 = (bf16[256,128]{1,0:T(8,128)(2,1)S(1)}, bf16[256,128]{1,0:T(8,128)(2,1)S(1)}, u32[]{:S(2)}, u32[]{:S(2)}) collective-permute-start(bf16[256,128]{1,0:T(8,128)(2,1)S(1)} %collective-permute-done.4.refs_1_.rest_8_), channel_id=1, source_target_pairs={{0,1},{1,0},{2,3},{3,2},{4,5},{5,4},{6,7},{7,6},{8,9},{9,8},{10,11... | collective-permute-start | bytes 196616 | tf_op jit(solution)/shard_map/ppermute | solution.py:54
  19.0 2.7 %collective-permute-start.7 = (s32[2,12]{1,0:T(2,128)}, s32[2,12]{1,0:T(2,128)S(1)}, u32[]{:S(2)}, u32[]{:S(2)}) collective-permute-start(s32[2,12]{1,0:T(2,128)} %anc_hbm.1), channel_id=1, source_target_pairs={{0,16},{1,17},{2,18},{3,19},{4,20},{5,21},{6,22},{7,23},{8,24},{9,... | collective-permute-start | bytes 296 | tf_op jit(solution)/shard_map/ppermute | solution.py:42
  21.8 1.7 %collective-permute-done.7.third_ref = s32[2,12]{1,0:T(2,128)S(1)} collective-permute-done((s32[2,12]{1,0:T(2,128)}, s32[2,12]{1,0:T(2,128)S(1)}, u32[]{:S(2)}, u32[]{:S(2)}) %collective-permute-start.7) | collective-permute-done | bytes 128 | tf_op jit(solution)/shard_map/ppermute | solution.py:42
  23.4 1.2 %collective-permute-start.5 = (s32[2,12]{1,0:T(2,128)}, s32[2,12]{1,0:T(2,128)S(1)}, u32[]{:S(2)}, u32[]{:S(2)}) collective-permute-start(s32[2,12]{1,0:T(2,128)} %anc_hbm.1), channel_id=1, source_target_pairs={{0,24},{1,9},{2,26},{3,11},{4,28},{5,13},{6,30},{7,15},{8,0},{9,17... | collective-permute-start | bytes 296 | tf_op jit(solution)/shard_map/ppermute | solution.py:42
  24.7 2.6 %collective-permute-done.5.first_ref = s32[2,12]{1,0:T(2,128)S(1)} collective-permute-done((s32[2,12]{1,0:T(2,128)}, s32[2,12]{1,0:T(2,128)S(1)}, u32[]{:S(2)}, u32[]{:S(2)}) %collective-permute-start.5) | collective-permute-done | bytes 128 | tf_op jit(solution)/shard_map/ppermute | solution.py:42
  27.3 1.3 %collective-permute-start.6 = (s32[2,12]{1,0:T(2,128)S(1)}, s32[2,12]{1,0:T(2,128)S(1)}, u32[]{:S(2)}, u32[]{:S(2)}) collective-permute-start(s32[2,12]{1,0:T(2,128)S(1)} %collective-permute-done.5.first_ref), channel_id=1, source_target_pairs={{0,1},{1,0},{2,3},{3,2},{4,5},{5,4},{6,7},{7,6},{8,9},{9,8},{10,11... | collective-permute-start | bytes 296 | tf_op jit(solution)/shard_map/ppermute | solution.py:54
  30.1 2.3 %collective-permute-start.8 = (bf16[640,128]{1,0:T(8,128)(2,1)S(1)}, bf16[640,128]{1,0:T(8,128)(2,1)S(1)}, u32[]{:S(2)}, u32[]{:S(2)}) collective-permute-start(bf16[640,128]{1,0:T(8,128)(2,1)S(1)} %get-tuple-element.21), channel_id=1, source_target_pairs={{0,16},{1,17},{2,18},{3,19},{4,20},{5,21},{6,22},{7,23},{8,24},{9,... | collective-permute-start | bytes 491528 | tf_op jit(solution)/shard_map/ppermute | solution.py:42
  32.5 1.5 %collective-permute-start.9 = (bf16[640,128]{1,0:T(8,128)(2,1)S(1)}, bf16[640,128]{1,0:T(8,128)(2,1)S(1)}, u32[]{:S(2)}, u32[]{:S(2)}) collective-permute-start(bf16[640,128]{1,0:T(8,128)(2,1)S(1)} %get-tuple-element.22), channel_id=1, source_target_pairs={{0,24},{1,9},{2,26},{3,11},{4,28},{5,13},{6,30},{7,15},{8,0},{9,17... | collective-permute-start | bytes 491528 | tf_op jit(solution)/shard_map/ppermute | solution.py:42
  34.0 1.2 %collective-permute-start.10 = (bf16[640,128]{1,0:T(8,128)(2,1)S(1)}, bf16[640,128]{1,0:T(8,128)(2,1)S(1)}, u32[]{:S(2)}, u32[]{:S(2)}) collective-permute-start(bf16[640,128]{1,0:T(8,128)(2,1)S(1)} %get-tuple-element.23), channel_id=1, source_target_pairs={{0,8},{1,25},{2,10},{3,27},{4,12},{5,29},{6,14},{7,31},{8,16},{9,1... | collective-permute-start | bytes 491528 | tf_op jit(solution)/shard_map/ppermute | solution.py:42
  36.0 1.3 %collective-permute-done.8.rest_9_ = bf16[640,128]{1,0:T(8,128)(2,1)S(1)} collective-permute-done((bf16[640,128]{1,0:T(8,128)(2,1)S(1)}, bf16[640,128]{1,0:T(8,128)(2,1)S(1)}, u32[]{:S(2)}, u32[]{:S(2)}) %collective-permute-start.8) | collective-permute-done | bytes 163872 | tf_op jit(solution)/shard_map/ppermute | solution.py:42
  38.2 2.7 %collective-permute-done.9.rest_10_ = bf16[640,128]{1,0:T(8,128)(2,1)S(1)} collective-permute-done((bf16[640,128]{1,0:T(8,128)(2,1)S(1)}, bf16[640,128]{1,0:T(8,128)(2,1)S(1)}, u32[]{:S(2)}, u32[]{:S(2)}) %collective-permute-start.9) | collective-permute-done | bytes 163872 | tf_op jit(solution)/shard_map/ppermute | solution.py:42
  40.9 2.4 %collective-permute-start.16 = (bf16[512,128]{1,0:T(8,128)(2,1)S(1)}, bf16[512,128]{1,0:T(8,128)(2,1)S(1)}, u32[]{:S(2)}, u32[]{:S(2)}) collective-permute-start(bf16[512,128]{1,0:T(8,128)(2,1)S(1)} %collective-permute-done.3.refs_0_.rest_7_), channel_id=1, source_target_pairs={{0,1},{1,0},{2,3},{3,2},{4,5},{5,4},{6,7},{7,6},{8,9},{9,8},{10,11... | collective-permute-start | bytes 393224 | tf_op jit(solution)/shard_map/ppermute | solution.py:54
  43.3 2.1 %collective-permute-start.13 = (bf16[384,128]{1,0:T(8,128)(2,1)S(1)}, bf16[384,128]{1,0:T(8,128)(2,1)S(1)}, u32[]{:S(2)}, u32[]{:S(2)}) collective-permute-start(bf16[384,128]{1,0:T(8,128)(2,1)S(1)} %get-tuple-element.26), channel_id=1, source_target_pairs={{0,8},{1,25},{2,10},{3,27},{4,12},{5,29},{6,14},{7,31},{8,16},{9,1... | collective-permute-start | bytes 294920 | tf_op jit(solution)/shard_map/ppermute | solution.py:42
  46.0 1.1 %collective-permute-done.13.rest_14_ = bf16[384,128]{1,0:T(8,128)(2,1)S(1)} collective-permute-done((bf16[384,128]{1,0:T(8,128)(2,1)S(1)}, bf16[384,128]{1,0:T(8,128)(2,1)S(1)}, u32[]{:S(2)}, u32[]{:S(2)}) %collective-permute-start.13) | collective-permute-done | bytes 98336 | tf_op jit(solution)/shard_map/ppermute | solution.py:42
  47.1 2.4 %collective-permute-start.18 = (bf16[640,128]{1,0:T(8,128)(2,1)S(1)}, bf16[640,128]{1,0:T(8,128)(2,1)S(1)}, u32[]{:S(2)}, u32[]{:S(2)}) collective-permute-start(bf16[640,128]{1,0:T(8,128)(2,1)S(1)} %collective-permute-done.8.rest_9_), channel_id=1, source_target_pairs={{0,1},{1,0},{2,3},{3,2},{4,5},{5,4},{6,7},{7,6},{8,9},{9,8},{10,11... | collective-permute-start | bytes 491528 | tf_op jit(solution)/shard_map/ppermute | solution.py:54
  50.1 1.2 %collective-permute-done.23.rest_24_ = bf16[384,128]{1,0:T(8,128)(2,1)S(1)} collective-permute-done((bf16[384,128]{1,0:T(8,128)(2,1)S(1)}, bf16[384,128]{1,0:T(8,128)(2,1)S(1)}, u32[]{:S(2)}, u32[]{:S(2)}) %collective-permute-start.23) | collective-permute-done | bytes 98336 | tf_op jit(solution)/shard_map/ppermute | solution.py:54
  51.3 5.2 %attend.1 = (bf16[256,512]{1,0:T(8,128)(2,1)S(1)}, bf16[4,512,1024]{2,1,0:T(8,128)(2,1)S(1)}, bf16[4,512,1024]{2,1,0:T(8,128)(2,1)S(1)}) custom-call(bf16[256,512]{1,0:T(8,128)(2,1)} %query_hbm.1, bf16[512,8192]{1,0:T(8,128)(2,1)} %rest_0_.1, bf16[512,8192]{1,0:T(8,128)(2,1)} %collective-permute-done.rest_1_, s32[2,12]{1,0:T(2,128)S(1)} %get-tuple-element.17.rest_2_, ...), custom_call_target="tpu_custom_call" | custom-call | tf_op jit(solution)/shard_map/attend/pallas_call | solution.py:325
  56.9 1.3 %collective-permute-done.24.b_ref = bf16[256,512]{1,0:T(8,128)(2,1)S(1)} collective-permute-done((bf16[256,512]{1,0:T(8,128)(2,1)S(1)}, bf16[256,512]{1,0:T(8,128)(2,1)S(1)}, u32[]{:S(2)}, u32[]{:S(2)}) %collective-permute-start.24) | collective-permute-done | bytes 262176 | tf_op jit(solution)/shard_map/ppermute | solution.py:54
  58.6 2.9 %collective-permute-start.25 = (bf16[128,1024]{1,0:T(8,128)(2,1)S(1)}, bf16[128,1024]{1,0:T(8,128)(2,1)S(1)}, u32[]{:S(2)}, u32[]{:S(2)}) collective-permute-start(bf16[128,1024]{1,0:T(8,128)(2,1)S(1)} %project.8), channel_id=1, source_target_pairs={{0,2},{1,7},{2,4},{3,1},{4,6},{5,3},{6,0},{7,5},{8,10},{9,15},{10,... | collective-permute-start | bytes 786440 | tf_op jit(solution)/shard_map/ppermute | solution.py:48
  63.1 2.7 %collective-permute-start.30 = (bf16[128,1024]{1,0:T(8,128)(2,1)S(1)}, bf16[128,1024]{1,0:T(8,128)(2,1)S(1)}, u32[]{:S(2)}, u32[]{:S(2)}) collective-permute-start(bf16[128,1024]{1,0:T(8,128)(2,1)S(1)} %project.13), channel_id=1, source_target_pairs={{0,2},{1,7},{2,4},{3,1},{4,6},{5,3},{6,0},{7,5},{8,10},{9,15},{10,... | collective-permute-start | bytes 786440 | tf_op jit(solution)/shard_map/ppermute | solution.py:48
  66.8 3.7 %collective-permute-start.26 = (bf16[128,1024]{1,0:T(8,128)(2,1)S(1)}, bf16[128,1024]{1,0:T(8,128)(2,1)S(1)}, u32[]{:S(2)}, u32[]{:S(2)}) collective-permute-start(bf16[128,1024]{1,0:T(8,128)(2,1)S(1)} %project.9), channel_id=1, source_target_pairs={{0,2},{1,7},{2,4},{3,1},{4,6},{5,3},{6,0},{7,5},{8,10},{9,15},{10,... | collective-permute-start | bytes 786440 | tf_op jit(solution)/shard_map/ppermute | solution.py:48
  71.7 1.7 %collective-permute-done.27.a0_ref = bf16[128,1024]{1,0:T(8,128)(2,1)S(1)} collective-permute-done((bf16[128,1024]{1,0:T(8,128)(2,1)S(1)}, bf16[128,1024]{1,0:T(8,128)(2,1)S(1)}, u32[]{:S(2)}, u32[]{:S(2)}) %collective-permute-start.27) | collective-permute-done | bytes 262176 | tf_op jit(solution)/shard_map/ppermute | solution.py:48
  73.5 4.1 %collective-permute-done.26.b0_ref = bf16[128,1024]{1,0:T(8,128)(2,1)S(1)} collective-permute-done((bf16[128,1024]{1,0:T(8,128)(2,1)S(1)}, bf16[128,1024]{1,0:T(8,128)(2,1)S(1)}, u32[]{:S(2)}, u32[]{:S(2)}) %collective-permute-start.26) | collective-permute-done | bytes 262176 | tf_op jit(solution)/shard_map/ppermute | solution.py:48
  77.6 2.3 %collective-permute-done.29.a1_ref = bf16[128,1024]{1,0:T(8,128)(2,1)S(1)} collective-permute-done((bf16[128,1024]{1,0:T(8,128)(2,1)S(1)}, bf16[128,1024]{1,0:T(8,128)(2,1)S(1)}, u32[]{:S(2)}, u32[]{:S(2)}) %collective-permute-start.29) | collective-permute-done | bytes 262176 | tf_op jit(solution)/shard_map/ppermute | solution.py:48
  80.5 8.8 %all_to_all.5.sums_ref = f32[8,1,256]{2,1,0:T(1,128)S(1)} all-to-all(f32[8,1,256]{2,1,0:T(1,128)S(1)} %get-tuple-element.31), channel_id=1, replica_groups=mesh['z'=8,'x'=4,'y'=4,'c'=2] {'y','c'}, dimensions={0} | all-to-all | bytes 16384 | tf_op jit(solution)/shard_map/all_to_all | solution.py:500
  89.3 1.0 %normalize.1 = (bf16[256,1024]{1,0:T(8,128)(2,1)}, bf16[256,1024]{1,0:T(8,128)(2,1)}) custom-call(bf16[256,1024]{1,0:T(8,128)(2,1)S(1)} %get-tuple-element.30.hidden_ref, f32[8,1,256]{2,1,0:T(1,128)S(1)} %all_to_all.5.sums_ref, f32[1,1024]{1,0:T(1,128)S(1)} %bitcast.6), custom_call_target="tpu_custom_call" | custom-call | tf_op jit(solution)/shard_map/normalize/pallas_call | solution.py:463
  (50 shorter events, 10.5 us)
Async XLA Ops:
  0.6 50.7 %collective-permute-start = (bf16[512,8192]{1,0:T(8,128)(2,1)}, bf16[512,8192]{1,0:T(8,128)(2,1)}, u32[]{:S(2)}, u32[]{:S(2)}) collective-permute-start(bf16[512,8192]{1,0:T(8,128)(2,1)} %rest_0_.1), channel_id=1, source_target_pairs={{0,1},{1,0},{2,3},{3,2},{4,5},{5,4},{6,7},{7,6},{8,9},{9,8},{10,11... | collective-permute-start | bytes 25165832 | tf_op jit(solution)/shard_map/ppermute | solution.py:54
  4.9 7.7 %collective-permute-start.2 = (bf16[512,128]{1,0:T(8,128)(2,1)S(1)}, bf16[512,128]{1,0:T(8,128)(2,1)S(1)}, u32[]{:S(2)}, u32[]{:S(2)}) collective-permute-start(bf16[512,128]{1,0:T(8,128)(2,1)S(1)} %bitcast.3), channel_id=1, source_target_pairs={{0,64},{1,193},{2,66},{3,195},{4,68},{5,197},{6,70},{7,199},{8,72}... | collective-permute-start | bytes 393224 | tf_op jit(solution)/shard_map/ppermute | solution.py:36
  9.3 7.3 %collective-permute-start.1 = (bf16[512,128]{1,0:T(8,128)(2,1)S(1)}, bf16[512,128]{1,0:T(8,128)(2,1)S(1)}, u32[]{:S(2)}, u32[]{:S(2)}) collective-permute-start(bf16[512,128]{1,0:T(8,128)(2,1)S(1)} %bitcast.4), channel_id=1, source_target_pairs={{0,32},{1,225},{2,34},{3,227},{4,36},{5,229},{6,38},{7,231},{8,40}... | collective-permute-start | bytes 393224 | tf_op jit(solution)/shard_map/ppermute | solution.py:36
  12.6 5.3 %collective-permute-start.4 = (bf16[256,128]{1,0:T(8,128)(2,1)S(1)}, bf16[256,128]{1,0:T(8,128)(2,1)S(1)}, u32[]{:S(2)}, u32[]{:S(2)}) collective-permute-start(bf16[256,128]{1,0:T(8,128)(2,1)S(1)} %constant_dynamic-slice_fusion), channel_id=1, source_target_pairs={{0,64},{1,193},{2,66},{3,195},{4,68},{5,197},{6,70},{7,199},{8,72}... | collective-permute-start | bytes 196616 | tf_op jit(solution)/shard_map/ppermute | solution.py:36
  16.6 15.8 %collective-permute-start.15 = (bf16[512,128]{1,0:T(8,128)(2,1)S(1)}, bf16[512,128]{1,0:T(8,128)(2,1)S(1)}, u32[]{:S(2)}, u32[]{:S(2)}) collective-permute-start(bf16[512,128]{1,0:T(8,128)(2,1)S(1)} %collective-permute-done.2.refs_2_.rest_6_), channel_id=1, source_target_pairs={{0,1},{1,0},{2,3},{3,2},{4,5},{5,4},{6,7},{7,6},{8,9},{9,8},{10,11... | collective-permute-start | bytes 393224 | tf_op jit(solution)/shard_map/ppermute | solution.py:54
  16.6 17.4 %collective-permute-start.3 = (bf16[512,128]{1,0:T(8,128)(2,1)S(1)}, bf16[512,128]{1,0:T(8,128)(2,1)S(1)}, u32[]{:S(2)}, u32[]{:S(2)}) collective-permute-start(bf16[512,128]{1,0:T(8,128)(2,1)S(1)} %collective-permute-done.1.refs_1_.rest_5_), channel_id=1, source_target_pairs={{0,64},{1,193},{2,66},{3,195},{4,68},{5,197},{6,70},{7,199},{8,72}... | collective-permute-start | bytes 393224 | tf_op jit(solution)/shard_map/ppermute | solution.py:36
  17.9 12.2 %collective-permute-start.17 = (bf16[256,128]{1,0:T(8,128)(2,1)S(1)}, bf16[256,128]{1,0:T(8,128)(2,1)S(1)}, u32[]{:S(2)}, u32[]{:S(2)}) collective-permute-start(bf16[256,128]{1,0:T(8,128)(2,1)S(1)} %collective-permute-done.4.refs_1_.rest_8_), channel_id=1, source_target_pairs={{0,1},{1,0},{2,3},{3,2},{4,5},{5,4},{6,7},{7,6},{8,9},{9,8},{10,11... | collective-permute-start | bytes 196616 | tf_op jit(solution)/shard_map/ppermute | solution.py:54
  19.0 4.4 %collective-permute-start.7 = (s32[2,12]{1,0:T(2,128)}, s32[2,12]{1,0:T(2,128)S(1)}, u32[]{:S(2)}, u32[]{:S(2)}) collective-permute-start(s32[2,12]{1,0:T(2,128)} %anc_hbm.1), channel_id=1, source_target_pairs={{0,16},{1,17},{2,18},{3,19},{4,20},{5,21},{6,22},{7,23},{8,24},{9,... | collective-permute-start | bytes 296 | tf_op jit(solution)/shard_map/ppermute | solution.py:42
  23.4 3.8 %collective-permute-start.5 = (s32[2,12]{1,0:T(2,128)}, s32[2,12]{1,0:T(2,128)S(1)}, u32[]{:S(2)}, u32[]{:S(2)}) collective-permute-start(s32[2,12]{1,0:T(2,128)} %anc_hbm.1), channel_id=1, source_target_pairs={{0,24},{1,9},{2,26},{3,11},{4,28},{5,13},{6,30},{7,15},{8,0},{9,17... | collective-permute-start | bytes 296 | tf_op jit(solution)/shard_map/ppermute | solution.py:42
  27.3 2.1 %collective-permute-start.6 = (s32[2,12]{1,0:T(2,128)S(1)}, s32[2,12]{1,0:T(2,128)S(1)}, u32[]{:S(2)}, u32[]{:S(2)}) collective-permute-start(s32[2,12]{1,0:T(2,128)S(1)} %collective-permute-done.5.first_ref), channel_id=1, source_target_pairs={{0,1},{1,0},{2,3},{3,2},{4,5},{5,4},{6,7},{7,6},{8,9},{9,8},{10,11... | collective-permute-start | bytes 296 | tf_op jit(solution)/shard_map/ppermute | solution.py:54
  29.4 5.8 %collective-permute-start.14 = (bf16[512,128]{1,0:T(8,128)(2,1)S(1)}, bf16[512,128]{1,0:T(8,128)(2,1)S(1)}, u32[]{:S(2)}, u32[]{:S(2)}) collective-permute-start(bf16[512,128]{1,0:T(8,128)(2,1)S(1)} %collective-permute-done.1.refs_1_.rest_5_), channel_id=1, source_target_pairs={{0,1},{1,0},{2,3},{3,2},{4,5},{5,4},{6,7},{7,6},{8,9},{9,8},{10,11... | collective-permute-start | bytes 393224 | tf_op jit(solution)/shard_map/ppermute | solution.py:54
  30.1 7.2 %collective-permute-start.8 = (bf16[640,128]{1,0:T(8,128)(2,1)S(1)}, bf16[640,128]{1,0:T(8,128)(2,1)S(1)}, u32[]{:S(2)}, u32[]{:S(2)}) collective-permute-start(bf16[640,128]{1,0:T(8,128)(2,1)S(1)} %get-tuple-element.21), channel_id=1, source_target_pairs={{0,16},{1,17},{2,18},{3,19},{4,20},{5,21},{6,22},{7,23},{8,24},{9,... | collective-permute-start | bytes 491528 | tf_op jit(solution)/shard_map/ppermute | solution.py:42
  32.5 8.5 %collective-permute-start.9 = (bf16[640,128]{1,0:T(8,128)(2,1)S(1)}, bf16[640,128]{1,0:T(8,128)(2,1)S(1)}, u32[]{:S(2)}, u32[]{:S(2)}) collective-permute-start(bf16[640,128]{1,0:T(8,128)(2,1)S(1)} %get-tuple-element.22), channel_id=1, source_target_pairs={{0,24},{1,9},{2,26},{3,11},{4,28},{5,13},{6,30},{7,15},{8,0},{9,17... | collective-permute-start | bytes 491528 | tf_op jit(solution)/shard_map/ppermute | solution.py:42
  34.0 9.3 %collective-permute-start.10 = (bf16[640,128]{1,0:T(8,128)(2,1)S(1)}, bf16[640,128]{1,0:T(8,128)(2,1)S(1)}, u32[]{:S(2)}, u32[]{:S(2)}) collective-permute-start(bf16[640,128]{1,0:T(8,128)(2,1)S(1)} %get-tuple-element.23), channel_id=1, source_target_pairs={{0,8},{1,25},{2,10},{3,27},{4,12},{5,29},{6,14},{7,31},{8,16},{9,1... | collective-permute-start | bytes 491528 | tf_op jit(solution)/shard_map/ppermute | solution.py:42
  35.2 10.2 %collective-permute-start.11 = (bf16[384,128]{1,0:T(8,128)(2,1)S(1)}, bf16[384,128]{1,0:T(8,128)(2,1)S(1)}, u32[]{:S(2)}, u32[]{:S(2)}) collective-permute-start(bf16[384,128]{1,0:T(8,128)(2,1)S(1)} %get-tuple-element.24), channel_id=1, source_target_pairs={{0,16},{1,17},{2,18},{3,19},{4,20},{5,21},{6,22},{7,23},{8,24},{9,... | collective-permute-start | bytes 294920 | tf_op jit(solution)/shard_map/ppermute | solution.py:42
  37.3 8.2 %collective-permute-start.12 = (bf16[384,128]{1,0:T(8,128)(2,1)S(1)}, bf16[384,128]{1,0:T(8,128)(2,1)S(1)}, u32[]{:S(2)}, u32[]{:S(2)}) collective-permute-start(bf16[384,128]{1,0:T(8,128)(2,1)S(1)} %get-tuple-element.25), channel_id=1, source_target_pairs={{0,24},{1,9},{2,26},{3,11},{4,28},{5,13},{6,30},{7,15},{8,0},{9,17... | collective-permute-start | bytes 294920 | tf_op jit(solution)/shard_map/ppermute | solution.py:42
  40.9 8.5 %collective-permute-start.16 = (bf16[512,128]{1,0:T(8,128)(2,1)S(1)}, bf16[512,128]{1,0:T(8,128)(2,1)S(1)}, u32[]{:S(2)}, u32[]{:S(2)}) collective-permute-start(bf16[512,128]{1,0:T(8,128)(2,1)S(1)} %collective-permute-done.3.refs_0_.rest_7_), channel_id=1, source_target_pairs={{0,1},{1,0},{2,3},{3,2},{4,5},{5,4},{6,7},{7,6},{8,9},{9,8},{10,11... | collective-permute-start | bytes 393224 | tf_op jit(solution)/shard_map/ppermute | solution.py:54
  43.3 3.8 %collective-permute-start.13 = (bf16[384,128]{1,0:T(8,128)(2,1)S(1)}, bf16[384,128]{1,0:T(8,128)(2,1)S(1)}, u32[]{:S(2)}, u32[]{:S(2)}) collective-permute-start(bf16[384,128]{1,0:T(8,128)(2,1)S(1)} %get-tuple-element.26), channel_id=1, source_target_pairs={{0,8},{1,25},{2,10},{3,27},{4,12},{5,29},{6,14},{7,31},{8,16},{9,1... | collective-permute-start | bytes 294920 | tf_op jit(solution)/shard_map/ppermute | solution.py:42
  45.4 4.0 %collective-permute-start.21 = (bf16[384,128]{1,0:T(8,128)(2,1)S(1)}, bf16[384,128]{1,0:T(8,128)(2,1)S(1)}, u32[]{:S(2)}, u32[]{:S(2)}) collective-permute-start(bf16[384,128]{1,0:T(8,128)(2,1)S(1)} %collective-permute-done.11.rest_12_), channel_id=1, source_target_pairs={{0,1},{1,0},{2,3},{3,2},{4,5},{5,4},{6,7},{7,6},{8,9},{9,8},{10,11... | collective-permute-start | bytes 294920 | tf_op jit(solution)/shard_map/ppermute | solution.py:54
  45.4 4.5 %collective-permute-start.22 = (bf16[384,128]{1,0:T(8,128)(2,1)S(1)}, bf16[384,128]{1,0:T(8,128)(2,1)S(1)}, u32[]{:S(2)}, u32[]{:S(2)}) collective-permute-start(bf16[384,128]{1,0:T(8,128)(2,1)S(1)} %collective-permute-done.12.rest_13_), channel_id=1, source_target_pairs={{0,1},{1,0},{2,3},{3,2},{4,5},{5,4},{6,7},{7,6},{8,9},{9,8},{10,11... | collective-permute-start | bytes 294920 | tf_op jit(solution)/shard_map/ppermute | solution.py:54
  47.1 4.2 %collective-permute-start.18 = (bf16[640,128]{1,0:T(8,128)(2,1)S(1)}, bf16[640,128]{1,0:T(8,128)(2,1)S(1)}, u32[]{:S(2)}, u32[]{:S(2)}) collective-permute-start(bf16[640,128]{1,0:T(8,128)(2,1)S(1)} %collective-permute-done.8.rest_9_), channel_id=1, source_target_pairs={{0,1},{1,0},{2,3},{3,2},{4,5},{5,4},{6,7},{7,6},{8,9},{9,8},{10,11... | collective-permute-start | bytes 491528 | tf_op jit(solution)/shard_map/ppermute | solution.py:54
  49.5 1.8 %collective-permute-start.19 = (bf16[640,128]{1,0:T(8,128)(2,1)S(1)}, bf16[640,128]{1,0:T(8,128)(2,1)S(1)}, u32[]{:S(2)}, u32[]{:S(2)}) collective-permute-start(bf16[640,128]{1,0:T(8,128)(2,1)S(1)} %collective-permute-done.9.rest_10_), channel_id=1, source_target_pairs={{0,1},{1,0},{2,3},{3,2},{4,5},{5,4},{6,7},{7,6},{8,9},{9,8},{10,11... | collective-permute-start | bytes 491528 | tf_op jit(solution)/shard_map/ppermute | solution.py:54
  49.5 1.8 %collective-permute-start.20 = (bf16[640,128]{1,0:T(8,128)(2,1)S(1)}, bf16[640,128]{1,0:T(8,128)(2,1)S(1)}, u32[]{:S(2)}, u32[]{:S(2)}) collective-permute-start(bf16[640,128]{1,0:T(8,128)(2,1)S(1)} %collective-permute-done.10.rest_11_), channel_id=1, source_target_pairs={{0,1},{1,0},{2,3},{3,2},{4,5},{5,4},{6,7},{7,6},{8,9},{9,8},{10,11... | collective-permute-start | bytes 491528 | tf_op jit(solution)/shard_map/ppermute | solution.py:54
  50.0 1.3 %collective-permute-start.23 = (bf16[384,128]{1,0:T(8,128)(2,1)S(1)}, bf16[384,128]{1,0:T(8,128)(2,1)S(1)}, u32[]{:S(2)}, u32[]{:S(2)}) collective-permute-start(bf16[384,128]{1,0:T(8,128)(2,1)S(1)} %collective-permute-done.13.rest_14_), channel_id=1, source_target_pairs={{0,1},{1,0},{2,3},{3,2},{4,5},{5,4},{6,7},{7,6},{8,9},{9,8},{10,11... | collective-permute-start | bytes 294920 | tf_op jit(solution)/shard_map/ppermute | solution.py:54
  56.6 1.6 %collective-permute-start.24 = (bf16[256,512]{1,0:T(8,128)(2,1)S(1)}, bf16[256,512]{1,0:T(8,128)(2,1)S(1)}, u32[]{:S(2)}, u32[]{:S(2)}) collective-permute-start(bf16[256,512]{1,0:T(8,128)(2,1)S(1)} %get-tuple-element.27.a_ref), channel_id=1, source_target_pairs={{0,1},{1,0},{2,3},{3,2},{4,5},{5,4},{6,7},{7,6},{8,9},{9,8},{10,11... | collective-permute-start | bytes 786440 | tf_op jit(solution)/shard_map/ppermute | solution.py:54
  58.6 7.7 %collective-permute-start.25 = (bf16[128,1024]{1,0:T(8,128)(2,1)S(1)}, bf16[128,1024]{1,0:T(8,128)(2,1)S(1)}, u32[]{:S(2)}, u32[]{:S(2)}) collective-permute-start(bf16[128,1024]{1,0:T(8,128)(2,1)S(1)} %project.8), channel_id=1, source_target_pairs={{0,2},{1,7},{2,4},{3,1},{4,6},{5,3},{6,0},{7,5},{8,10},{9,15},{10,... | collective-permute-start | bytes 786440 | tf_op jit(solution)/shard_map/ppermute | solution.py:48
  62.0 8.5 %collective-permute-start.28 = (bf16[128,1024]{1,0:T(8,128)(2,1)S(1)}, bf16[128,1024]{1,0:T(8,128)(2,1)S(1)}, u32[]{:S(2)}, u32[]{:S(2)}) collective-permute-start(bf16[128,1024]{1,0:T(8,128)(2,1)S(1)} %project.11), channel_id=1, source_target_pairs={{0,6},{1,3},{2,0},{3,5},{4,2},{5,7},{6,4},{7,1},{8,14},{9,11},{10,... | collective-permute-start | bytes 786440 | tf_op jit(solution)/shard_map/ppermute | solution.py:48
  62.5 10.9 %collective-permute-start.27 = (bf16[128,1024]{1,0:T(8,128)(2,1)S(1)}, bf16[128,1024]{1,0:T(8,128)(2,1)S(1)}, u32[]{:S(2)}, u32[]{:S(2)}) collective-permute-start(bf16[128,1024]{1,0:T(8,128)(2,1)S(1)} %project.10), channel_id=1, source_target_pairs={{0,6},{1,3},{2,0},{3,5},{4,2},{5,7},{6,4},{7,1},{8,14},{9,11},{10,... | collective-permute-start | bytes 786440 | tf_op jit(solution)/shard_map/ppermute | solution.py:48
  63.1 10.4 %collective-permute-start.30 = (bf16[128,1024]{1,0:T(8,128)(2,1)S(1)}, bf16[128,1024]{1,0:T(8,128)(2,1)S(1)}, u32[]{:S(2)}, u32[]{:S(2)}) collective-permute-start(bf16[128,1024]{1,0:T(8,128)(2,1)S(1)} %project.13), channel_id=1, source_target_pairs={{0,2},{1,7},{2,4},{3,1},{4,6},{5,3},{6,0},{7,5},{8,10},{9,15},{10,... | collective-permute-start | bytes 786440 | tf_op jit(solution)/shard_map/ppermute | solution.py:48
  66.8 10.8 %collective-permute-start.26 = (bf16[128,1024]{1,0:T(8,128)(2,1)S(1)}, bf16[128,1024]{1,0:T(8,128)(2,1)S(1)}, u32[]{:S(2)}, u32[]{:S(2)}) collective-permute-start(bf16[128,1024]{1,0:T(8,128)(2,1)S(1)} %project.9), channel_id=1, source_target_pairs={{0,2},{1,7},{2,4},{3,1},{4,6},{5,3},{6,0},{7,5},{8,10},{9,15},{10,... | collective-permute-start | bytes 786440 | tf_op jit(solution)/shard_map/ppermute | solution.py:48
  70.9 18.4 %copy-start.1 = (f32[1024]{0:T(1024)S(1)}, f32[1024]{0:T(1024)}, u32[]{:S(2)}) copy-start(f32[1024]{0:T(1024)} %param.12) | copy-start | bytes 12292
  70.9 8.9 %collective-permute-start.29 = (bf16[128,1024]{1,0:T(8,128)(2,1)S(1)}, bf16[128,1024]{1,0:T(8,128)(2,1)S(1)}, u32[]{:S(2)}, u32[]{:S(2)}) collective-permute-start(bf16[128,1024]{1,0:T(8,128)(2,1)S(1)} %project.12), channel_id=1, source_target_pairs={{0,6},{1,3},{2,0},{3,5},{4,2},{5,7},{6,4},{7,1},{8,14},{9,11},{10,... | collective-permute-start | bytes 786440 | tf_op jit(solution)/shard_map/ppermute | solution.py:48
  (1 other events, 13.1 us)
